TPU v7x, 512 devices: a whole 4x4x16 slice. The times are simulated.
512 devices in a mesh: elem: 8 (over y_hi, x), band: 64 (over z, y_lo, core).
Axes of the slice: x: 4, y: 4 (y_hi: 2, y_lo: 2; y = y_hi * 2 + y_lo), z: 16, core: 2. Of those that a mesh axis runs over, the one named last changes fastest.
Arguments:
- start_bands: bfloat16 [2048, 6144], P('band', 'elem'), may hold values from -6 to 6
- hamiltonian: bfloat16 [32, 7, 192, 192], P('elem'), may hold values from -0.15625 to 0.15625
- neighbours: int32 [32, 6], P('elem'), may hold values from 0 to 3
- basis_count: int32 [32], P('elem'), may hold values from 128 to 192, as said below
- owner_rows: int32 [64], replicated, may hold values from 1 to 36, 768 in all
- rotation: bfloat16 [2048, 2048], P(None, 'band'), may hold values from -0.125 to 0.125
Outputs:
- filtered: bfloat16 [2048, 6144], P('band', 'elem')
- rotated: bfloat16 [18432, 2048], P(('elem', 'band'))
Inputs may be any that keep to these rules, and one draw needn't show every extreme that they name: `basis_count`: each element holds 128 to 192 basis functions; some element holds exactly 192 and some exactly 128. `neighbours`: any position 0 to 3 may appear in any slot, the element's own position too. `owner_rows`: the entries sum to 768; the largest is exactly 36.
All inputs are finite; a program needn't handle non-finite values.
Results may differ from a plain program's by a relative error of at most 0.013.
Values may be sent and summed in bfloat16 or wider, within the bound.
No kernel may reach another device: no remote copies, remote signals or barrier semaphores. Data moves between devices by JAX's collectives and lax.ppermute only.
A program may use at most 64 MiB of HBM per device.

v0:
```python
import jax
import jax.numpy as jnp
from jax import lax
from jax.sharding import PartitionSpec as P

DEGREE = 8


def padded(block, sides, width):
    for axis, dim in sides:
        count = lax.axis_size(axis)
        forward = [(i, i + 1) for i in range(count - 1)]
        forward.append((count - 1, 0))
        backward = [(target, source) for source, target in forward]
        low = lax.ppermute(
            lax.slice_in_dim(block, block.shape[dim] - width, None, axis=dim), axis, forward
        )
        high = lax.ppermute(lax.slice_in_dim(block, 0, width, axis=dim), axis, backward)
        block = jnp.concatenate([low, block, high], axis=dim)
    return block


def from_partner(value, axis, stride):
    mask = 2**stride
    pairs = [(source, source ^ mask) for source in range(lax.axis_size(axis))]
    return lax.ppermute(value, axis, pairs)


def per_device(start_bands, hamiltonian, neighbours, basis_count, owner_rows, rotation):
    bands_dev, rows_dev = start_bands.shape
    elem_count = hamiltonian.shape[0]
    basis_max = hamiltonian.shape[2]
    planes_dev = elem_count // 4
    basis_ids = lax.broadcasted_iota(jnp.int32, (elem_count, basis_max), 1)
    row_mask = (basis_ids < basis_count[:, None]).astype(jnp.float32).reshape(rows_dev)
    partner_pick = (neighbours[:, :, None] == jnp.arange(4, dtype=jnp.int32)[None, None, :]).astype(
        jnp.bfloat16
    )
    partner_pick = partner_pick.reshape(planes_dev, 4, 6, 4)
    weights = hamiltonian.reshape(elem_count, 7 * basis_max, basis_max)

    def apply_ham(state):
        plane_slab = state.reshape(bands_dev, planes_dev, 4 * basis_max)
        extended = padded(plane_slab, (("elem", 1),), 1)
        extended = extended.reshape(bands_dev, planes_dev + 2, 4, basis_max)
        plane_below = extended[:, :planes_dev]
        plane_mid = extended[:, 1 : planes_dev + 1]
        plane_above = extended[:, 2:]
        inplane = jnp.einsum(
            "pism,bpmk->bpisk",
            partner_pick[:, :, :4],
            plane_mid,
            preferred_element_type=jnp.float32,
        ).astype(jnp.bfloat16)
        lower = jnp.einsum(
            "pim,bpmk->bpik", partner_pick[:, :, 4], plane_below, preferred_element_type=jnp.float32
        ).astype(jnp.bfloat16)
        upper = jnp.einsum(
            "pim,bpmk->bpik", partner_pick[:, :, 5], plane_above, preferred_element_type=jnp.float32
        ).astype(jnp.bfloat16)
        sources = jnp.concatenate(
            [plane_mid[:, :, :, None], inplane, lower[:, :, :, None], upper[:, :, :, None]], axis=3
        )
        sources = sources.reshape(bands_dev, elem_count, 7 * basis_max)
        product = jnp.einsum("bej,ejl->bel", sources, weights, preferred_element_type=jnp.float32)
        return product.reshape(bands_dev, rows_dev) * row_mask

    earlier = (start_bands.astype(jnp.float32) * row_mask).astype(jnp.bfloat16)
    current = (0.5 * apply_ham(earlier)).astype(jnp.bfloat16)
    for repeat in range(DEGREE - 1):
        following = (apply_ham(current) - earlier.astype(jnp.float32)).astype(jnp.bfloat16)
        earlier = current
        current = following
    owners = lax.axis_size("band")
    slot_cap = 3 * rows_dev // owners
    row_starts = jnp.cumsum(owner_rows) - owner_rows
    slot_keep = jnp.arange(slot_cap, dtype=jnp.int32)[None, :] < owner_rows[:, None]
    total_bits = owners.bit_length() - 1
    low_bits = total_bits // 2
    low_count = 1 << low_bits
    high_count = owners // low_count
    window = rows_dev // low_count
    position = lax.axis_index("band")
    low_index = position % low_count
    buffer = current.reshape(bands_dev, low_count, window).transpose(1, 0, 2)
    for bit_no in range(low_bits):
        my_bit = position // (1 << bit_no) % 2
        shaped = buffer.reshape(low_count >> bit_no + 1, 2, 1 << bit_no, bands_dev, window)
        outgoing = lax.dynamic_index_in_dim(shaped, 1 - my_bit, 1, keepdims=False)
        incoming = from_partner(outgoing, "band", bit_no)
        shaped = lax.dynamic_update_index_in_dim(shaped, incoming, 1 - my_bit, 1)
        buffer = shaped.reshape(low_count, bands_dev, window)
    window_bands = buffer.reshape(low_count * bands_dev, window)
    for bit_no in range(low_bits, total_bits):
        other_half = from_partner(window_bands, "band", bit_no)
        my_bit = position // (1 << bit_no) % 2
        window_bands = jnp.where(
            my_bit == 0,
            jnp.concatenate([window_bands, other_half], axis=0),
            jnp.concatenate([other_half, window_bands], axis=0),
        )
    column_block = rotation
    for bit_no in range(low_bits):
        other_cols = from_partner(column_block, "band", bit_no)
        my_bit = position // (1 << bit_no) % 2
        column_block = jnp.where(
            my_bit == 0,
            jnp.concatenate([column_block, other_cols], axis=1),
            jnp.concatenate([other_cols, column_block], axis=1),
        )
    block_cols = column_block.shape[1]
    turned_block = lax.dot_general(
        window_bands, column_block, (((0,), (0,)), ((), ())), preferred_element_type=jnp.float32
    ).astype(jnp.bfloat16)
    slot_ids = jnp.arange(slot_cap, dtype=jnp.int32)
    local_row = row_starts[:, None] + slot_ids[None, :] - low_index * window
    valid = slot_keep & (local_row >= 0) & (local_row < window)
    clipped = jnp.clip(local_row, 0, window - 1).reshape(-1)
    picked = jnp.take(turned_block, clipped, axis=0).reshape(owners, slot_cap, block_cols)
    pieces = jnp.where(valid[:, :, None], picked, jnp.zeros((), jnp.bfloat16))
    received = lax.all_to_all(pieces, "band", split_axis=0, concat_axis=0, tiled=True)
    summed = (
        received.reshape(high_count, low_count, slot_cap, block_cols)
        .astype(jnp.float32)
        .sum(axis=1)
    )
    rotated = (
        summed.transpose(1, 0, 2).reshape(slot_cap, high_count * block_cols).astype(jnp.bfloat16)
    )
    return (current, rotated)


def solution(mesh):
    placed = (
        P("band", "elem"),
        P("elem", None, None, None),
        P("elem", None),
        P("elem"),
        P(),
        P(None, "band"),
    )
    return jax.shard_map(
        per_device,
        mesh=mesh,
        in_specs=placed,
        out_specs=(P("band", "elem"), P(("elem", "band"), None)),
        check_vma=False,
    )
```

profile of v0, /device:TPU:8, one launch (start us, length us, event | category | flops | bytes accessed | tf_op | source)
XLA Modules:
  0.0 321.6 jit_solution(15081339424707527882)
XLA Ops:
  2.4 6.4 %collective-permute-start.1 = (bf16[32,1,768]{2,0,1:T(8,128)(2,1)S(1)}, bf16[32,1,768]{2,0,1:T(8,128)(2,1)S(1)}, u32[]{:S(2)}, u32[]{:S(2)}) collective-permute-start(bf16[32,1,768]{2,0,1:T(8,128)(2,1)S(1)} %fusion.100), channel_id=1, source_target_pairs={{64,0},{128,64},{192,128},{256,192},{320,256},{384,320},{448,384},... | collective-permute-start | bytes 147464 | tf_op jit(solution)/shard_map/ppermute | solution.py:18
  8.8 1.9 collective-permute-start
  10.8 1.9 collective-permute-start.22
  18.9 1.6 pad_maximum_fusion
  23.5 7.2 %collective-permute-start.3 = (bf16[32,1,768]{2,0,1:T(8,128)(2,1)S(1)}, bf16[32,1,768]{2,0,1:T(8,128)(2,1)S(1)}, u32[]{:S(2)}, u32[]{:S(2)}) collective-permute-start(bf16[32,1,768]{2,0,1:T(8,128)(2,1)S(1)} %multiply_convert_fusion.1), channel_id=1, source_target_pairs={{64,0},{128,64},{192,128},{256,192},{320,256},{384,320},{448,384},... | collective-permute-start | bytes 147464 | tf_op jit(solution)/shard_map/ppermute | solution.py:18
  30.7 1.9 collective-permute-start.2
  34.7 5.6 %collective-permute-done.2 = bf16[32,1,768]{2,0,1:T(8,128)(2,1)S(1)} collective-permute-done((bf16[32,1,768]{2,0,1:T(8,128)(2,1)S(1)}, bf16[32,1,768]{2,0,1:T(8,128)(2,1)S(1)}, u32[]{:S(2)}, u32[]{:S(2)}) %collective-permute-start.2) | collective-permute-done | bytes 49184 | tf_op jit(solution)/shard_map/ppermute | solution.py:15
  40.9 1.7 pad_maximum_fusion.1
  45.5 1.9 collective-permute-start.5
  47.4 3.9 %collective-permute-start.4 = (bf16[32,1,768]{2,0,1:T(8,128)(2,1)S(1)}, bf16[32,1,768]{2,0,1:T(8,128)(2,1)S(1)}, u32[]{:S(2)}, u32[]{:S(2)}) collective-permute-start(bf16[32,1,768]{2,0,1:T(8,128)(2,1)S(1)} %bitcast.338), channel_id=1, source_target_pairs={{0,64},{64,128},{128,192},{192,256},{256,320},{320,384},{384,448},... | collective-permute-start | bytes 147464 | tf_op jit(solution)/shard_map/ppermute | solution.py:15
  54.2 2.9 collective-permute-done.4
  58.1 1.6 pad_maximum_fusion.2
  63.4 2.7 collective-permute-start.7
  66.1 3.2 collective-permute-start.6
  71.9 3.8 %collective-permute-done.6 = bf16[32,1,768]{2,0,1:T(8,128)(2,1)S(1)} collective-permute-done((bf16[32,1,768]{2,0,1:T(8,128)(2,1)S(1)}, bf16[32,1,768]{2,0,1:T(8,128)(2,1)S(1)}, u32[]{:S(2)}, u32[]{:S(2)}) %collective-permute-start.6) | collective-permute-done | bytes 49184 | tf_op jit(solution)/shard_map/ppermute | solution.py:15
  76.8 1.6 pad_maximum_fusion.3
  81.5 2.5 collective-permute-start.9
  84.0 3.5 %collective-permute-start.8 = (bf16[32,1,768]{2,0,1:T(8,128)(2,1)S(1)}, bf16[32,1,768]{2,0,1:T(8,128)(2,1)S(1)}, u32[]{:S(2)}, u32[]{:S(2)}) collective-permute-start(bf16[32,1,768]{2,0,1:T(8,128)(2,1)S(1)} %bitcast.336), channel_id=1, source_target_pairs={{0,64},{64,128},{128,192},{192,256},{256,320},{320,384},{384,448},... | collective-permute-start | bytes 147464 | tf_op jit(solution)/shard_map/ppermute | solution.py:15
  89.7 3.9 %collective-permute-done.8 = bf16[32,1,768]{2,0,1:T(8,128)(2,1)S(1)} collective-permute-done((bf16[32,1,768]{2,0,1:T(8,128)(2,1)S(1)}, bf16[32,1,768]{2,0,1:T(8,128)(2,1)S(1)}, u32[]{:S(2)}, u32[]{:S(2)}) %collective-permute-start.8) | collective-permute-done | bytes 49184 | tf_op jit(solution)/shard_map/ppermute | solution.py:15
  94.1 1.6 pad_maximum_fusion.4
  99.6 2.3 collective-permute-start.11
  101.8 3.6 %collective-permute-start.10 = (bf16[32,1,768]{2,0,1:T(8,128)(2,1)S(1)}, bf16[32,1,768]{2,0,1:T(8,128)(2,1)S(1)}, u32[]{:S(2)}, u32[]{:S(2)}) collective-permute-start(bf16[32,1,768]{2,0,1:T(8,128)(2,1)S(1)} %subtract_convert_fusion.6), channel_id=1, source_target_pairs={{0,64},{64,128},{128,192},{192,256},{256,320},{320,384},{384,448},... | collective-permute-start | bytes 147464 | tf_op jit(solution)/shard_map/ppermute | solution.py:15
  107.4 4.0 %collective-permute-done.10 = bf16[32,1,768]{2,0,1:T(8,128)(2,1)S(1)} collective-permute-done((bf16[32,1,768]{2,0,1:T(8,128)(2,1)S(1)}, bf16[32,1,768]{2,0,1:T(8,128)(2,1)S(1)}, u32[]{:S(2)}, u32[]{:S(2)}) %collective-permute-start.10) | collective-permute-done | bytes 49184 | tf_op jit(solution)/shard_map/ppermute | solution.py:15
  111.9 1.6 pad_maximum_fusion.5
  116.6 1.9 collective-permute-start.13
  118.5 3.9 %collective-permute-start.12 = (bf16[32,1,768]{2,0,1:T(8,128)(2,1)S(1)}, bf16[32,1,768]{2,0,1:T(8,128)(2,1)S(1)}, u32[]{:S(2)}, u32[]{:S(2)}) collective-permute-start(bf16[32,1,768]{2,0,1:T(8,128)(2,1)S(1)} %bitcast.334), channel_id=1, source_target_pairs={{0,64},{64,128},{128,192},{192,256},{256,320},{320,384},{384,448},... | collective-permute-start | bytes 147464 | tf_op jit(solution)/shard_map/ppermute | solution.py:15
  124.0 4.1 %collective-permute-done.12 = bf16[32,1,768]{2,0,1:T(8,128)(2,1)S(1)} collective-permute-done((bf16[32,1,768]{2,0,1:T(8,128)(2,1)S(1)}, bf16[32,1,768]{2,0,1:T(8,128)(2,1)S(1)}, u32[]{:S(2)}, u32[]{:S(2)}) %collective-permute-start.12) | collective-permute-done | bytes 49184 | tf_op jit(solution)/shard_map/ppermute | solution.py:15
  128.6 1.6 pad_maximum_fusion.6
  133.2 1.9 collective-permute-start.15
  135.2 3.9 %collective-permute-start.14 = (bf16[32,1,768]{2,0,1:T(8,128)(2,1)S(1)}, bf16[32,1,768]{2,0,1:T(8,128)(2,1)S(1)}, u32[]{:S(2)}, u32[]{:S(2)}) collective-permute-start(bf16[32,1,768]{2,0,1:T(8,128)(2,1)S(1)} %subtract_convert_fusion.4), channel_id=1, source_target_pairs={{0,64},{64,128},{128,192},{192,256},{256,320},{320,384},{384,448},... | collective-permute-start | bytes 147464 | tf_op jit(solution)/shard_map/ppermute | solution.py:15
  140.4 4.3 %collective-permute-done.14 = bf16[32,1,768]{2,0,1:T(8,128)(2,1)S(1)} collective-permute-done((bf16[32,1,768]{2,0,1:T(8,128)(2,1)S(1)}, bf16[32,1,768]{2,0,1:T(8,128)(2,1)S(1)}, u32[]{:S(2)}, u32[]{:S(2)}) %collective-permute-start.14) | collective-permute-done | bytes 49184 | tf_op jit(solution)/shard_map/ppermute | solution.py:15
  145.3 1.6 pad_maximum_fusion.7
  148.1 1.6 convolution_bitcast_fusion
  150.1 1.9 collective-permute-start.16
  153.2 3.2 %collective-permute-start.17 = (bf16[2,2,32,96]{3,2,1,0:T(8,128)(2,1)S(1)}, bf16[2,2,32,96]{3,2,1,0:T(8,128)(2,1)S(1)}, u32[]{:S(2)}, u32[]{:S(2)}) collective-permute-start(bf16[2,2,32,96]{3,2,1,0:T(8,128)(2,1)S(1)} %dynamic-slice_bitcast_fusion.1), channel_id=1, source_target_pairs={{0,2},{1,3},{2,0},{3,1},{4,6},{5,7},{6,4},{7,5},{8,10},{9,11},{10,... | collective-permute-start | bytes 73736 | tf_op jit(solution)/shard_map/ppermute | solution.py:26
  157.5 2.6 collective-permute-start.23
  160.2 3.8 %collective-permute-start.18 = (bf16[1,4,32,96]{3,2,1,0:T(8,128)(2,1)S(1)}, bf16[1,4,32,96]{3,2,1,0:T(8,128)(2,1)S(1)}, u32[]{:S(2)}, u32[]{:S(2)}) collective-permute-start(bf16[1,4,32,96]{3,2,1,0:T(8,128)(2,1)S(1)} %dynamic-slice_bitcast_fusion), channel_id=1, source_target_pairs={{0,4},{1,5},{2,6},{3,7},{4,0},{5,1},{6,2},{7,3},{8,12},{9,13},{10,... | collective-permute-start | bytes 73736 | tf_op jit(solution)/shard_map/ppermute | solution.py:26
  164.1 1.8 collective-permute-done.18
  166.0 5.2 %collective-permute-start.19 = (bf16[256,96]{1,0:T(8,128)(2,1)S(1)}, bf16[256,96]{1,0:T(8,128)(2,1)S(1)}, u32[]{:S(2)}, u32[]{:S(2)}) collective-permute-start(bf16[256,96]{1,0:T(8,128)(2,1)S(1)} %bitcast.331), channel_id=1, source_target_pairs={{0,8},{1,9},{2,10},{3,11},{4,12},{5,13},{6,14},{7,15},{8,0},{9,1},... | collective-permute-start | bytes 147464 | tf_op jit(solution)/shard_map/ppermute | solution.py:26
  171.3 4.0 %collective-permute-start.24 = (bf16[2048,128]{0,1:T(8,128)(2,1)S(1)}, bf16[2048,128]{0,1:T(8,128)(2,1)S(1)}, u32[]{:S(2)}, u32[]{:S(2)}) collective-permute-start(bf16[2048,128]{0,1:T(8,128)(2,1)S(1)} %maximum_select_fusion.4), channel_id=1, source_target_pairs={{0,4},{1,5},{2,6},{3,7},{4,0},{5,1},{6,2},{7,3},{8,12},{9,13},{10,... | collective-permute-start | bytes 1572872 | tf_op jit(solution)/shard_map/ppermute | solution.py:26
  175.4 9.1 %collective-permute-start.20 = (bf16[512,96]{1,0:T(8,128)(2,1)S(1)}, bf16[512,96]{1,0:T(8,128)(2,1)S(1)}, u32[]{:S(2)}, u32[]{:S(2)}) collective-permute-start(bf16[512,96]{1,0:T(8,128)(2,1)S(1)} %maximum_select_fusion.7), channel_id=1, source_target_pairs={{0,16},{1,17},{2,18},{3,19},{4,20},{5,21},{6,22},{7,23},{8,24},{9,... | collective-permute-start | bytes 294920 | tf_op jit(solution)/shard_map/ppermute | solution.py:26
  184.5 4.7 %collective-permute-done.20 = bf16[512,96]{1,0:T(8,128)(2,1)S(1)} collective-permute-done((bf16[512,96]{1,0:T(8,128)(2,1)S(1)}, bf16[512,96]{1,0:T(8,128)(2,1)S(1)}, u32[]{:S(2)}, u32[]{:S(2)}) %collective-permute-start.20) | collective-permute-done | bytes 98336 | tf_op jit(solution)/shard_map/ppermute | solution.py:26
  189.4 13.9 %collective-permute-start.21 = (bf16[1024,96]{1,0:T(8,128)(2,1)S(1)}, bf16[1024,96]{1,0:T(8,128)(2,1)S(1)}, u32[]{:S(2)}, u32[]{:S(2)}) collective-permute-start(bf16[1024,96]{1,0:T(8,128)(2,1)S(1)} %maximum_select_fusion.5), channel_id=1, source_target_pairs={{0,32},{1,33},{2,34},{3,35},{4,36},{5,37},{6,38},{7,39},{8,40},{9,... | collective-permute-start | bytes 589832 | tf_op jit(solution)/shard_map/ppermute | solution.py:26
  203.4 4.8 %collective-permute-done.21 = bf16[1024,96]{1,0:T(8,128)(2,1)S(1)} collective-permute-done((bf16[1024,96]{1,0:T(8,128)(2,1)S(1)}, bf16[1024,96]{1,0:T(8,128)(2,1)S(1)}, u32[]{:S(2)}, u32[]{:S(2)}) %collective-permute-start.21) | collective-permute-done | bytes 196640 | tf_op jit(solution)/shard_map/ppermute | solution.py:26
  208.8 7.5 %gather_fusion = bf16[2304,256]{1,0:T(8,128)(2,1)} fusion(bf16[96,256]{1,0:T(8,128)(2,1)S(1)} %convolution_convert_fusion.24, s32[3072]{0:T(1024)S(1)} %pad_clamp_fusion), kind=kCustom, calls=%fused_computation | custom fusion | bytes 2368512 | tf_op jit(solution)/shard_map/jit(_take)/gather | solution.py:119
  216.3 2.9 gather.7
  219.2 2.7 select_select_fusion
  221.9 98.7 %all_to_all.5 = bf16[64,36,256]{2,1,0:T(8,128)(2,1)S(1)} all-to-all(bf16[64,36,256]{2,1,0:T(8,128)(2,1)S(1)} %select_select_fusion), channel_id=1, replica_groups=mesh['elem'=8,'band'=64] {'band'}, dimensions={0} | all-to-all | bytes 2359296 | tf_op jit(solution)/shard_map/all_to_all | solution.py:121
  (203 shorter events, 54.8 us)
Async XLA Ops:
  0.6 21.1 %copy-start = (bf16[4,7,192,192]{3,2,1,0:T(8,128)(2,1)S(1)}, bf16[4,7,192,192]{3,2,1,0:T(8,128)(2,1)}, u32[]{:S(2)}) copy-start(bf16[4,7,192,192]{3,2,1,0:T(8,128)(2,1)} %param.7) | copy-start | bytes 6193156
  1.5 21.7 %copy-start.15 = (f32[4,192]{1,0:T(4,128)}, f32[4,192]{1,0:T(4,128)S(1)}, u32[]{:S(2)}) copy-start(f32[4,192]{1,0:T(4,128)S(1)} %fusion.66) | copy-start | bytes 9220
  1.6 21.9 %copy-start.3 = (f32[768]{0:T(1024)}, f32[768]{0:T(1024)S(1)}, u32[]{:S(2)}) copy-start(f32[768]{0:T(1024)S(1)} %reshape.862) | copy-start | bytes 9220
  2.4 15.4 %collective-permute-start.1 = (bf16[32,1,768]{2,0,1:T(8,128)(2,1)S(1)}, bf16[32,1,768]{2,0,1:T(8,128)(2,1)S(1)}, u32[]{:S(2)}, u32[]{:S(2)}) collective-permute-start(bf16[32,1,768]{2,0,1:T(8,128)(2,1)S(1)} %fusion.100), channel_id=1, source_target_pairs={{64,0},{128,64},{192,128},{256,192},{320,256},{384,320},{448,384},... | collective-permute-start | bytes 147464 | tf_op jit(solution)/shard_map/ppermute | solution.py:18
  8.8 9.6 %collective-permute-start = (bf16[32,1,768]{2,0,1:T(8,128)(2,1)S(1)}, bf16[32,1,768]{2,0,1:T(8,128)(2,1)S(1)}, u32[]{:S(2)}, u32[]{:S(2)}) collective-permute-start(bf16[32,1,768]{2,0,1:T(8,128)(2,1)S(1)} %fusion.100), channel_id=1, source_target_pairs={{0,64},{64,128},{128,192},{192,256},{256,320},{320,384},{384,448},... | collective-permute-start | bytes 147464 | tf_op jit(solution)/shard_map/ppermute | solution.py:15
  10.8 145.7 %collective-permute-start.22 = (bf16[2048,32]{0,1:T(8,128)(2,1)}, bf16[2048,32]{0,1:T(8,128)(2,1)}, u32[]{:S(2)}, u32[]{:S(2)}) collective-permute-start(bf16[2048,32]{0,1:T(8,128)(2,1)} %param.11), channel_id=1, source_target_pairs={{0,1},{1,0},{2,3},{3,2},{4,5},{5,4},{6,7},{7,6},{8,9},{9,8},{10,11... | collective-permute-start | bytes 393224 | tf_op jit(solution)/shard_map/ppermute | solution.py:26
  14.3 26.1 %copy-start.19 = (pred[1,4,6,4]{3,1,2,0:T(4,128)(4,1)}, pred[1,4,6,4]{3,1,2,0:T(4,128)(4,1)S(1)}, u32[]{:S(2)}) copy-start(pred[1,4,6,4]{3,1,2,0:T(4,128)(4,1)S(1)} %iota_compare_fusion.1) | copy-start | bytes 292
  14.4 18.3 %copy-start.10 = (pred[1,4,4,4]{3,1,2,0:T(4,128)(4,1)}, pred[1,4,4,4]{3,1,2,0:T(4,128)(4,1)S(1)}, u32[]{:S(2)}) copy-start(pred[1,4,4,4]{3,1,2,0:T(4,128)(4,1)S(1)} %slice.11) | copy-start | bytes 196
  23.5 10.9 %collective-permute-start.3 = (bf16[32,1,768]{2,0,1:T(8,128)(2,1)S(1)}, bf16[32,1,768]{2,0,1:T(8,128)(2,1)S(1)}, u32[]{:S(2)}, u32[]{:S(2)}) collective-permute-start(bf16[32,1,768]{2,0,1:T(8,128)(2,1)S(1)} %multiply_convert_fusion.1), channel_id=1, source_target_pairs={{64,0},{128,64},{192,128},{256,192},{320,256},{384,320},{448,384},... | collective-permute-start | bytes 147464 | tf_op jit(solution)/shard_map/ppermute | solution.py:18
  30.7 9.6 %collective-permute-start.2 = (bf16[32,1,768]{2,0,1:T(8,128)(2,1)S(1)}, bf16[32,1,768]{2,0,1:T(8,128)(2,1)S(1)}, u32[]{:S(2)}, u32[]{:S(2)}) collective-permute-start(bf16[32,1,768]{2,0,1:T(8,128)(2,1)S(1)} %multiply_convert_fusion.1), channel_id=1, source_target_pairs={{0,64},{64,128},{128,192},{192,256},{256,320},{320,384},{384,448},... | collective-permute-start | bytes 147464 | tf_op jit(solution)/shard_map/ppermute | solution.py:15
  40.8 4.6 %copy-start.4 = (f32[768]{0:T(1024)S(1)}, f32[768]{0:T(1024)}, u32[]{:S(2)}) copy-start(f32[768]{0:T(1024)} %copy-done.3) | copy-start | bytes 9220
  40.8 4.6 %copy-start.7 = (bf16[32,768]{1,0:T(8,128)(2,1)S(1)}, bf16[32,768]{1,0:T(8,128)(2,1)}, u32[]{:S(2)}) copy-start(bf16[32,768]{1,0:T(8,128)(2,1)} %param.6) | copy-start | bytes 147460
  43.7 7.8 %copy-start.11 = (pred[1,4,4,4]{3,1,2,0:T(4,128)(4,1)S(1)}, pred[1,4,4,4]{3,1,2,0:T(4,128)(4,1)}, u32[]{:S(2)}) copy-start(pred[1,4,4,4]{3,1,2,0:T(4,128)(4,1)} %copy-done.10) | copy-start | bytes 196
  45.5 7.8 %collective-permute-start.5 = (bf16[32,1,768]{2,0,1:T(8,128)(2,1)S(1)}, bf16[32,1,768]{2,0,1:T(8,128)(2,1)S(1)}, u32[]{:S(2)}, u32[]{:S(2)}) collective-permute-start(bf16[32,1,768]{2,0,1:T(8,128)(2,1)S(1)} %bitcast.337), channel_id=1, source_target_pairs={{64,0},{128,64},{192,128},{256,192},{320,256},{384,320},{448,384},... | collective-permute-start | bytes 147464 | tf_op jit(solution)/shard_map/ppermute | solution.py:18
  47.4 9.6 %collective-permute-start.4 = (bf16[32,1,768]{2,0,1:T(8,128)(2,1)S(1)}, bf16[32,1,768]{2,0,1:T(8,128)(2,1)S(1)}, u32[]{:S(2)}, u32[]{:S(2)}) collective-permute-start(bf16[32,1,768]{2,0,1:T(8,128)(2,1)S(1)} %bitcast.338), channel_id=1, source_target_pairs={{0,64},{64,128},{128,192},{192,256},{256,320},{320,384},{384,448},... | collective-permute-start | bytes 147464 | tf_op jit(solution)/shard_map/ppermute | solution.py:15
  61.0 8.3 %copy-start.12 = (pred[1,4,4,4]{3,1,2,0:T(4,128)(4,1)S(1)}, pred[1,4,4,4]{3,1,2,0:T(4,128)(4,1)}, u32[]{:S(2)}) copy-start(pred[1,4,4,4]{3,1,2,0:T(4,128)(4,1)} %copy-done.10) | copy-start | bytes 196
  63.4 13.3 %copy-start.9 = (bf16[32,1,768]{2,0,1:T(8,128)(2,1)}, bf16[32,1,768]{2,0,1:T(8,128)(2,1)S(1)}, u32[]{:S(2)}) copy-start(bf16[32,1,768]{2,0,1:T(8,128)(2,1)S(1)} %subtract_convert_fusion.8) | copy-start | bytes 147460
  63.4 7.6 %collective-permute-start.7 = (bf16[32,1,768]{2,0,1:T(8,128)(2,1)S(1)}, bf16[32,1,768]{2,0,1:T(8,128)(2,1)S(1)}, u32[]{:S(2)}, u32[]{:S(2)}) collective-permute-start(bf16[32,1,768]{2,0,1:T(8,128)(2,1)S(1)} %subtract_convert_fusion.8), channel_id=1, source_target_pairs={{64,0},{128,64},{192,128},{256,192},{320,256},{384,320},{448,384},... | collective-permute-start | bytes 147464 | tf_op jit(solution)/shard_map/ppermute | solution.py:18
  66.1 9.6 %collective-permute-start.6 = (bf16[32,1,768]{2,0,1:T(8,128)(2,1)S(1)}, bf16[32,1,768]{2,0,1:T(8,128)(2,1)S(1)}, u32[]{:S(2)}, u32[]{:S(2)}) collective-permute-start(bf16[32,1,768]{2,0,1:T(8,128)(2,1)S(1)} %subtract_convert_fusion.8), channel_id=1, source_target_pairs={{0,64},{64,128},{128,192},{192,256},{256,320},{320,384},{384,448},... | collective-permute-start | bytes 147464 | tf_op jit(solution)/shard_map/ppermute | solution.py:15
  76.8 4.6 %copy-start.5 = (f32[768]{0:T(1024)S(1)}, f32[768]{0:T(1024)}, u32[]{:S(2)}) copy-start(f32[768]{0:T(1024)} %copy-done.3) | copy-start | bytes 9220
  78.5 9.2 %copy-start.13 = (pred[1,4,4,4]{3,1,2,0:T(4,128)(4,1)S(1)}, pred[1,4,4,4]{3,1,2,0:T(4,128)(4,1)}, u32[]{:S(2)}) copy-start(pred[1,4,4,4]{3,1,2,0:T(4,128)(4,1)} %copy-done.10) | copy-start | bytes 196
  78.5 11.1 %copy-start.20 = (pred[1,4,6,4]{3,1,2,0:T(4,128)(4,1)S(1)}, pred[1,4,6,4]{3,1,2,0:T(4,128)(4,1)}, u32[]{:S(2)}) copy-start(pred[1,4,6,4]{3,1,2,0:T(4,128)(4,1)} %copy-done.19) | copy-start | bytes 292
  81.2 15.7 %copy-start.16 = (f32[4,192]{1,0:T(4,128)S(1)}, f32[4,192]{1,0:T(4,128)}, u32[]{:S(2)}) copy-start(f32[4,192]{1,0:T(4,128)} %copy-done.15) | copy-start | bytes 9220
  81.5 7.9 %collective-permute-start.9 = (bf16[32,1,768]{2,0,1:T(8,128)(2,1)S(1)}, bf16[32,1,768]{2,0,1:T(8,128)(2,1)S(1)}, u32[]{:S(2)}, u32[]{:S(2)}) collective-permute-start(bf16[32,1,768]{2,0,1:T(8,128)(2,1)S(1)} %bitcast.335), channel_id=1, source_target_pairs={{64,0},{128,64},{192,128},{256,192},{320,256},{384,320},{448,384},... | collective-permute-start | bytes 147464 | tf_op jit(solution)/shard_map/ppermute | solution.py:18
  84.0 9.6 %collective-permute-start.8 = (bf16[32,1,768]{2,0,1:T(8,128)(2,1)S(1)}, bf16[32,1,768]{2,0,1:T(8,128)(2,1)S(1)}, u32[]{:S(2)}, u32[]{:S(2)}) collective-permute-start(bf16[32,1,768]{2,0,1:T(8,128)(2,1)S(1)} %bitcast.336), channel_id=1, source_target_pairs={{0,64},{64,128},{128,192},{192,256},{256,320},{320,384},{384,448},... | collective-permute-start | bytes 147464 | tf_op jit(solution)/shard_map/ppermute | solution.py:15
  99.6 7.6 %collective-permute-start.11 = (bf16[32,1,768]{2,0,1:T(8,128)(2,1)S(1)}, bf16[32,1,768]{2,0,1:T(8,128)(2,1)S(1)}, u32[]{:S(2)}, u32[]{:S(2)}) collective-permute-start(bf16[32,1,768]{2,0,1:T(8,128)(2,1)S(1)} %subtract_convert_fusion.6), channel_id=1, source_target_pairs={{64,0},{128,64},{192,128},{256,192},{320,256},{384,320},{448,384},... | collective-permute-start | bytes 147464 | tf_op jit(solution)/shard_map/ppermute | solution.py:18
  101.8 9.6 %collective-permute-start.10 = (bf16[32,1,768]{2,0,1:T(8,128)(2,1)S(1)}, bf16[32,1,768]{2,0,1:T(8,128)(2,1)S(1)}, u32[]{:S(2)}, u32[]{:S(2)}) collective-permute-start(bf16[32,1,768]{2,0,1:T(8,128)(2,1)S(1)} %subtract_convert_fusion.6), channel_id=1, source_target_pairs={{0,64},{64,128},{128,192},{192,256},{256,320},{320,384},{384,448},... | collective-permute-start | bytes 147464 | tf_op jit(solution)/shard_map/ppermute | solution.py:15
  113.6 10.2 %copy-start.21 = (pred[1,4,6,4]{3,1,2,0:T(4,128)(4,1)S(1)}, pred[1,4,6,4]{3,1,2,0:T(4,128)(4,1)}, u32[]{:S(2)}) copy-start(pred[1,4,6,4]{3,1,2,0:T(4,128)(4,1)} %copy-done.19) | copy-start | bytes 292
  116.3 15.1 %copy-start.17 = (f32[4,192]{1,0:T(4,128)S(1)}, f32[4,192]{1,0:T(4,128)}, u32[]{:S(2)}) copy-start(f32[4,192]{1,0:T(4,128)} %copy-done.15) | copy-start | bytes 9220
  116.6 11.9 %copy-start.1 = (bf16[32,768]{1,0:T(8,128)(2,1)}, bf16[32,768]{1,0:T(8,128)(2,1)S(1)}, u32[]{:S(2)}) copy-start(bf16[32,768]{1,0:T(8,128)(2,1)S(1)} %subtract_convert_fusion.5) | copy-start | bytes 147460
  116.6 7.1 %collective-permute-start.13 = (bf16[32,1,768]{2,0,1:T(8,128)(2,1)S(1)}, bf16[32,1,768]{2,0,1:T(8,128)(2,1)S(1)}, u32[]{:S(2)}, u32[]{:S(2)}) collective-permute-start(bf16[32,1,768]{2,0,1:T(8,128)(2,1)S(1)} %bitcast.333), channel_id=1, source_target_pairs={{64,0},{128,64},{192,128},{256,192},{320,256},{384,320},{448,384},... | collective-permute-start | bytes 147464 | tf_op jit(solution)/shard_map/ppermute | solution.py:18
  118.5 9.6 %collective-permute-start.12 = (bf16[32,1,768]{2,0,1:T(8,128)(2,1)S(1)}, bf16[32,1,768]{2,0,1:T(8,128)(2,1)S(1)}, u32[]{:S(2)}, u32[]{:S(2)}) collective-permute-start(bf16[32,1,768]{2,0,1:T(8,128)(2,1)S(1)} %bitcast.334), channel_id=1, source_target_pairs={{0,64},{64,128},{128,192},{192,256},{256,320},{320,384},{384,448},... | collective-permute-start | bytes 147464 | tf_op jit(solution)/shard_map/ppermute | solution.py:15
  130.2 8.8 %copy-start.14 = (pred[1,4,4,4]{3,1,2,0:T(4,128)(4,1)S(1)}, pred[1,4,4,4]{3,1,2,0:T(4,128)(4,1)}, u32[]{:S(2)}) copy-start(pred[1,4,4,4]{3,1,2,0:T(4,128)(4,1)} %copy-done.10) | copy-start | bytes 196
  133.2 6.9 %collective-permute-start.15 = (bf16[32,1,768]{2,0,1:T(8,128)(2,1)S(1)}, bf16[32,1,768]{2,0,1:T(8,128)(2,1)S(1)}, u32[]{:S(2)}, u32[]{:S(2)}) collective-permute-start(bf16[32,1,768]{2,0,1:T(8,128)(2,1)S(1)} %subtract_convert_fusion.4), channel_id=1, source_target_pairs={{64,0},{128,64},{192,128},{256,192},{320,256},{384,320},{448,384},... | collective-permute-start | bytes 147464 | tf_op jit(solution)/shard_map/ppermute | solution.py:18
  135.2 9.6 %collective-permute-start.14 = (bf16[32,1,768]{2,0,1:T(8,128)(2,1)S(1)}, bf16[32,1,768]{2,0,1:T(8,128)(2,1)S(1)}, u32[]{:S(2)}, u32[]{:S(2)}) collective-permute-start(bf16[32,1,768]{2,0,1:T(8,128)(2,1)S(1)} %subtract_convert_fusion.4), channel_id=1, source_target_pairs={{0,64},{64,128},{128,192},{192,256},{256,320},{320,384},{384,448},... | collective-permute-start | bytes 147464 | tf_op jit(solution)/shard_map/ppermute | solution.py:15
  145.3 4.6 %copy-start.6 = (f32[768]{0:T(1024)S(1)}, f32[768]{0:T(1024)}, u32[]{:S(2)}) copy-start(f32[768]{0:T(1024)} %copy-done.3) | copy-start | bytes 9220
  146.9 5.1 %copy-start.23 = (s32[64]{0:T(128)S(1)}, s32[64]{0:T(128)}, u32[]{:S(2)}) copy-start(s32[64]{0:T(128)} %sub.136) | copy-start | bytes 772
  148.1 8.4 %copy-start.18 = (bf16[2048,32]{0,1:T(8,128)(2,1)S(1)}, bf16[2048,32]{0,1:T(8,128)(2,1)}, u32[]{:S(2)}) copy-start(bf16[2048,32]{0,1:T(8,128)(2,1)} %param.11) | copy-start | bytes 393220
  149.6 53.7 %copy-start.22 = (s32[64]{0:T(128)S(1)}, s32[64]{0:T(128)}, u32[]{:S(2)}) copy-start(s32[64]{0:T(128)} %param.10) | copy-start | bytes 772
  149.9 58.9 %copy-start.8 = (bf16[32,768]{1,0:T(8,128)(2,1)}, bf16[32,768]{1,0:T(8,128)(2,1)S(1)}, u32[]{:S(2)}) copy-start(bf16[32,768]{1,0:T(8,128)(2,1)S(1)} %subtract_convert_fusion.3) | copy-start | bytes 147460
  150.1 3.1 collective-permute-start.16
  153.2 6.9 %collective-permute-start.17 = (bf16[2,2,32,96]{3,2,1,0:T(8,128)(2,1)S(1)}, bf16[2,2,32,96]{3,2,1,0:T(8,128)(2,1)S(1)}, u32[]{:S(2)}, u32[]{:S(2)}) collective-permute-start(bf16[2,2,32,96]{3,2,1,0:T(8,128)(2,1)S(1)} %dynamic-slice_bitcast_fusion.1), channel_id=1, source_target_pairs={{0,2},{1,3},{2,0},{3,1},{4,6},{5,7},{6,4},{7,5},{8,10},{9,11},{10,... | collective-permute-start | bytes 73736 | tf_op jit(solution)/shard_map/ppermute | solution.py:26
  157.5 13.6 %collective-permute-start.23 = (bf16[2048,64]{0,1:T(8,128)(2,1)S(1)}, bf16[2048,64]{0,1:T(8,128)(2,1)S(1)}, u32[]{:S(2)}, u32[]{:S(2)}) collective-permute-start(bf16[2048,64]{0,1:T(8,128)(2,1)S(1)} %maximum_select_fusion.6), channel_id=1, source_target_pairs={{0,2},{1,3},{2,0},{3,1},{4,6},{5,7},{6,4},{7,5},{8,10},{9,11},{10,... | collective-permute-start | bytes 786440 | tf_op jit(solution)/shard_map/ppermute | solution.py:26
  160.2 5.8 %collective-permute-start.18 = (bf16[1,4,32,96]{3,2,1,0:T(8,128)(2,1)S(1)}, bf16[1,4,32,96]{3,2,1,0:T(8,128)(2,1)S(1)}, u32[]{:S(2)}, u32[]{:S(2)}) collective-permute-start(bf16[1,4,32,96]{3,2,1,0:T(8,128)(2,1)S(1)} %dynamic-slice_bitcast_fusion), channel_id=1, source_target_pairs={{0,4},{1,5},{2,6},{3,7},{4,0},{5,1},{6,2},{7,3},{8,12},{9,13},{10,... | collective-permute-start | bytes 73736 | tf_op jit(solution)/shard_map/ppermute | solution.py:26
  166.0 9.4 %collective-permute-start.19 = (bf16[256,96]{1,0:T(8,128)(2,1)S(1)}, bf16[256,96]{1,0:T(8,128)(2,1)S(1)}, u32[]{:S(2)}, u32[]{:S(2)}) collective-permute-start(bf16[256,96]{1,0:T(8,128)(2,1)S(1)} %bitcast.331), channel_id=1, source_target_pairs={{0,8},{1,9},{2,10},{3,11},{4,12},{5,13},{6,14},{7,15},{8,0},{9,1},... | collective-permute-start | bytes 147464 | tf_op jit(solution)/shard_map/ppermute | solution.py:26
  171.3 37.0 %collective-permute-start.24 = (bf16[2048,128]{0,1:T(8,128)(2,1)S(1)}, bf16[2048,128]{0,1:T(8,128)(2,1)S(1)}, u32[]{:S(2)}, u32[]{:S(2)}) collective-permute-start(bf16[2048,128]{0,1:T(8,128)(2,1)S(1)} %maximum_select_fusion.4), channel_id=1, source_target_pairs={{0,4},{1,5},{2,6},{3,7},{4,0},{5,1},{6,2},{7,3},{8,12},{9,13},{10,... | collective-permute-start | bytes 1572872 | tf_op jit(solution)/shard_map/ppermute | solution.py:26
  175.4 13.8 %collective-permute-start.20 = (bf16[512,96]{1,0:T(8,128)(2,1)S(1)}, bf16[512,96]{1,0:T(8,128)(2,1)S(1)}, u32[]{:S(2)}, u32[]{:S(2)}) collective-permute-start(bf16[512,96]{1,0:T(8,128)(2,1)S(1)} %maximum_select_fusion.7), channel_id=1, source_target_pairs={{0,16},{1,17},{2,18},{3,19},{4,20},{5,21},{6,22},{7,23},{8,24},{9,... | collective-permute-start | bytes 294920 | tf_op jit(solution)/shard_map/ppermute | solution.py:26
  189.4 18.9 %collective-permute-start.21 = (bf16[1024,96]{1,0:T(8,128)(2,1)S(1)}, bf16[1024,96]{1,0:T(8,128)(2,1)S(1)}, u32[]{:S(2)}, u32[]{:S(2)}) collective-permute-start(bf16[1024,96]{1,0:T(8,128)(2,1)S(1)} %maximum_select_fusion.5), channel_id=1, source_target_pairs={{0,32},{1,33},{2,34},{3,35},{4,36},{5,37},{6,38},{7,39},{8,40},{9,... | collective-permute-start | bytes 589832 | tf_op jit(solution)/shard_map/ppermute | solution.py:26
  (1 other events, 3.0 us)
where the time goes:
time: 323 us; the launch traced here: 322 us
  blocking collectives  98.7 us (31%)
  starting transfers between devices  98.4 us (30%)
  waiting for transfers between devices  41.3 us (13%)
  local copies, waits for them, and re-layouts  34.1 us (11%)
  matrix products  24.1 us (7%)
  other arithmetic  23.1 us (7%)
    all_to_all x1, blocking collectives, per_device(): lax.all_to_all(pieces, 'band', split_axis=0, concat_axis=0, tiled=True)  98.7 us
    ppermute x9, starting transfers between devices, from_partner(): return lax.ppermute(value, axis, pairs)  45.8 us
    ppermute x8, waiting for transfers between devices, padded(): lax.ppermute(lax.slice_in_dim(block, block.shape[dim] - width, None, axis...  28.9 us
    ppermute x8, starting transfers between devices, padded(): lax.ppermute(lax.slice_in_dim(block, 0, width, axis=dim), axis, backward)  26.8 us
    ppermute x8, starting transfers between devices, padded(): lax.ppermute(lax.slice_in_dim(block, block.shape[dim] - width, None, axis...  25.9 us
    concatenate x8, other arithmetic, apply_ham(): jnp.concatenate([plane_mid[:, :, :, None], inplane, lower[:, :, :, None],...  13 us
    ppermute x9, waiting for transfers between devices, from_partner(): return lax.ppermute(value, axis, pairs)  12.3 us
    dot_general x8, matrix products, apply_ham(): jnp.einsum('bej,ejl->bel', sources, weights, preferred_element_type=jnp.f...  12.3 us
  transfers between devices with their start and end apart: 25, of which 12 were waited for; matrix products, arithmetic and copies ran while one was open for 20% of the time, Pallas kernels for 0%

commit v1 on v0

v1 whole, which is shorter than its diff:
```python
import jax
import jax.numpy as jnp
from jax import lax
from jax.experimental import pallas as pl
from jax.experimental.pallas import tpu as pltpu
from jax.sharding import Mesh
from jax.sharding import PartitionSpec as P

DEGREE = 8
NB = 192
ELEMS_DEV = 4
ROWS = ELEMS_DEV * NB
BANDS_DEV = 32
CAP = 36
CAP_PAD = 40
Z = 16
QUAD = 4
BF16 = jnp.bfloat16
F32 = jnp.float32
BAND_AXES = ("z", "yl", "c")

VMEM = pl.BlockSpec(memory_space=pltpu.VMEM)
SMEM = pl.BlockSpec(memory_space=pltpu.SMEM)


def params(mib):
    return pltpu.CompilerParams(vmem_limit_bytes=mib << 20)


def lanes(i):
    return slice(NB * i, NB * (i + 1))


def column_mask(count, rows):
    return lax.broadcasted_iota(jnp.int32, (rows, NB), 1) < count


def mask_kernel(counts, start_ref, y_ref):
    for i in range(ELEMS_DEV):
        block = start_ref[:, lanes(i)]
        y_ref[:, lanes(i)] = jnp.where(
            column_mask(counts[i], BANDS_DEV), block, jnp.zeros_like(block)
        )


def couple_kernel(neighbours, counts, parity, h_ref, even_ref, odd_ref):
    even_ref[...] = jnp.zeros_like(even_ref)
    odd_ref[...] = jnp.zeros_like(odd_ref)
    slot_even = 6 - parity[0]
    slot_odd = 5 + parity[0]
    for i in range(ELEMS_DEV):
        keep = column_mask(counts[i], NB)
        for slot, out_ref in ((slot_even, even_ref), (slot_odd, odd_ref)):
            block = h_ref[i, slot]
            block = jnp.where(keep, block, jnp.zeros_like(block))
            source = neighbours[i, slot - 1]
            out_ref[pl.ds(pl.multiple_of(source * NB, NB), NB), lanes(i)] = block


def local_kernel(scale, has_prev, neighbours, counts, y_ref, *refs):
    if has_prev:
        prev_ref, h_ref, p_ref, split = refs
    else:
        h_ref, p_ref, split = refs
    for i in range(ELEMS_DEV):
        split[i] = y_ref[:, lanes(i)]
    for i in range(ELEMS_DEV):
        total = jnp.dot(split[i], h_ref[i, 0], preferred_element_type=F32)
        for slot in range(4):
            total += jnp.dot(
                split[neighbours[i, slot]], h_ref[i, slot + 1], preferred_element_type=F32
            )
        total = jnp.where(column_mask(counts[i], BANDS_DEV), total * scale, 0.0)
        if has_prev:
            total = total - prev_ref[:, lanes(i)].astype(F32)
        p_ref[:, lanes(i)] = total


def halo_kernel(scale, p_ref, even_ref, odd_ref, w_even_ref, w_odd_ref, y_ref):
    total = jnp.dot(even_ref[...], w_even_ref[...], preferred_element_type=F32)
    total += jnp.dot(odd_ref[...], w_odd_ref[...], preferred_element_type=F32)
    y_ref[...] = (p_ref[...] + total * scale).astype(BF16)


def pick_kernel(starts, counts, y_ref, out_ref, turned):
    for block in range(ROWS // 128):
        part = y_ref[:, 128 * block : 128 * (block + 1)].astype(F32)
        turned[128 * block : 128 * (block + 1), :] = part.T
    slot = lax.broadcasted_iota(jnp.int32, (CAP_PAD, QUAD * BANDS_DEV), 0)
    for z in range(Z):
        rows = turned[pl.ds(starts[z], CAP_PAD), :]
        out_ref[z] = jnp.where(slot < counts[z], rows, 0.0).astype(BF16)


def rotate_kernel(x_ref, r_ref, out_ref, gathered):
    @pl.when(pl.program_id(0) == 0)
    def _():
        for z in range(Z):
            gathered[:, 128 * z : 128 * (z + 1)] = x_ref[z]

    pieces = []
    for block in range(r_ref.shape[0] // 128):
        for piece in (0, 2, 1, 3):
            first = 128 * block + 32 * piece
            pieces.append(r_ref[first : first + 32, :])
    weights = jnp.concatenate(pieces, axis=0)
    product = lax.dot_general(
        gathered[...], weights, (((1,), (1,)), ((), ())), preferred_element_type=F32
    )
    out_ref[...] = product[:CAP].astype(BF16)


def per_device(start_bands, hamiltonian, neighbours, basis_count, owner_rows, rotation):
    elem_size = lax.axis_size("elem")
    near = [(i, i ^ 1) for i in range(elem_size)]
    far = [(i, (i + 1 if i % 2 else i - 1) % elem_size) for i in range(elem_size)]
    parity = (lax.axis_index("elem") % 2).astype(jnp.int32).reshape(1)
    quad = lax.axis_index("yl") * 2 + lax.axis_index("c")
    row_starts = jnp.cumsum(owner_rows) - owner_rows
    my_starts = lax.dynamic_index_in_dim(row_starts.reshape(Z, QUAD), quad, 1, keepdims=False)
    my_counts = lax.dynamic_index_in_dim(owner_rows.reshape(Z, QUAD), quad, 1, keepdims=False)

    pieces = lax.all_gather(rotation.T, "yl", axis=0, tiled=True)
    rotation_all = lax.all_gather(pieces, ("z", "c"), axis=0, tiled=True)

    block_bf16 = jax.ShapeDtypeStruct((BANDS_DEV, ROWS), BF16)
    block_f32 = jax.ShapeDtypeStruct((BANDS_DEV, ROWS), F32)
    operator = jax.ShapeDtypeStruct((ROWS, ROWS), BF16)
    current = pl.pallas_call(
        mask_kernel, out_shape=block_bf16, in_specs=[SMEM, VMEM], out_specs=VMEM, compiler_params=params(4)
    )(basis_count, start_bands)
    w_even, w_odd = pl.pallas_call(
        couple_kernel,
        out_shape=(operator, operator),
        in_specs=[SMEM, SMEM, SMEM, VMEM],
        out_specs=(VMEM, VMEM),
        compiler_params=params(16),
    )(neighbours, basis_count, parity, hamiltonian)
    earlier = None
    for step in range(DEGREE):
        scale = 0.5 if step == 0 else 1.0
        from_far = lax.ppermute(current, "elem", far)
        from_near = lax.ppermute(current, "elem", near)
        previous = [] if earlier is None else [earlier]
        partial = pl.pallas_call(
            lambda *refs, scale=scale, has_prev=bool(previous): local_kernel(scale, has_prev, *refs),
            out_shape=block_f32,
            in_specs=[SMEM, SMEM, VMEM] + [VMEM] * len(previous) + [VMEM],
            out_specs=VMEM,
            scratch_shapes=[pltpu.VMEM((ELEMS_DEV, BANDS_DEV, NB), BF16)],
            compiler_params=params(8),
            cost_estimate=pl.CostEstimate(flops=3 * 10**8, bytes_accessed=3 << 20, transcendentals=0),
            name="local",
        )(neighbours, basis_count, current, *previous, hamiltonian)
        following = pl.pallas_call(
            lambda *refs, scale=scale: halo_kernel(scale, *refs),
            out_shape=block_bf16,
            in_specs=[VMEM] * 5,
            out_specs=VMEM,
            compiler_params=params(8),
            name="halo",
        )(partial, from_near, from_far, w_even, w_odd)
        earlier, current = current, following

    bands_quad = lax.all_gather(current, ("yl", "c"), axis=0, tiled=True)
    sent = pl.pallas_call(
        pick_kernel,
        out_shape=jax.ShapeDtypeStruct((Z, CAP_PAD, QUAD * BANDS_DEV), BF16),
        in_specs=[SMEM, SMEM, VMEM],
        out_specs=VMEM,
        scratch_shapes=[pltpu.VMEM((ROWS + 48, QUAD * BANDS_DEV), F32)],
        compiler_params=params(8),
        name="pick",
    )(my_starts, my_counts, bands_quad)
    received = lax.all_to_all(sent, "z", split_axis=0, concat_axis=0, tiled=True)
    bands = rotation_all.shape[1]
    tile = 256
    rotated = pl.pallas_call(
        rotate_kernel,
        out_shape=jax.ShapeDtypeStruct((CAP, bands), BF16),
        grid=(bands // tile,),
        in_specs=[
            pl.BlockSpec((Z, CAP_PAD, QUAD * BANDS_DEV), lambda n: (0, 0, 0)),
            pl.BlockSpec((tile, bands), lambda n: (n, 0)),
        ],
        out_specs=pl.BlockSpec((CAP, tile), lambda n: (0, n)),
        scratch_shapes=[pltpu.VMEM((CAP_PAD, bands), BF16)],
        compiler_params=params(16),
        name="rotate",
    )(received, rotation_all)
    return current, rotated


def solution(mesh):
    fine = Mesh(mesh.devices.reshape(mesh.shape["elem"], Z, 2, 2), ("elem",) + BAND_AXES)
    placed = (
        P(BAND_AXES, "elem"),
        P("elem", None, None, None),
        P("elem", None),
        P("elem"),
        P(),
        P(None, BAND_AXES),
    )
    return jax.shard_map(
        per_device,
        mesh=fine,
        in_specs=placed,
        out_specs=(P(BAND_AXES, "elem"), P(("elem",) + BAND_AXES, None)),
        check_vma=False,
    )
```

time: 323 us -> 170 us (0.53)
  the two profiles are of different devices: /device:TPU:8 before, /device:TPU:32 now
where the time goes in v1:
time: 170 us; the launch traced here: 169 us
  starting transfers between devices  54 us (32%)
  blocking collectives  43.6 us (26%)
  waiting for transfers between devices  27.8 us (16%)
  Pallas kernels  20.8 us (12%)
  between operations  14.4 us (8%)
  local copies, waits for them, and re-layouts  8.44 us (5%)
    ppermute x8, starting transfers between devices, per_device(): from_far = lax.ppermute(current, 'elem', far)  36.8 us
    all_to_all x1, blocking collectives, per_device(): lax.all_to_all(sent, 'z', split_axis=0, concat_axis=0, tiled=True)  30.3 us
    ppermute x8, waiting for transfers between devices, per_device(): from_far = lax.ppermute(current, 'elem', far)  27.7 us
    ppermute x8, starting transfers between devices, per_device(): from_near = lax.ppermute(current, 'elem', near)  17.1 us
    pallas_call x8, Pallas kernels, per_device(): pl.pallas_call(lambda *refs, scale=scale, has_prev=bool(previous): local_...  9.29 us
    unnamed x28, local copies, waits for them, and re-layouts  8 us
    all_gather x1, blocking collectives, per_device(): pieces = lax.all_gather(rotation.T, 'yl', axis=0, tiled=True)  7.58 us
    all_gather x1, blocking collectives, per_device(): bands_quad = lax.all_gather(current, ('yl', 'c'), axis=0, tiled=True)  5.79 us
  transfers between devices with their start and end apart: 17, of which 7 were waited for; matrix products, arithmetic and copies ran while one was open for 0% of the time, Pallas kernels for 10%

profile of v1, /device:TPU:32, one launch (start us, length us, event | category | flops | bytes accessed | tf_op | source)
XLA Modules:
  0.0 169.2 jit_solution(10390507538355229706)
XLA Ops:
  7.2 7.6 %all_gather.10 = bf16[64,2048]{1,0:T(8,128)(2,1)} all-gather(bf16[32,2048]{1,0:T(8,128)(2,1)} %bitcast.3), channel_id=1, replica_groups=mesh['elem'=8,'z'=16,'yl'=2,'c'=2] {'yl'}, dimensions={0}, use_global_device_ids=true | all-gather | bytes 393216 | tf_op jit(solution)/shard_map/all_gather | solution.py:123
  14.8 0.6 copy-done.9
  15.5 0.8 copy-done.12
  16.3 0.7 shard_map.77.refs_2_.refs_3_
  17.0 3.4 %collective-permute-start = (bf16[32,768]{1,0:T(8,128)(2,1)S(1)}, bf16[32,768]{1,0:T(8,128)(2,1)S(1)}, u32[]{:S(2)}, u32[]{:S(2)}) collective-permute-start(bf16[32,768]{1,0:T(8,128)(2,1)S(1)} %shard_map.77.refs_2_.refs_3_), channel_id=1, source_target_pairs={{0,64},{64,0},{128,192},{192,128},{256,320},{320,256},{384,448},{4... | collective-permute-start | bytes 147464 | tf_op jit(solution)/shard_map/ppermute | solution.py:143
  20.4 6.3 %collective-permute-start.1 = (bf16[32,768]{1,0:T(8,128)(2,1)S(1)}, bf16[32,768]{1,0:T(8,128)(2,1)S(1)}, u32[]{:S(2)}, u32[]{:S(2)}) collective-permute-start(bf16[32,768]{1,0:T(8,128)(2,1)S(1)} %shard_map.77.refs_2_.refs_3_), channel_id=1, source_target_pairs={{0,448},{64,128},{128,64},{192,256},{256,192},{320,384},{384,320},... | collective-permute-start | bytes 147464 | tf_op jit(solution)/shard_map/ppermute | solution.py:142
  26.7 1.8 %copy-done = bf16[4,7,192,192]{3,2,1,0:T(8,128)(2,1)S(1)} copy-done((bf16[4,7,192,192]{3,2,1,0:T(8,128)(2,1)S(1)}, bf16[4,7,192,192]{3,2,1,0:T(8,128)(2,1)}, u32[]{:S(2)}) %copy-start) | copy-done | bytes 2064408
  28.5 0.7 copy-done.7
  29.2 0.7 copy-done.10
  29.8 0.9 shard_map.78
  30.8 1.2 local.8.refs_0_
  31.9 0.5 halo.8.refs_2_.refs_3_
  32.4 1.9 %collective-permute-start.2 = (bf16[32,768]{1,0:T(8,128)(2,1)S(1)}, bf16[32,768]{1,0:T(8,128)(2,1)S(1)}, u32[]{:S(2)}, u32[]{:S(2)}) collective-permute-start(bf16[32,768]{1,0:T(8,128)(2,1)S(1)} %halo.8.refs_2_.refs_3_), channel_id=1, source_target_pairs={{0,64},{64,0},{128,192},{192,128},{256,320},{320,256},{384,448},{4... | collective-permute-start | bytes 147464 | tf_op jit(solution)/shard_map/ppermute | solution.py:143
  34.4 4.3 %collective-permute-start.3 = (bf16[32,768]{1,0:T(8,128)(2,1)S(1)}, bf16[32,768]{1,0:T(8,128)(2,1)S(1)}, u32[]{:S(2)}, u32[]{:S(2)}) collective-permute-start(bf16[32,768]{1,0:T(8,128)(2,1)S(1)} %halo.8.refs_2_.refs_3_), channel_id=1, source_target_pairs={{0,448},{64,128},{128,64},{192,256},{256,192},{320,384},{384,320},... | collective-permute-start | bytes 147464 | tf_op jit(solution)/shard_map/ppermute | solution.py:142
  38.7 1.2 local.9.refs_0_
  39.9 4.1 %collective-permute-done.3.refs_2_ = bf16[32,768]{1,0:T(8,128)(2,1)S(1)} collective-permute-done((bf16[32,768]{1,0:T(8,128)(2,1)S(1)}, bf16[32,768]{1,0:T(8,128)(2,1)S(1)}, u32[]{:S(2)}, u32[]{:S(2)}) %collective-permute-start.3) | collective-permute-done | bytes 49184 | tf_op jit(solution)/shard_map/ppermute | solution.py:142
  44.5 1.9 %collective-permute-start.4 = (bf16[32,768]{1,0:T(8,128)(2,1)S(1)}, bf16[32,768]{1,0:T(8,128)(2,1)S(1)}, u32[]{:S(2)}, u32[]{:S(2)}) collective-permute-start(bf16[32,768]{1,0:T(8,128)(2,1)S(1)} %halo.9.refs_2_.refs_3_), channel_id=1, source_target_pairs={{0,64},{64,0},{128,192},{192,128},{256,320},{320,256},{384,448},{4... | collective-permute-start | bytes 147464 | tf_op jit(solution)/shard_map/ppermute | solution.py:143
  46.4 4.3 %collective-permute-start.5 = (bf16[32,768]{1,0:T(8,128)(2,1)S(1)}, bf16[32,768]{1,0:T(8,128)(2,1)S(1)}, u32[]{:S(2)}, u32[]{:S(2)}) collective-permute-start(bf16[32,768]{1,0:T(8,128)(2,1)S(1)} %halo.9.refs_2_.refs_3_), channel_id=1, source_target_pairs={{0,448},{64,128},{128,64},{192,256},{256,192},{320,384},{384,320},... | collective-permute-start | bytes 147464 | tf_op jit(solution)/shard_map/ppermute | solution.py:142
  50.8 1.2 local.10.refs_0_
  51.9 4.1 %collective-permute-done.5.refs_2_ = bf16[32,768]{1,0:T(8,128)(2,1)S(1)} collective-permute-done((bf16[32,768]{1,0:T(8,128)(2,1)S(1)}, bf16[32,768]{1,0:T(8,128)(2,1)S(1)}, u32[]{:S(2)}, u32[]{:S(2)}) %collective-permute-start.5) | collective-permute-done | bytes 49184 | tf_op jit(solution)/shard_map/ppermute | solution.py:142
  56.5 1.9 %collective-permute-start.6 = (bf16[32,768]{1,0:T(8,128)(2,1)S(1)}, bf16[32,768]{1,0:T(8,128)(2,1)S(1)}, u32[]{:S(2)}, u32[]{:S(2)}) collective-permute-start(bf16[32,768]{1,0:T(8,128)(2,1)S(1)} %halo.10.refs_2_.refs_3_), channel_id=1, source_target_pairs={{0,64},{64,0},{128,192},{192,128},{256,320},{320,256},{384,448},{4... | collective-permute-start | bytes 147464 | tf_op jit(solution)/shard_map/ppermute | solution.py:143
  58.4 4.3 %collective-permute-start.7 = (bf16[32,768]{1,0:T(8,128)(2,1)S(1)}, bf16[32,768]{1,0:T(8,128)(2,1)S(1)}, u32[]{:S(2)}, u32[]{:S(2)}) collective-permute-start(bf16[32,768]{1,0:T(8,128)(2,1)S(1)} %halo.10.refs_2_.refs_3_), channel_id=1, source_target_pairs={{0,448},{64,128},{128,64},{192,256},{256,192},{320,384},{384,320},... | collective-permute-start | bytes 147464 | tf_op jit(solution)/shard_map/ppermute | solution.py:142
  62.8 1.2 local.11.refs_0_
  64.0 4.1 %collective-permute-done.7.refs_2_ = bf16[32,768]{1,0:T(8,128)(2,1)S(1)} collective-permute-done((bf16[32,768]{1,0:T(8,128)(2,1)S(1)}, bf16[32,768]{1,0:T(8,128)(2,1)S(1)}, u32[]{:S(2)}, u32[]{:S(2)}) %collective-permute-start.7) | collective-permute-done | bytes 49184 | tf_op jit(solution)/shard_map/ppermute | solution.py:142
  68.0 0.5 halo.11.refs_2_.refs_3_
  68.5 1.9 %collective-permute-start.8 = (bf16[32,768]{1,0:T(8,128)(2,1)S(1)}, bf16[32,768]{1,0:T(8,128)(2,1)S(1)}, u32[]{:S(2)}, u32[]{:S(2)}) collective-permute-start(bf16[32,768]{1,0:T(8,128)(2,1)S(1)} %halo.11.refs_2_.refs_3_), channel_id=1, source_target_pairs={{0,64},{64,0},{128,192},{192,128},{256,320},{320,256},{384,448},{4... | collective-permute-start | bytes 147464 | tf_op jit(solution)/shard_map/ppermute | solution.py:143
  70.5 4.3 %collective-permute-start.9 = (bf16[32,768]{1,0:T(8,128)(2,1)S(1)}, bf16[32,768]{1,0:T(8,128)(2,1)S(1)}, u32[]{:S(2)}, u32[]{:S(2)}) collective-permute-start(bf16[32,768]{1,0:T(8,128)(2,1)S(1)} %halo.11.refs_2_.refs_3_), channel_id=1, source_target_pairs={{0,448},{64,128},{128,64},{192,256},{256,192},{320,384},{384,320},... | collective-permute-start | bytes 147464 | tf_op jit(solution)/shard_map/ppermute | solution.py:142
  74.8 1.2 local.12.refs_0_
  76.0 4.1 %collective-permute-done.9.refs_2_ = bf16[32,768]{1,0:T(8,128)(2,1)S(1)} collective-permute-done((bf16[32,768]{1,0:T(8,128)(2,1)S(1)}, bf16[32,768]{1,0:T(8,128)(2,1)S(1)}, u32[]{:S(2)}, u32[]{:S(2)}) %collective-permute-start.9) | collective-permute-done | bytes 49184 | tf_op jit(solution)/shard_map/ppermute | solution.py:142
  80.6 1.9 %collective-permute-start.10 = (bf16[32,768]{1,0:T(8,128)(2,1)S(1)}, bf16[32,768]{1,0:T(8,128)(2,1)S(1)}, u32[]{:S(2)}, u32[]{:S(2)}) collective-permute-start(bf16[32,768]{1,0:T(8,128)(2,1)S(1)} %halo.12.refs_2_.refs_3_), channel_id=1, source_target_pairs={{0,64},{64,0},{128,192},{192,128},{256,320},{320,256},{384,448},{4... | collective-permute-start | bytes 147464 | tf_op jit(solution)/shard_map/ppermute | solution.py:143
  82.5 4.3 %collective-permute-start.11 = (bf16[32,768]{1,0:T(8,128)(2,1)S(1)}, bf16[32,768]{1,0:T(8,128)(2,1)S(1)}, u32[]{:S(2)}, u32[]{:S(2)}) collective-permute-start(bf16[32,768]{1,0:T(8,128)(2,1)S(1)} %halo.12.refs_2_.refs_3_), channel_id=1, source_target_pairs={{0,448},{64,128},{128,64},{192,256},{256,192},{320,384},{384,320},... | collective-permute-start | bytes 147464 | tf_op jit(solution)/shard_map/ppermute | solution.py:142
  86.8 1.2 local.13.refs_0_
  88.0 4.1 %collective-permute-done.11.refs_2_ = bf16[32,768]{1,0:T(8,128)(2,1)S(1)} collective-permute-done((bf16[32,768]{1,0:T(8,128)(2,1)S(1)}, bf16[32,768]{1,0:T(8,128)(2,1)S(1)}, u32[]{:S(2)}, u32[]{:S(2)}) %collective-permute-start.11) | collective-permute-done | bytes 49184 | tf_op jit(solution)/shard_map/ppermute | solution.py:142
  92.6 2.2 %collective-permute-start.12 = (bf16[32,768]{1,0:T(8,128)(2,1)S(1)}, bf16[32,768]{1,0:T(8,128)(2,1)S(1)}, u32[]{:S(2)}, u32[]{:S(2)}) collective-permute-start(bf16[32,768]{1,0:T(8,128)(2,1)S(1)} %halo.13.refs_2_.refs_3_), channel_id=1, source_target_pairs={{0,64},{64,0},{128,192},{192,128},{256,320},{320,256},{384,448},{4... | collective-permute-start | bytes 147464 | tf_op jit(solution)/shard_map/ppermute | solution.py:143
  94.8 4.3 %collective-permute-start.13 = (bf16[32,768]{1,0:T(8,128)(2,1)S(1)}, bf16[32,768]{1,0:T(8,128)(2,1)S(1)}, u32[]{:S(2)}, u32[]{:S(2)}) collective-permute-start(bf16[32,768]{1,0:T(8,128)(2,1)S(1)} %halo.13.refs_2_.refs_3_), channel_id=1, source_target_pairs={{0,448},{64,128},{128,64},{192,256},{256,192},{320,384},{384,320},... | collective-permute-start | bytes 147464 | tf_op jit(solution)/shard_map/ppermute | solution.py:142
  99.2 1.2 local.14.refs_0_
  100.4 4.1 %collective-permute-done.13.refs_2_ = bf16[32,768]{1,0:T(8,128)(2,1)S(1)} collective-permute-done((bf16[32,768]{1,0:T(8,128)(2,1)S(1)}, bf16[32,768]{1,0:T(8,128)(2,1)S(1)}, u32[]{:S(2)}, u32[]{:S(2)}) %collective-permute-start.13) | collective-permute-done | bytes 49184 | tf_op jit(solution)/shard_map/ppermute | solution.py:142
  104.4 0.5 halo.14.refs_2_
  104.9 1.9 %collective-permute-start.14 = (bf16[32,768]{1,0:T(8,128)(2,1)S(1)}, bf16[32,768]{1,0:T(8,128)(2,1)S(1)}, u32[]{:S(2)}, u32[]{:S(2)}) collective-permute-start(bf16[32,768]{1,0:T(8,128)(2,1)S(1)} %halo.14.refs_2_), channel_id=1, source_target_pairs={{0,64},{64,0},{128,192},{192,128},{256,320},{320,256},{384,448},{4... | collective-permute-start | bytes 147464 | tf_op jit(solution)/shard_map/ppermute | solution.py:143
  106.9 4.3 %collective-permute-start.15 = (bf16[32,768]{1,0:T(8,128)(2,1)S(1)}, bf16[32,768]{1,0:T(8,128)(2,1)S(1)}, u32[]{:S(2)}, u32[]{:S(2)}) collective-permute-start(bf16[32,768]{1,0:T(8,128)(2,1)S(1)} %halo.14.refs_2_), channel_id=1, source_target_pairs={{0,448},{64,128},{128,64},{192,256},{256,192},{320,384},{384,320},... | collective-permute-start | bytes 147464 | tf_op jit(solution)/shard_map/ppermute | solution.py:142
  112.0 1.2 local.15.refs_0_
  113.1 3.3 %collective-permute-done.15.refs_2_ = bf16[32,768]{1,0:T(8,128)(2,1)S(1)} collective-permute-done((bf16[32,768]{1,0:T(8,128)(2,1)S(1)}, bf16[32,768]{1,0:T(8,128)(2,1)S(1)}, u32[]{:S(2)}, u32[]{:S(2)}) %collective-permute-start.15) | collective-permute-done | bytes 49184 | tf_op jit(solution)/shard_map/ppermute | solution.py:142
  116.5 1.1 halo.15
  117.6 5.8 %all_gather.9.y_ref = bf16[128,768]{1,0:T(8,128)(2,1)S(1)} all-gather(bf16[32,768]{1,0:T(8,128)(2,1)} %halo.15), channel_id=1, replica_groups=mesh['elem'=8,'z'=16,'yl'=2,'c'=2] {'yl','c'}, dimensions={0}, use_global_device_ids=true | all-gather | bytes 245760 | tf_op jit(solution)/shard_map/all_gather | solution.py:165
  123.4 0.7 pick.1
  124.1 30.3 %all_to_all.5.x_ref = bf16[16,40,128]{2,1,0:T(8,128)(2,1)S(1)} all-to-all(bf16[16,40,128]{2,1,0:T(8,128)(2,1)S(1)} %pick.1), channel_id=1, replica_groups=mesh['elem'=8,'z'=16,'yl'=2,'c'=2] {'z'}, dimensions={0} | all-to-all | bytes 327680 | tf_op jit(solution)/shard_map/all_to_all | solution.py:175
  154.4 3.4 %copy-done.6 = bf16[2048,2048]{1,0:T(8,128)(2,1)S(1)} copy-done((bf16[2048,2048]{1,0:T(8,128)(2,1)S(1)}, bf16[2048,2048]{1,0:T(8,128)(2,1)}, u32[]{:S(2)}) %copy-start.6) | copy-done | bytes 8388632
  157.8 4.6 %rotate.1 = bf16[36,2048]{1,0:T(8,128)(2,1)} custom-call(bf16[16,40,128]{2,1,0:T(8,128)(2,1)S(1)} %all_to_all.5.x_ref, bf16[2048,2048]{1,0:T(8,128)(2,1)S(1)} %copy-done.6), custom_call_target="tpu_custom_call" | custom-call | tf_op jit(solution)/shard_map/rotate/pallas_call | solution.py:178
  (45 shorter events, 2.8 us)
Async XLA Ops:
  7.2 147.2 %all-gather.2.cloned.1.call-start = ((), (), s32[]{:S(2)}) async-start(), calls=%async_computation.1 | async-start | bytes 8650752 | tf_op jit(solution)/shard_map/all_gather | solution.py:124
  14.8 0.7 copy-start.9
  15.5 0.8 copy-start.12
  17.0 15.0 %collective-permute-start = (bf16[32,768]{1,0:T(8,128)(2,1)S(1)}, bf16[32,768]{1,0:T(8,128)(2,1)S(1)}, u32[]{:S(2)}, u32[]{:S(2)}) collective-permute-start(bf16[32,768]{1,0:T(8,128)(2,1)S(1)} %shard_map.77.refs_2_.refs_3_), channel_id=1, source_target_pairs={{0,64},{64,0},{128,192},{192,128},{256,320},{320,256},{384,448},{4... | collective-permute-start | bytes 147464 | tf_op jit(solution)/shard_map/ppermute | solution.py:143
  20.4 11.6 %collective-permute-start.1 = (bf16[32,768]{1,0:T(8,128)(2,1)S(1)}, bf16[32,768]{1,0:T(8,128)(2,1)S(1)}, u32[]{:S(2)}, u32[]{:S(2)}) collective-permute-start(bf16[32,768]{1,0:T(8,128)(2,1)S(1)} %shard_map.77.refs_2_.refs_3_), channel_id=1, source_target_pairs={{0,448},{64,128},{128,64},{192,256},{256,192},{320,384},{384,320},... | collective-permute-start | bytes 147464 | tf_op jit(solution)/shard_map/ppermute | solution.py:142
  26.7 1.8 %copy-start = (bf16[4,7,192,192]{3,2,1,0:T(8,128)(2,1)S(1)}, bf16[4,7,192,192]{3,2,1,0:T(8,128)(2,1)}, u32[]{:S(2)}) copy-start(bf16[4,7,192,192]{3,2,1,0:T(8,128)(2,1)} %refs_4_.13) | copy-start | bytes 6193156
  28.5 0.7 copy-start.7
  29.2 0.7 copy-start.10
  30.7 73.7 %copy-start.2 = (bf16[768,768]{1,0:T(8,128)(2,1)}, bf16[768,768]{1,0:T(8,128)(2,1)S(1)}, u32[]{:S(2)}) copy-start(bf16[768,768]{1,0:T(8,128)(2,1)S(1)} %get-tuple-element.4.refs_3_) | copy-start | bytes 3538948
  30.8 73.7 %copy-start.4 = (bf16[768,768]{1,0:T(8,128)(2,1)}, bf16[768,768]{1,0:T(8,128)(2,1)S(1)}, u32[]{:S(2)}) copy-start(bf16[768,768]{1,0:T(8,128)(2,1)S(1)} %get-tuple-element.5.refs_4_) | copy-start | bytes 3538948
  32.4 7.5 %collective-permute-start.2 = (bf16[32,768]{1,0:T(8,128)(2,1)S(1)}, bf16[32,768]{1,0:T(8,128)(2,1)S(1)}, u32[]{:S(2)}, u32[]{:S(2)}) collective-permute-start(bf16[32,768]{1,0:T(8,128)(2,1)S(1)} %halo.8.refs_2_.refs_3_), channel_id=1, source_target_pairs={{0,64},{64,0},{128,192},{192,128},{256,320},{320,256},{384,448},{4... | collective-permute-start | bytes 147464 | tf_op jit(solution)/shard_map/ppermute | solution.py:143
  34.4 9.6 %collective-permute-start.3 = (bf16[32,768]{1,0:T(8,128)(2,1)S(1)}, bf16[32,768]{1,0:T(8,128)(2,1)S(1)}, u32[]{:S(2)}, u32[]{:S(2)}) collective-permute-start(bf16[32,768]{1,0:T(8,128)(2,1)S(1)} %halo.8.refs_2_.refs_3_), channel_id=1, source_target_pairs={{0,448},{64,128},{128,64},{192,256},{256,192},{320,384},{384,320},... | collective-permute-start | bytes 147464 | tf_op jit(solution)/shard_map/ppermute | solution.py:142
  44.5 7.5 %collective-permute-start.4 = (bf16[32,768]{1,0:T(8,128)(2,1)S(1)}, bf16[32,768]{1,0:T(8,128)(2,1)S(1)}, u32[]{:S(2)}, u32[]{:S(2)}) collective-permute-start(bf16[32,768]{1,0:T(8,128)(2,1)S(1)} %halo.9.refs_2_.refs_3_), channel_id=1, source_target_pairs={{0,64},{64,0},{128,192},{192,128},{256,320},{320,256},{384,448},{4... | collective-permute-start | bytes 147464 | tf_op jit(solution)/shard_map/ppermute | solution.py:143
  46.4 9.6 %collective-permute-start.5 = (bf16[32,768]{1,0:T(8,128)(2,1)S(1)}, bf16[32,768]{1,0:T(8,128)(2,1)S(1)}, u32[]{:S(2)}, u32[]{:S(2)}) collective-permute-start(bf16[32,768]{1,0:T(8,128)(2,1)S(1)} %halo.9.refs_2_.refs_3_), channel_id=1, source_target_pairs={{0,448},{64,128},{128,64},{192,256},{256,192},{320,384},{384,320},... | collective-permute-start | bytes 147464 | tf_op jit(solution)/shard_map/ppermute | solution.py:142
  56.5 7.5 %collective-permute-start.6 = (bf16[32,768]{1,0:T(8,128)(2,1)S(1)}, bf16[32,768]{1,0:T(8,128)(2,1)S(1)}, u32[]{:S(2)}, u32[]{:S(2)}) collective-permute-start(bf16[32,768]{1,0:T(8,128)(2,1)S(1)} %halo.10.refs_2_.refs_3_), channel_id=1, source_target_pairs={{0,64},{64,0},{128,192},{192,128},{256,320},{320,256},{384,448},{4... | collective-permute-start | bytes 147464 | tf_op jit(solution)/shard_map/ppermute | solution.py:143
  58.4 9.6 %collective-permute-start.7 = (bf16[32,768]{1,0:T(8,128)(2,1)S(1)}, bf16[32,768]{1,0:T(8,128)(2,1)S(1)}, u32[]{:S(2)}, u32[]{:S(2)}) collective-permute-start(bf16[32,768]{1,0:T(8,128)(2,1)S(1)} %halo.10.refs_2_.refs_3_), channel_id=1, source_target_pairs={{0,448},{64,128},{128,64},{192,256},{256,192},{320,384},{384,320},... | collective-permute-start | bytes 147464 | tf_op jit(solution)/shard_map/ppermute | solution.py:142
  68.5 7.5 %collective-permute-start.8 = (bf16[32,768]{1,0:T(8,128)(2,1)S(1)}, bf16[32,768]{1,0:T(8,128)(2,1)S(1)}, u32[]{:S(2)}, u32[]{:S(2)}) collective-permute-start(bf16[32,768]{1,0:T(8,128)(2,1)S(1)} %halo.11.refs_2_.refs_3_), channel_id=1, source_target_pairs={{0,64},{64,0},{128,192},{192,128},{256,320},{320,256},{384,448},{4... | collective-permute-start | bytes 147464 | tf_op jit(solution)/shard_map/ppermute | solution.py:143
  70.5 9.6 %collective-permute-start.9 = (bf16[32,768]{1,0:T(8,128)(2,1)S(1)}, bf16[32,768]{1,0:T(8,128)(2,1)S(1)}, u32[]{:S(2)}, u32[]{:S(2)}) collective-permute-start(bf16[32,768]{1,0:T(8,128)(2,1)S(1)} %halo.11.refs_2_.refs_3_), channel_id=1, source_target_pairs={{0,448},{64,128},{128,64},{192,256},{256,192},{320,384},{384,320},... | collective-permute-start | bytes 147464 | tf_op jit(solution)/shard_map/ppermute | solution.py:142
  80.6 7.5 %collective-permute-start.10 = (bf16[32,768]{1,0:T(8,128)(2,1)S(1)}, bf16[32,768]{1,0:T(8,128)(2,1)S(1)}, u32[]{:S(2)}, u32[]{:S(2)}) collective-permute-start(bf16[32,768]{1,0:T(8,128)(2,1)S(1)} %halo.12.refs_2_.refs_3_), channel_id=1, source_target_pairs={{0,64},{64,0},{128,192},{192,128},{256,320},{320,256},{384,448},{4... | collective-permute-start | bytes 147464 | tf_op jit(solution)/shard_map/ppermute | solution.py:143
  82.5 9.6 %collective-permute-start.11 = (bf16[32,768]{1,0:T(8,128)(2,1)S(1)}, bf16[32,768]{1,0:T(8,128)(2,1)S(1)}, u32[]{:S(2)}, u32[]{:S(2)}) collective-permute-start(bf16[32,768]{1,0:T(8,128)(2,1)S(1)} %halo.12.refs_2_.refs_3_), channel_id=1, source_target_pairs={{0,448},{64,128},{128,64},{192,256},{256,192},{320,384},{384,320},... | collective-permute-start | bytes 147464 | tf_op jit(solution)/shard_map/ppermute | solution.py:142
  92.6 18.6 %copy-start.13 = (s32[64]{0:T(128)S(1)}, s32[64]{0:T(128)}, u32[]{:S(2)}) copy-start(s32[64]{0:T(128)} %param.10) | copy-start | bytes 772
  92.6 19.3 %copy-start.1 = (bf16[4,7,192,192]{3,2,1,0:T(8,128)(2,1)S(1)}, bf16[4,7,192,192]{3,2,1,0:T(8,128)(2,1)}, u32[]{:S(2)}) copy-start(bf16[4,7,192,192]{3,2,1,0:T(8,128)(2,1)} %refs_4_.13) | copy-start | bytes 6193156
  92.6 19.3 %copy-start.8 = (s32[4,6]{1,0:T(4,128)S(1)}, s32[4,6]{1,0:T(4,128)}, u32[]{:S(2)}) copy-start(s32[4,6]{1,0:T(4,128)} %refs_0_.15) | copy-start | bytes 292
  92.6 19.3 %copy-start.11 = (s32[4]{0:T(128)S(1)}, s32[4]{0:T(128)}, u32[]{:S(2)}) copy-start(s32[4]{0:T(128)} %refs_1_.15) | copy-start | bytes 52
  92.6 7.7 %collective-permute-start.12 = (bf16[32,768]{1,0:T(8,128)(2,1)S(1)}, bf16[32,768]{1,0:T(8,128)(2,1)S(1)}, u32[]{:S(2)}, u32[]{:S(2)}) collective-permute-start(bf16[32,768]{1,0:T(8,128)(2,1)S(1)} %halo.13.refs_2_.refs_3_), channel_id=1, source_target_pairs={{0,64},{64,0},{128,192},{192,128},{256,320},{320,256},{384,448},{4... | collective-permute-start | bytes 147464 | tf_op jit(solution)/shard_map/ppermute | solution.py:143
  94.8 9.6 %collective-permute-start.13 = (bf16[32,768]{1,0:T(8,128)(2,1)S(1)}, bf16[32,768]{1,0:T(8,128)(2,1)S(1)}, u32[]{:S(2)}, u32[]{:S(2)}) collective-permute-start(bf16[32,768]{1,0:T(8,128)(2,1)S(1)} %halo.13.refs_2_.refs_3_), channel_id=1, source_target_pairs={{0,448},{64,128},{128,64},{192,256},{256,192},{320,384},{384,320},... | collective-permute-start | bytes 147464 | tf_op jit(solution)/shard_map/ppermute | solution.py:142
  104.9 8.2 %collective-permute-start.14 = (bf16[32,768]{1,0:T(8,128)(2,1)S(1)}, bf16[32,768]{1,0:T(8,128)(2,1)S(1)}, u32[]{:S(2)}, u32[]{:S(2)}) collective-permute-start(bf16[32,768]{1,0:T(8,128)(2,1)S(1)} %halo.14.refs_2_), channel_id=1, source_target_pairs={{0,64},{64,0},{128,192},{192,128},{256,320},{320,256},{384,448},{4... | collective-permute-start | bytes 147464 | tf_op jit(solution)/shard_map/ppermute | solution.py:143
  106.9 9.6 %collective-permute-start.15 = (bf16[32,768]{1,0:T(8,128)(2,1)S(1)}, bf16[32,768]{1,0:T(8,128)(2,1)S(1)}, u32[]{:S(2)}, u32[]{:S(2)}) collective-permute-start(bf16[32,768]{1,0:T(8,128)(2,1)S(1)} %halo.14.refs_2_), channel_id=1, source_target_pairs={{0,448},{64,128},{128,64},{192,256},{256,192},{320,384},{384,320},... | collective-permute-start | bytes 147464 | tf_op jit(solution)/shard_map/ppermute | solution.py:142
  111.7 4.7 %copy-start.3 = (bf16[768,768]{1,0:T(8,128)(2,1)S(1)}, bf16[768,768]{1,0:T(8,128)(2,1)}, u32[]{:S(2)}) copy-start(bf16[768,768]{1,0:T(8,128)(2,1)} %copy-done.2) | copy-start | bytes 3538948
  111.7 4.7 %copy-start.5 = (bf16[768,768]{1,0:T(8,128)(2,1)S(1)}, bf16[768,768]{1,0:T(8,128)(2,1)}, u32[]{:S(2)}) copy-start(bf16[768,768]{1,0:T(8,128)(2,1)} %copy-done.4) | copy-start | bytes 3538948
  154.4 3.4 %copy-start.6 = (bf16[2048,2048]{1,0:T(8,128)(2,1)S(1)}, bf16[2048,2048]{1,0:T(8,128)(2,1)}, u32[]{:S(2)}) copy-start(bf16[2048,2048]{1,0:T(8,128)(2,1)} %all-gather.2.cloned.1.call-done.r_ref) | copy-start | bytes 25165828
Sparse Core Ops, SparseCore 0:
  14.9 82.5 all-gather.1

commit v2 on v1

--- a/solution.py
+++ b/solution.py
@@ -5,6 +5,7 @@
 from jax.experimental.pallas import tpu as pltpu
 from jax.sharding import Mesh
 from jax.sharding import PartitionSpec as P
+
 
 DEGREE = 8
 NB = 192
@@ -17,6 +18,7 @@
 QUAD = 4
 BF16 = jnp.bfloat16
 F32 = jnp.float32
+TILE = 256
 BAND_AXES = ("z", "yl", "c")
 
 VMEM = pl.BlockSpec(memory_space=pltpu.VMEM)
@@ -33,14 +35,6 @@
 
 def column_mask(count, rows):
     return lax.broadcasted_iota(jnp.int32, (rows, NB), 1) < count
-
-
-def mask_kernel(counts, start_ref, y_ref):
-    for i in range(ELEMS_DEV):
-        block = start_ref[:, lanes(i)]
-        y_ref[:, lanes(i)] = jnp.where(
-            column_mask(counts[i], BANDS_DEV), block, jnp.zeros_like(block)
-        )
 
 
 def couple_kernel(neighbours, counts, parity, h_ref, even_ref, odd_ref):
@@ -92,22 +86,33 @@
         out_ref[z] = jnp.where(slot < counts[z], rows, 0.0).astype(BF16)
 
 
-def rotate_kernel(x_ref, r_ref, out_ref, gathered):
-    @pl.when(pl.program_id(0) == 0)
-    def _():
-        for z in range(Z):
-            gathered[:, 128 * z : 128 * (z + 1)] = x_ref[z]
-
-    pieces = []
-    for block in range(r_ref.shape[0] // 128):
-        for piece in (0, 2, 1, 3):
-            first = 128 * block + 32 * piece
-            pieces.append(r_ref[first : first + 32, :])
-    weights = jnp.concatenate(pieces, axis=0)
-    product = lax.dot_general(
-        gathered[...], weights, (((1,), (1,)), ((), ())), preferred_element_type=F32
-    )
-    out_ref[...] = product[:CAP].astype(BF16)
+def rotate_kernel(low, x_ref, r_hbm, out_ref, gathered, weights, sems):
+    chunks = r_hbm.shape[0] // TILE
+    copies = [
+        pltpu.make_async_copy(
+            r_hbm.at[pl.ds(TILE * n, TILE)], weights.at[pl.ds(TILE * n, TILE)], sems.at[n]
+        )
+        for n in range(chunks)
+    ]
+    for copy in copies:
+        copy.start()
+    for z in range(Z):
+        gathered[:, 128 * z : 128 * (z + 1)] = x_ref[z]
+    mine = low[0]
+    for n in range(chunks):
+        copies[n].wait()
+        pieces = []
+        for block in range(TILE // 128):
+            for y, core in ((0, 0), (0, 1), (1, 0), (1, 1)):
+                first = n * TILE + 128 * block + 64 * core + 32 * (y ^ mine)
+                pieces.append(weights[pl.ds(pl.multiple_of(first, 32), 32), :])
+        product = lax.dot_general(
+            gathered[...],
+            jnp.concatenate(pieces, axis=0),
+            (((1,), (1,)), ((), ())),
+            preferred_element_type=F32,
+        )
+        out_ref[:, TILE * n : TILE * (n + 1)] = product[:CAP].astype(BF16)
 
 
 def per_device(start_bands, hamiltonian, neighbours, basis_count, owner_rows, rotation):
@@ -115,20 +120,23 @@
     near = [(i, i ^ 1) for i in range(elem_size)]
     far = [(i, (i + 1 if i % 2 else i - 1) % elem_size) for i in range(elem_size)]
     parity = (lax.axis_index("elem") % 2).astype(jnp.int32).reshape(1)
+    low = lax.axis_index("yl").astype(jnp.int32).reshape(1)
     quad = lax.axis_index("yl") * 2 + lax.axis_index("c")
     row_starts = jnp.cumsum(owner_rows) - owner_rows
     my_starts = lax.dynamic_index_in_dim(row_starts.reshape(Z, QUAD), quad, 1, keepdims=False)
     my_counts = lax.dynamic_index_in_dim(owner_rows.reshape(Z, QUAD), quad, 1, keepdims=False)
 
-    pieces = lax.all_gather(rotation.T, "yl", axis=0, tiled=True)
-    rotation_all = lax.all_gather(pieces, ("z", "c"), axis=0, tiled=True)
+    columns = rotation.T
+    other_columns = lax.ppermute(columns, "yl", [(0, 1), (1, 0)])
 
     block_bf16 = jax.ShapeDtypeStruct((BANDS_DEV, ROWS), BF16)
     block_f32 = jax.ShapeDtypeStruct((BANDS_DEV, ROWS), F32)
     operator = jax.ShapeDtypeStruct((ROWS, ROWS), BF16)
-    current = pl.pallas_call(
-        mask_kernel, out_shape=block_bf16, in_specs=[SMEM, VMEM], out_specs=VMEM, compiler_params=params(4)
-    )(basis_count, start_bands)
+    column = lax.broadcasted_iota(jnp.int32, (BANDS_DEV, ROWS), 1)
+    keep = jnp.zeros((BANDS_DEV, ROWS), jnp.bool_)
+    for i in range(ELEMS_DEV):
+        keep = keep | ((column >= NB * i) & (column < NB * i + basis_count[i]))
+    current = jnp.where(keep, start_bands, jnp.zeros_like(start_bands))
     w_even, w_odd = pl.pallas_call(
         couple_kernel,
         out_shape=(operator, operator),
@@ -139,8 +147,8 @@
     earlier = None
     for step in range(DEGREE):
         scale = 0.5 if step == 0 else 1.0
+        from_near = lax.ppermute(current, "elem", near)
         from_far = lax.ppermute(current, "elem", far)
-        from_near = lax.ppermute(current, "elem", near)
         previous = [] if earlier is None else [earlier]
         partial = pl.pallas_call(
             lambda *refs, scale=scale, has_prev=bool(previous): local_kernel(scale, has_prev, *refs),
@@ -152,6 +160,10 @@
             cost_estimate=pl.CostEstimate(flops=3 * 10**8, bytes_accessed=3 << 20, transcendentals=0),
             name="local",
         )(neighbours, basis_count, current, *previous, hamiltonian)
+        if step == 0:
+            other_columns, partial = lax.optimization_barrier((other_columns, partial))
+            pieces = jnp.concatenate([columns, other_columns], axis=0)
+            rotation_all = lax.all_gather(pieces, ("z", "c"), axis=0, tiled=True)
         following = pl.pallas_call(
             lambda *refs, scale=scale: halo_kernel(scale, *refs),
             out_shape=block_bf16,
@@ -172,22 +184,21 @@
         compiler_params=params(8),
         name="pick",
     )(my_starts, my_counts, bands_quad)
+    sent, rotation_all = lax.optimization_barrier((sent, rotation_all))
     received = lax.all_to_all(sent, "z", split_axis=0, concat_axis=0, tiled=True)
-    bands = rotation_all.shape[1]
-    tile = 256
     rotated = pl.pallas_call(
         rotate_kernel,
-        out_shape=jax.ShapeDtypeStruct((CAP, bands), BF16),
-        grid=(bands // tile,),
-        in_specs=[
-            pl.BlockSpec((Z, CAP_PAD, QUAD * BANDS_DEV), lambda n: (0, 0, 0)),
-            pl.BlockSpec((tile, bands), lambda n: (n, 0)),
+        out_shape=jax.ShapeDtypeStruct((CAP, rotation_all.shape[1]), BF16),
+        in_specs=[SMEM, VMEM, pl.BlockSpec(memory_space=pltpu.HBM)],
+        out_specs=VMEM,
+        scratch_shapes=[
+            pltpu.VMEM((CAP_PAD, rotation_all.shape[1]), BF16),
+            pltpu.VMEM(rotation_all.shape, BF16),
+            pltpu.SemaphoreType.DMA((rotation_all.shape[0] // TILE,)),
         ],
-        out_specs=pl.BlockSpec((CAP, tile), lambda n: (0, n)),
-        scratch_shapes=[pltpu.VMEM((CAP_PAD, bands), BF16)],
-        compiler_params=params(16),
+        compiler_params=params(58),
         name="rotate",
-    )(received, rotation_all)
+    )(low, received, rotation_all)
     return current, rotated
 
 

time: 170 us -> 173 us (1.018)
  starting transfers between devices: 54 us -> 63.1 us
  blocking collectives: 43.6 us -> 36.2 us
  local copies, waits for them, and re-layouts: 8.44 us -> 5.07 us
  Pallas kernels: 20.8 us -> 23.7 us
  waiting for transfers between devices: 27.8 us -> 25.1 us
  other arithmetic: 0.22 us -> 2.41 us
  between operations: 14.4 us -> 16.4 us
    all_gather x1 -> x0, blocking collectives: 7.58 us -> none  [per_device(): pieces = lax.all_gather(rotation.T, 'yl', axis=0, tiled=True)]
    ppermute x8, starting transfers between devices: 36.8 us -> 42.5 us  [per_device(): from_far = lax.ppermute(current, 'elem', far)]
    ppermute x8, waiting for transfers between devices: 27.7 us -> 22.3 us  [per_device(): from_far = lax.ppermute(current, 'elem', far)]
    unnamed x28 -> x24, local copies, waits for them, and re-layouts: 8 us -> 3.16 us
    ppermute x0 -> x1, starting transfers between devices: none -> 3.49 us  [per_device(): other_columns = lax.ppermute(columns, 'yl', [(0, 1), (1, 0)])]
    pallas_call x2 -> x1, Pallas kernels: 5.3 us -> 8.23 us  [per_device(): pl.pallas_call(rotate_kernel, out_shape=jax.ShapeDtypeStruct((CAP, rotati...]
    ppermute x8, waiting for transfers between devices: 0.02 us -> 2.75 us  [per_device(): from_near = lax.ppermute(current, 'elem', near)]
  transfers between devices with their start and end apart: 17 -> 18, of which waited for: 7 -> 9; matrix products, arithmetic and copies ran while one was open for 0% -> 2% of each run, Pallas kernels for 10% -> 9%
where the time goes in v2:
time: 173 us; the launch traced here: 172 us
  starting transfers between devices  63.1 us (36%)
  blocking collectives  36.2 us (21%)
  waiting for transfers between devices  25.1 us (15%)
  Pallas kernels  23.7 us (14%)
  between operations  16.4 us (9%)
  local copies, waits for them, and re-layouts  5.07 us (3%)
  other arithmetic  2.41 us (1%)
    ppermute x8, starting transfers between devices, per_device(): from_far = lax.ppermute(current, 'elem', far)  42.5 us
    all_to_all x1, blocking collectives, per_device(): lax.all_to_all(sent, 'z', split_axis=0, concat_axis=0, tiled=True)  30.4 us
    ppermute x8, waiting for transfers between devices, per_device(): from_far = lax.ppermute(current, 'elem', far)  22.3 us
    ppermute x8, starting transfers between devices, per_device(): from_near = lax.ppermute(current, 'elem', near)  17 us
    pallas_call x8, Pallas kernels, per_device(): pl.pallas_call(lambda *refs, scale=scale, has_prev=bool(previous): local_...  9.32 us
    pallas_call x1, Pallas kernels, per_device(): pl.pallas_call(rotate_kernel, out_shape=jax.ShapeDtypeStruct((CAP, rotati...  8.23 us
    all_gather x1, blocking collectives, per_device(): bands_quad = lax.all_gather(current, ('yl', 'c'), axis=0, tiled=True)  5.79 us
    pallas_call x8, Pallas kernels, per_device(): pl.pallas_call(lambda *refs, scale=scale: halo_kernel(scale, *refs), out_...  4.59 us
  transfers between devices with their start and end apart: 18, of which 9 were waited for; matrix products, arithmetic and copies ran while one was open for 2% of the time, Pallas kernels for 9%

profile of v2, /device:TPU:32, one launch (start us, length us, event | category | flops | bytes accessed | tf_op | source)
XLA Modules:
  0.0 172.0 jit_solution(13228354988169229700)
XLA Ops:
  7.2 3.5 %collective-permute-start = (bf16[32,2048]{1,0:T(8,128)(2,1)}, bf16[32,2048]{1,0:T(8,128)(2,1)S(1)}, u32[]{:S(2)}, u32[]{:S(2)}) collective-permute-start(bf16[32,2048]{1,0:T(8,128)(2,1)} %bitcast.8), channel_id=1, source_target_pairs={{0,2},{2,0},{1,3},{3,1},{4,6},{6,4},{5,7},{7,5},{8,10},{10,8},{9,1... | collective-permute-start | bytes 393224 | tf_op jit(solution)/shard_map/ppermute | solution.py:130
  10.7 1.5 fusion.6
  14.2 0.7 fusion.2
  14.8 0.8 broadcast_select_fusion.refs_2_.refs_3_
  15.7 1.8 %copy-done = bf16[4,7,192,192]{3,2,1,0:T(8,128)(2,1)S(1)} copy-done((bf16[4,7,192,192]{3,2,1,0:T(8,128)(2,1)S(1)}, bf16[4,7,192,192]{3,2,1,0:T(8,128)(2,1)}, u32[]{:S(2)}) %copy-start) | copy-done | bytes 2064408
  17.4 0.7 copy-done.6
  18.1 0.7 copy-done.8
  18.8 1.2 local.8.refs_0_
  20.0 0.7 pad_maximum_fusion
  20.7 3.4 %collective-permute-start.1 = (bf16[32,768]{1,0:T(8,128)(2,1)S(1)}, bf16[32,768]{1,0:T(8,128)(2,1)S(1)}, u32[]{:S(2)}, u32[]{:S(2)}) collective-permute-start(bf16[32,768]{1,0:T(8,128)(2,1)S(1)} %broadcast_select_fusion.refs_2_.refs_3_), channel_id=1, source_target_pairs={{0,64},{64,0},{128,192},{192,128},{256,320},{320,256},{384,448},{4... | collective-permute-start | bytes 147464 | tf_op jit(solution)/shard_map/ppermute | solution.py:150
  24.1 6.3 %collective-permute-start.2 = (bf16[32,768]{1,0:T(8,128)(2,1)S(1)}, bf16[32,768]{1,0:T(8,128)(2,1)S(1)}, u32[]{:S(2)}, u32[]{:S(2)}) collective-permute-start(bf16[32,768]{1,0:T(8,128)(2,1)S(1)} %broadcast_select_fusion.refs_2_.refs_3_), channel_id=1, source_target_pairs={{0,448},{64,128},{128,64},{192,256},{256,192},{320,384},{384,320},... | collective-permute-start | bytes 147464 | tf_op jit(solution)/shard_map/ppermute | solution.py:151
  30.5 0.9 shard_map.77
  31.4 2.3 %collective-permute-done.2.refs_2_ = bf16[32,768]{1,0:T(8,128)(2,1)S(1)} collective-permute-done((bf16[32,768]{1,0:T(8,128)(2,1)S(1)}, bf16[32,768]{1,0:T(8,128)(2,1)S(1)}, u32[]{:S(2)}, u32[]{:S(2)}) %collective-permute-start.2) | collective-permute-done | bytes 49184 | tf_op jit(solution)/shard_map/ppermute | solution.py:151
  33.7 0.5 halo.8.refs_2_.refs_3_
  34.2 1.9 %collective-permute-start.3 = (bf16[32,768]{1,0:T(8,128)(2,1)S(1)}, bf16[32,768]{1,0:T(8,128)(2,1)S(1)}, u32[]{:S(2)}, u32[]{:S(2)}) collective-permute-start(bf16[32,768]{1,0:T(8,128)(2,1)S(1)} %halo.8.refs_2_.refs_3_), channel_id=1, source_target_pairs={{0,64},{64,0},{128,192},{192,128},{256,320},{320,256},{384,448},{4... | collective-permute-start | bytes 147464 | tf_op jit(solution)/shard_map/ppermute | solution.py:150
  36.1 6.3 %collective-permute-start.4 = (bf16[32,768]{1,0:T(8,128)(2,1)S(1)}, bf16[32,768]{1,0:T(8,128)(2,1)S(1)}, u32[]{:S(2)}, u32[]{:S(2)}) collective-permute-start(bf16[32,768]{1,0:T(8,128)(2,1)S(1)} %halo.8.refs_2_.refs_3_), channel_id=1, source_target_pairs={{0,448},{64,128},{128,64},{192,256},{256,192},{320,384},{384,320},... | collective-permute-start | bytes 147464 | tf_op jit(solution)/shard_map/ppermute | solution.py:151
  42.5 1.2 local.9.refs_0_
  43.7 2.1 %collective-permute-done.4.refs_2_ = bf16[32,768]{1,0:T(8,128)(2,1)S(1)} collective-permute-done((bf16[32,768]{1,0:T(8,128)(2,1)S(1)}, bf16[32,768]{1,0:T(8,128)(2,1)S(1)}, u32[]{:S(2)}, u32[]{:S(2)}) %collective-permute-start.4) | collective-permute-done | bytes 49184 | tf_op jit(solution)/shard_map/ppermute | solution.py:151
  46.2 1.9 %collective-permute-start.5 = (bf16[32,768]{1,0:T(8,128)(2,1)S(1)}, bf16[32,768]{1,0:T(8,128)(2,1)S(1)}, u32[]{:S(2)}, u32[]{:S(2)}) collective-permute-start(bf16[32,768]{1,0:T(8,128)(2,1)S(1)} %halo.9.refs_2_.refs_3_), channel_id=1, source_target_pairs={{0,64},{64,0},{128,192},{192,128},{256,320},{320,256},{384,448},{4... | collective-permute-start | bytes 147464 | tf_op jit(solution)/shard_map/ppermute | solution.py:150
  48.2 6.3 %collective-permute-start.6 = (bf16[32,768]{1,0:T(8,128)(2,1)S(1)}, bf16[32,768]{1,0:T(8,128)(2,1)S(1)}, u32[]{:S(2)}, u32[]{:S(2)}) collective-permute-start(bf16[32,768]{1,0:T(8,128)(2,1)S(1)} %halo.9.refs_2_.refs_3_), channel_id=1, source_target_pairs={{0,448},{64,128},{128,64},{192,256},{256,192},{320,384},{384,320},... | collective-permute-start | bytes 147464 | tf_op jit(solution)/shard_map/ppermute | solution.py:151
  54.5 1.2 local.10.refs_0_
  55.7 2.1 %collective-permute-done.6.refs_2_ = bf16[32,768]{1,0:T(8,128)(2,1)S(1)} collective-permute-done((bf16[32,768]{1,0:T(8,128)(2,1)S(1)}, bf16[32,768]{1,0:T(8,128)(2,1)S(1)}, u32[]{:S(2)}, u32[]{:S(2)}) %collective-permute-start.6) | collective-permute-done | bytes 49184 | tf_op jit(solution)/shard_map/ppermute | solution.py:151
  58.3 1.9 %collective-permute-start.7 = (bf16[32,768]{1,0:T(8,128)(2,1)S(1)}, bf16[32,768]{1,0:T(8,128)(2,1)S(1)}, u32[]{:S(2)}, u32[]{:S(2)}) collective-permute-start(bf16[32,768]{1,0:T(8,128)(2,1)S(1)} %halo.10.refs_2_.refs_3_), channel_id=1, source_target_pairs={{0,64},{64,0},{128,192},{192,128},{256,320},{320,256},{384,448},{4... | collective-permute-start | bytes 147464 | tf_op jit(solution)/shard_map/ppermute | solution.py:150
  60.2 6.3 %collective-permute-start.8 = (bf16[32,768]{1,0:T(8,128)(2,1)S(1)}, bf16[32,768]{1,0:T(8,128)(2,1)S(1)}, u32[]{:S(2)}, u32[]{:S(2)}) collective-permute-start(bf16[32,768]{1,0:T(8,128)(2,1)S(1)} %halo.10.refs_2_.refs_3_), channel_id=1, source_target_pairs={{0,448},{64,128},{128,64},{192,256},{256,192},{320,384},{384,320},... | collective-permute-start | bytes 147464 | tf_op jit(solution)/shard_map/ppermute | solution.py:151
  66.5 1.2 local.11.refs_0_
  67.7 2.1 %collective-permute-done.8.refs_2_ = bf16[32,768]{1,0:T(8,128)(2,1)S(1)} collective-permute-done((bf16[32,768]{1,0:T(8,128)(2,1)S(1)}, bf16[32,768]{1,0:T(8,128)(2,1)S(1)}, u32[]{:S(2)}, u32[]{:S(2)}) %collective-permute-start.8) | collective-permute-done | bytes 49184 | tf_op jit(solution)/shard_map/ppermute | solution.py:151
  70.3 6.3 %collective-permute-start.10 = (bf16[32,768]{1,0:T(8,128)(2,1)S(1)}, bf16[32,768]{1,0:T(8,128)(2,1)S(1)}, u32[]{:S(2)}, u32[]{:S(2)}) collective-permute-start(bf16[32,768]{1,0:T(8,128)(2,1)S(1)} %halo.11.refs_2_.refs_3_), channel_id=1, source_target_pairs={{0,448},{64,128},{128,64},{192,256},{256,192},{320,384},{384,320},... | collective-permute-start | bytes 147464 | tf_op jit(solution)/shard_map/ppermute | solution.py:151
  76.6 1.9 %collective-permute-start.9 = (bf16[32,768]{1,0:T(8,128)(2,1)S(1)}, bf16[32,768]{1,0:T(8,128)(2,1)S(1)}, u32[]{:S(2)}, u32[]{:S(2)}) collective-permute-start(bf16[32,768]{1,0:T(8,128)(2,1)S(1)} %halo.11.refs_2_.refs_3_), channel_id=1, source_target_pairs={{0,64},{64,0},{128,192},{192,128},{256,320},{320,256},{384,448},{4... | collective-permute-start | bytes 147464 | tf_op jit(solution)/shard_map/ppermute | solution.py:150
  78.6 1.2 local.12.refs_0_
  79.9 2.7 %collective-permute-done.9.refs_1_ = bf16[32,768]{1,0:T(8,128)(2,1)S(1)} collective-permute-done((bf16[32,768]{1,0:T(8,128)(2,1)S(1)}, bf16[32,768]{1,0:T(8,128)(2,1)S(1)}, u32[]{:S(2)}, u32[]{:S(2)}) %collective-permute-start.9) | collective-permute-done | bytes 49184 | tf_op jit(solution)/shard_map/ppermute | solution.py:150
  83.1 1.9 %collective-permute-start.11 = (bf16[32,768]{1,0:T(8,128)(2,1)S(1)}, bf16[32,768]{1,0:T(8,128)(2,1)S(1)}, u32[]{:S(2)}, u32[]{:S(2)}) collective-permute-start(bf16[32,768]{1,0:T(8,128)(2,1)S(1)} %halo.12.refs_2_.refs_3_), channel_id=1, source_target_pairs={{0,64},{64,0},{128,192},{192,128},{256,320},{320,256},{384,448},{4... | collective-permute-start | bytes 147464 | tf_op jit(solution)/shard_map/ppermute | solution.py:150
  85.1 3.6 %collective-permute-start.12 = (bf16[32,768]{1,0:T(8,128)(2,1)S(1)}, bf16[32,768]{1,0:T(8,128)(2,1)S(1)}, u32[]{:S(2)}, u32[]{:S(2)}) collective-permute-start(bf16[32,768]{1,0:T(8,128)(2,1)S(1)} %halo.12.refs_2_.refs_3_), channel_id=1, source_target_pairs={{0,448},{64,128},{128,64},{192,256},{256,192},{320,384},{384,320},... | collective-permute-start | bytes 147464 | tf_op jit(solution)/shard_map/ppermute | solution.py:151
  88.7 1.2 local.13.refs_0_
  89.9 4.8 %collective-permute-done.12.refs_2_ = bf16[32,768]{1,0:T(8,128)(2,1)S(1)} collective-permute-done((bf16[32,768]{1,0:T(8,128)(2,1)S(1)}, bf16[32,768]{1,0:T(8,128)(2,1)S(1)}, u32[]{:S(2)}, u32[]{:S(2)}) %collective-permute-start.12) | collective-permute-done | bytes 49184 | tf_op jit(solution)/shard_map/ppermute | solution.py:151
  95.1 2.1 %collective-permute-start.13 = (bf16[32,768]{1,0:T(8,128)(2,1)S(1)}, bf16[32,768]{1,0:T(8,128)(2,1)S(1)}, u32[]{:S(2)}, u32[]{:S(2)}) collective-permute-start(bf16[32,768]{1,0:T(8,128)(2,1)S(1)} %halo.13.refs_2_.refs_3_), channel_id=1, source_target_pairs={{0,64},{64,0},{128,192},{192,128},{256,320},{320,256},{384,448},{4... | collective-permute-start | bytes 147464 | tf_op jit(solution)/shard_map/ppermute | solution.py:150
  97.2 3.6 %collective-permute-start.14 = (bf16[32,768]{1,0:T(8,128)(2,1)S(1)}, bf16[32,768]{1,0:T(8,128)(2,1)S(1)}, u32[]{:S(2)}, u32[]{:S(2)}) collective-permute-start(bf16[32,768]{1,0:T(8,128)(2,1)S(1)} %halo.13.refs_2_.refs_3_), channel_id=1, source_target_pairs={{0,448},{64,128},{128,64},{192,256},{256,192},{320,384},{384,320},... | collective-permute-start | bytes 147464 | tf_op jit(solution)/shard_map/ppermute | solution.py:151
  100.8 1.2 local.14.refs_0_
  102.0 4.8 %collective-permute-done.14.refs_2_ = bf16[32,768]{1,0:T(8,128)(2,1)S(1)} collective-permute-done((bf16[32,768]{1,0:T(8,128)(2,1)S(1)}, bf16[32,768]{1,0:T(8,128)(2,1)S(1)}, u32[]{:S(2)}, u32[]{:S(2)}) %collective-permute-start.14) | collective-permute-done | bytes 49184 | tf_op jit(solution)/shard_map/ppermute | solution.py:151
  106.8 0.5 halo.14.refs_2_
  107.3 1.9 %collective-permute-start.15 = (bf16[32,768]{1,0:T(8,128)(2,1)S(1)}, bf16[32,768]{1,0:T(8,128)(2,1)S(1)}, u32[]{:S(2)}, u32[]{:S(2)}) collective-permute-start(bf16[32,768]{1,0:T(8,128)(2,1)S(1)} %halo.14.refs_2_), channel_id=1, source_target_pairs={{0,64},{64,0},{128,192},{192,128},{256,320},{320,256},{384,448},{4... | collective-permute-start | bytes 147464 | tf_op jit(solution)/shard_map/ppermute | solution.py:150
  109.3 3.6 %collective-permute-start.16 = (bf16[32,768]{1,0:T(8,128)(2,1)S(1)}, bf16[32,768]{1,0:T(8,128)(2,1)S(1)}, u32[]{:S(2)}, u32[]{:S(2)}) collective-permute-start(bf16[32,768]{1,0:T(8,128)(2,1)S(1)} %halo.14.refs_2_), channel_id=1, source_target_pairs={{0,448},{64,128},{128,64},{192,256},{256,192},{320,384},{384,320},... | collective-permute-start | bytes 147464 | tf_op jit(solution)/shard_map/ppermute | solution.py:151
  113.6 1.2 local.15.refs_0_
  114.8 4.1 %collective-permute-done.16.refs_2_ = bf16[32,768]{1,0:T(8,128)(2,1)S(1)} collective-permute-done((bf16[32,768]{1,0:T(8,128)(2,1)S(1)}, bf16[32,768]{1,0:T(8,128)(2,1)S(1)}, u32[]{:S(2)}, u32[]{:S(2)}) %collective-permute-start.16) | collective-permute-done | bytes 49184 | tf_op jit(solution)/shard_map/ppermute | solution.py:151
  118.9 1.1 halo.15
  120.0 5.8 %all_gather.6.y_ref = bf16[128,768]{1,0:T(8,128)(2,1)S(1)} all-gather(bf16[32,768]{1,0:T(8,128)(2,1)} %halo.15), channel_id=1, replica_groups=mesh['elem'=8,'z'=16,'yl'=2,'c'=2] {'yl','c'}, dimensions={0}, use_global_device_ids=true | all-gather | bytes 245760 | tf_op jit(solution)/shard_map/all_gather | solution.py:177
  125.8 0.7 pick.1
  126.5 30.4 %all_to_all.5.x_ref = bf16[16,40,128]{2,1,0:T(8,128)(2,1)} all-to-all(bf16[16,40,128]{2,1,0:T(8,128)(2,1)S(1)} %pick.1), channel_id=1, replica_groups=mesh['elem'=8,'z'=16,'yl'=2,'c'=2] {'z'}, dimensions={0} | all-to-all | bytes 327680 | tf_op jit(solution)/shard_map/all_to_all | solution.py:188
  156.9 8.2 %rotate.1 = bf16[36,2048]{1,0:T(8,128)(2,1)} custom-call(s32[1]{0:T(128)} %bitcast.6.low, bf16[16,40,128]{2,1,0:T(8,128)(2,1)} %all_to_all.5.x_ref, bf16[2048,2048]{1,0:T(8,128)(2,1)} %all-gather.2.cloned.1.call-done.r_hbm), custom_call_target="tpu_custom_call" | custom-call | tf_op jit(solution)/shard_map/rotate/pallas_call | solution.py:189
  (45 shorter events, 3.4 us)
Async XLA Ops:
  7.2 23.3 %copy-start.9 = (s32[4]{0:T(128)S(1)}, s32[4]{0:T(128)}, u32[]{:S(2)}) copy-start(s32[4]{0:T(128)} %refs_1_.15) | copy-start | bytes 52
  7.2 23.3 %copy-start.7 = (s32[4,6]{1,0:T(4,128)S(1)}, s32[4,6]{1,0:T(4,128)}, u32[]{:S(2)}) copy-start(s32[4,6]{1,0:T(4,128)} %refs_0_.15) | copy-start | bytes 292
  7.2 119.3 %all-gather.2.cloned.1.call-start = ((), (), s32[]{:S(2)}) async-start(), calls=%async_computation.1 | async-start | bytes 8650752 | tf_op jit(solution)/shard_map/all_gather | solution.py:166
  7.2 12.7 %collective-permute-start = (bf16[32,2048]{1,0:T(8,128)(2,1)}, bf16[32,2048]{1,0:T(8,128)(2,1)S(1)}, u32[]{:S(2)}, u32[]{:S(2)}) collective-permute-start(bf16[32,2048]{1,0:T(8,128)(2,1)} %bitcast.8), channel_id=1, source_target_pairs={{0,2},{2,0},{1,3},{3,1},{4,6},{6,4},{5,7},{7,5},{8,10},{10,8},{9,1... | collective-permute-start | bytes 393224 | tf_op jit(solution)/shard_map/ppermute | solution.py:130
  15.6 1.8 %copy-start = (bf16[4,7,192,192]{3,2,1,0:T(8,128)(2,1)S(1)}, bf16[4,7,192,192]{3,2,1,0:T(8,128)(2,1)}, u32[]{:S(2)}) copy-start(bf16[4,7,192,192]{3,2,1,0:T(8,128)(2,1)} %refs_4_.13) | copy-start | bytes 6193156
  17.4 0.7 copy-start.6
  18.1 0.7 copy-start.8
  18.8 1.2 copy-start.10
  18.8 11.7 %copy-start.1 = (bf16[4,7,192,192]{3,2,1,0:T(8,128)(2,1)S(1)}, bf16[4,7,192,192]{3,2,1,0:T(8,128)(2,1)}, u32[]{:S(2)}) copy-start(bf16[4,7,192,192]{3,2,1,0:T(8,128)(2,1)} %refs_4_.13) | copy-start | bytes 6193156
  20.7 10.7 %collective-permute-start.1 = (bf16[32,768]{1,0:T(8,128)(2,1)S(1)}, bf16[32,768]{1,0:T(8,128)(2,1)S(1)}, u32[]{:S(2)}, u32[]{:S(2)}) collective-permute-start(bf16[32,768]{1,0:T(8,128)(2,1)S(1)} %broadcast_select_fusion.refs_2_.refs_3_), channel_id=1, source_target_pairs={{0,64},{64,0},{128,192},{192,128},{256,320},{320,256},{384,448},{4... | collective-permute-start | bytes 147464 | tf_op jit(solution)/shard_map/ppermute | solution.py:150
  24.1 9.6 %collective-permute-start.2 = (bf16[32,768]{1,0:T(8,128)(2,1)S(1)}, bf16[32,768]{1,0:T(8,128)(2,1)S(1)}, u32[]{:S(2)}, u32[]{:S(2)}) collective-permute-start(bf16[32,768]{1,0:T(8,128)(2,1)S(1)} %broadcast_select_fusion.refs_2_.refs_3_), channel_id=1, source_target_pairs={{0,448},{64,128},{128,64},{192,256},{256,192},{320,384},{384,320},... | collective-permute-start | bytes 147464 | tf_op jit(solution)/shard_map/ppermute | solution.py:151
  31.4 75.4 %copy-start.2 = (bf16[768,768]{1,0:T(8,128)(2,1)}, bf16[768,768]{1,0:T(8,128)(2,1)S(1)}, u32[]{:S(2)}) copy-start(bf16[768,768]{1,0:T(8,128)(2,1)S(1)} %get-tuple-element.9.refs_3_) | copy-start | bytes 3538948
  31.4 75.4 %copy-start.4 = (bf16[768,768]{1,0:T(8,128)(2,1)}, bf16[768,768]{1,0:T(8,128)(2,1)S(1)}, u32[]{:S(2)}) copy-start(bf16[768,768]{1,0:T(8,128)(2,1)S(1)} %get-tuple-element.10.refs_4_) | copy-start | bytes 3538948
  34.2 9.5 %collective-permute-start.3 = (bf16[32,768]{1,0:T(8,128)(2,1)S(1)}, bf16[32,768]{1,0:T(8,128)(2,1)S(1)}, u32[]{:S(2)}, u32[]{:S(2)}) collective-permute-start(bf16[32,768]{1,0:T(8,128)(2,1)S(1)} %halo.8.refs_2_.refs_3_), channel_id=1, source_target_pairs={{0,64},{64,0},{128,192},{192,128},{256,320},{320,256},{384,448},{4... | collective-permute-start | bytes 147464 | tf_op jit(solution)/shard_map/ppermute | solution.py:150
  36.1 9.6 %collective-permute-start.4 = (bf16[32,768]{1,0:T(8,128)(2,1)S(1)}, bf16[32,768]{1,0:T(8,128)(2,1)S(1)}, u32[]{:S(2)}, u32[]{:S(2)}) collective-permute-start(bf16[32,768]{1,0:T(8,128)(2,1)S(1)} %halo.8.refs_2_.refs_3_), channel_id=1, source_target_pairs={{0,448},{64,128},{128,64},{192,256},{256,192},{320,384},{384,320},... | collective-permute-start | bytes 147464 | tf_op jit(solution)/shard_map/ppermute | solution.py:151
  46.2 9.5 %collective-permute-start.5 = (bf16[32,768]{1,0:T(8,128)(2,1)S(1)}, bf16[32,768]{1,0:T(8,128)(2,1)S(1)}, u32[]{:S(2)}, u32[]{:S(2)}) collective-permute-start(bf16[32,768]{1,0:T(8,128)(2,1)S(1)} %halo.9.refs_2_.refs_3_), channel_id=1, source_target_pairs={{0,64},{64,0},{128,192},{192,128},{256,320},{320,256},{384,448},{4... | collective-permute-start | bytes 147464 | tf_op jit(solution)/shard_map/ppermute | solution.py:150
  48.2 9.6 %collective-permute-start.6 = (bf16[32,768]{1,0:T(8,128)(2,1)S(1)}, bf16[32,768]{1,0:T(8,128)(2,1)S(1)}, u32[]{:S(2)}, u32[]{:S(2)}) collective-permute-start(bf16[32,768]{1,0:T(8,128)(2,1)S(1)} %halo.9.refs_2_.refs_3_), channel_id=1, source_target_pairs={{0,448},{64,128},{128,64},{192,256},{256,192},{320,384},{384,320},... | collective-permute-start | bytes 147464 | tf_op jit(solution)/shard_map/ppermute | solution.py:151
  58.3 9.5 %collective-permute-start.7 = (bf16[32,768]{1,0:T(8,128)(2,1)S(1)}, bf16[32,768]{1,0:T(8,128)(2,1)S(1)}, u32[]{:S(2)}, u32[]{:S(2)}) collective-permute-start(bf16[32,768]{1,0:T(8,128)(2,1)S(1)} %halo.10.refs_2_.refs_3_), channel_id=1, source_target_pairs={{0,64},{64,0},{128,192},{192,128},{256,320},{320,256},{384,448},{4... | collective-permute-start | bytes 147464 | tf_op jit(solution)/shard_map/ppermute | solution.py:150
  60.2 9.6 %collective-permute-start.8 = (bf16[32,768]{1,0:T(8,128)(2,1)S(1)}, bf16[32,768]{1,0:T(8,128)(2,1)S(1)}, u32[]{:S(2)}, u32[]{:S(2)}) collective-permute-start(bf16[32,768]{1,0:T(8,128)(2,1)S(1)} %halo.10.refs_2_.refs_3_), channel_id=1, source_target_pairs={{0,448},{64,128},{128,64},{192,256},{256,192},{320,384},{384,320},... | collective-permute-start | bytes 147464 | tf_op jit(solution)/shard_map/ppermute | solution.py:151
  70.3 9.6 %collective-permute-start.10 = (bf16[32,768]{1,0:T(8,128)(2,1)S(1)}, bf16[32,768]{1,0:T(8,128)(2,1)S(1)}, u32[]{:S(2)}, u32[]{:S(2)}) collective-permute-start(bf16[32,768]{1,0:T(8,128)(2,1)S(1)} %halo.11.refs_2_.refs_3_), channel_id=1, source_target_pairs={{0,448},{64,128},{128,64},{192,256},{256,192},{320,384},{384,320},... | collective-permute-start | bytes 147464 | tf_op jit(solution)/shard_map/ppermute | solution.py:151
  76.6 6.0 %collective-permute-start.9 = (bf16[32,768]{1,0:T(8,128)(2,1)S(1)}, bf16[32,768]{1,0:T(8,128)(2,1)S(1)}, u32[]{:S(2)}, u32[]{:S(2)}) collective-permute-start(bf16[32,768]{1,0:T(8,128)(2,1)S(1)} %halo.11.refs_2_.refs_3_), channel_id=1, source_target_pairs={{0,64},{64,0},{128,192},{192,128},{256,320},{320,256},{384,448},{4... | collective-permute-start | bytes 147464 | tf_op jit(solution)/shard_map/ppermute | solution.py:150
  83.1 6.7 %collective-permute-start.11 = (bf16[32,768]{1,0:T(8,128)(2,1)S(1)}, bf16[32,768]{1,0:T(8,128)(2,1)S(1)}, u32[]{:S(2)}, u32[]{:S(2)}) collective-permute-start(bf16[32,768]{1,0:T(8,128)(2,1)S(1)} %halo.12.refs_2_.refs_3_), channel_id=1, source_target_pairs={{0,64},{64,0},{128,192},{192,128},{256,320},{320,256},{384,448},{4... | collective-permute-start | bytes 147464 | tf_op jit(solution)/shard_map/ppermute | solution.py:150
  85.1 9.6 %collective-permute-start.12 = (bf16[32,768]{1,0:T(8,128)(2,1)S(1)}, bf16[32,768]{1,0:T(8,128)(2,1)S(1)}, u32[]{:S(2)}, u32[]{:S(2)}) collective-permute-start(bf16[32,768]{1,0:T(8,128)(2,1)S(1)} %halo.12.refs_2_.refs_3_), channel_id=1, source_target_pairs={{0,448},{64,128},{128,64},{192,256},{256,192},{320,384},{384,320},... | collective-permute-start | bytes 147464 | tf_op jit(solution)/shard_map/ppermute | solution.py:151
  95.1 17.7 %copy-start.11 = (s32[64]{0:T(128)S(1)}, s32[64]{0:T(128)}, u32[]{:S(2)}) copy-start(s32[64]{0:T(128)} %param.10) | copy-start | bytes 772
  95.1 6.9 %collective-permute-start.13 = (bf16[32,768]{1,0:T(8,128)(2,1)S(1)}, bf16[32,768]{1,0:T(8,128)(2,1)S(1)}, u32[]{:S(2)}, u32[]{:S(2)}) collective-permute-start(bf16[32,768]{1,0:T(8,128)(2,1)S(1)} %halo.13.refs_2_.refs_3_), channel_id=1, source_target_pairs={{0,64},{64,0},{128,192},{192,128},{256,320},{320,256},{384,448},{4... | collective-permute-start | bytes 147464 | tf_op jit(solution)/shard_map/ppermute | solution.py:150
  97.2 9.6 %collective-permute-start.14 = (bf16[32,768]{1,0:T(8,128)(2,1)S(1)}, bf16[32,768]{1,0:T(8,128)(2,1)S(1)}, u32[]{:S(2)}, u32[]{:S(2)}) collective-permute-start(bf16[32,768]{1,0:T(8,128)(2,1)S(1)} %halo.13.refs_2_.refs_3_), channel_id=1, source_target_pairs={{0,448},{64,128},{128,64},{192,256},{256,192},{320,384},{384,320},... | collective-permute-start | bytes 147464 | tf_op jit(solution)/shard_map/ppermute | solution.py:151
  107.3 7.4 %collective-permute-start.15 = (bf16[32,768]{1,0:T(8,128)(2,1)S(1)}, bf16[32,768]{1,0:T(8,128)(2,1)S(1)}, u32[]{:S(2)}, u32[]{:S(2)}) collective-permute-start(bf16[32,768]{1,0:T(8,128)(2,1)S(1)} %halo.14.refs_2_), channel_id=1, source_target_pairs={{0,64},{64,0},{128,192},{192,128},{256,320},{320,256},{384,448},{4... | collective-permute-start | bytes 147464 | tf_op jit(solution)/shard_map/ppermute | solution.py:150
  109.3 9.6 %collective-permute-start.16 = (bf16[32,768]{1,0:T(8,128)(2,1)S(1)}, bf16[32,768]{1,0:T(8,128)(2,1)S(1)}, u32[]{:S(2)}, u32[]{:S(2)}) collective-permute-start(bf16[32,768]{1,0:T(8,128)(2,1)S(1)} %halo.14.refs_2_), channel_id=1, source_target_pairs={{0,448},{64,128},{128,64},{192,256},{256,192},{320,384},{384,320},... | collective-permute-start | bytes 147464 | tf_op jit(solution)/shard_map/ppermute | solution.py:151
  113.4 5.5 %copy-start.3 = (bf16[768,768]{1,0:T(8,128)(2,1)S(1)}, bf16[768,768]{1,0:T(8,128)(2,1)}, u32[]{:S(2)}) copy-start(bf16[768,768]{1,0:T(8,128)(2,1)} %copy-done.2) | copy-start | bytes 3538948
  113.4 5.5 %copy-start.5 = (bf16[768,768]{1,0:T(8,128)(2,1)S(1)}, bf16[768,768]{1,0:T(8,128)(2,1)}, u32[]{:S(2)}) copy-start(bf16[768,768]{1,0:T(8,128)(2,1)} %copy-done.4) | copy-start | bytes 3538948
Sparse Core Ops, SparseCore 0:
  20.8 82.4 all-gather.1

commit v3 on v2

v3 whole, which is shorter than its diff:
```python
import jax
import jax.numpy as jnp
from jax import lax
from jax.experimental import pallas as pl
from jax.experimental.pallas import tpu as pltpu
from jax.sharding import Mesh
from jax.sharding import PartitionSpec as P


DEGREE = 8
NB = 192
ELEMS_DEV = 4
ROWS = ELEMS_DEV * NB
BANDS_DEV = 32
CAP = 36
CAP_PAD = 40
Z = 16
QUAD = 4
BF16 = jnp.bfloat16
F32 = jnp.float32
TILE = 256
BAND_AXES = ("z", "yl", "c")

VMEM = pl.BlockSpec(memory_space=pltpu.VMEM)
SMEM = pl.BlockSpec(memory_space=pltpu.SMEM)


def params(mib):
    return pltpu.CompilerParams(vmem_limit_bytes=mib << 20)


def lanes(i):
    return slice(NB * i, NB * (i + 1))


def column_mask(count, rows):
    return lax.broadcasted_iota(jnp.int32, (rows, NB), 1) < count


def mask_kernel(counts, start_ref, y_ref):
    for i in range(ELEMS_DEV):
        block = start_ref[:, lanes(i)]
        y_ref[:, lanes(i)] = jnp.where(
            column_mask(counts[i], BANDS_DEV), block, jnp.zeros_like(block)
        )


def couple_kernel(neighbours, counts, parity, h_ref, even_ref, odd_ref):
    even_ref[...] = jnp.zeros_like(even_ref)
    odd_ref[...] = jnp.zeros_like(odd_ref)
    slot_even = 6 - parity[0]
    slot_odd = 5 + parity[0]
    for i in range(ELEMS_DEV):
        keep = column_mask(counts[i], NB)
        for slot, out_ref in ((slot_even, even_ref), (slot_odd, odd_ref)):
            block = h_ref[i, slot]
            block = jnp.where(keep, block, jnp.zeros_like(block))
            source = neighbours[i, slot - 1]
            out_ref[pl.ds(pl.multiple_of(source * NB, NB), NB), lanes(i)] = block


def inside_kernel(scale, has_prev, neighbours, counts, parity, y_ref, pair_ref, *refs):
    if has_prev:
        prev_ref, h_ref, w_ref, p_ref, split = refs
    else:
        h_ref, w_ref, p_ref, split = refs
    other = pl.multiple_of(BANDS_DEV * (1 - parity[0]), BANDS_DEV)
    near = jnp.dot(pair_ref[pl.ds(other, BANDS_DEV), :], w_ref[...], preferred_element_type=F32)
    for i in range(ELEMS_DEV):
        split[i] = y_ref[:, lanes(i)]
    for i in range(ELEMS_DEV):
        total = jnp.dot(split[i], h_ref[i, 0], preferred_element_type=F32)
        for slot in range(4):
            total += jnp.dot(
                split[neighbours[i, slot]], h_ref[i, slot + 1], preferred_element_type=F32
            )
        total = jnp.where(column_mask(counts[i], BANDS_DEV), total, 0.0)
        total = (total + near[:, lanes(i)]) * scale
        if has_prev:
            total = total - prev_ref[:, lanes(i)].astype(F32)
        p_ref[:, lanes(i)] = total


def far_kernel(scale, p_ref, far_ref, w_ref, y_ref):
    total = jnp.dot(far_ref[...], w_ref[...], preferred_element_type=F32)
    y_ref[...] = (p_ref[...] + total * scale).astype(BF16)


def pick_kernel(starts, counts, y_ref, out_ref, turned):
    for block in range(ROWS // 128):
        part = y_ref[:, 128 * block : 128 * (block + 1)].astype(F32)
        turned[128 * block : 128 * (block + 1), :] = part.T
    slot = lax.broadcasted_iota(jnp.int32, (CAP_PAD, QUAD * BANDS_DEV), 0)
    for z in range(Z):
        rows = turned[pl.ds(starts[z], CAP_PAD), :]
        out_ref[z] = jnp.where(slot < counts[z], rows, 0.0).astype(BF16)


def rotate_kernel(low, x_ref, r_ref, out_ref, gathered):
    for z in range(Z):
        gathered[:, 128 * z : 128 * (z + 1)] = x_ref[z]
    mine = low[0]
    for n in range(r_ref.shape[0] // TILE):
        pieces = []
        for block in range(TILE // 128):
            for y, core in ((0, 0), (0, 1), (1, 0), (1, 1)):
                first = n * TILE + 128 * block + 64 * core + 32 * (y ^ mine)
                pieces.append(r_ref[pl.ds(pl.multiple_of(first, 32), 32), :])
        product = lax.dot_general(
            jnp.concatenate(pieces, axis=0),
            gathered[...],
            (((1,), (1,)), ((), ())),
            preferred_element_type=F32,
        )
        out_ref[:, TILE * n : TILE * (n + 1)] = product.T[:CAP].astype(BF16)


def per_device(start_bands, hamiltonian, neighbours, basis_count, owner_rows, rotation):
    elem_size = lax.axis_size("elem")
    near = [[i, i + 1] for i in range(0, elem_size, 2)]
    far = [(i, (i + 1 if i % 2 else i - 1) % elem_size) for i in range(elem_size)]
    parity = (lax.axis_index("elem") % 2).astype(jnp.int32).reshape(1)
    low = lax.axis_index("yl").astype(jnp.int32).reshape(1)
    quad = lax.axis_index("yl") * 2 + lax.axis_index("c")
    row_starts = jnp.cumsum(owner_rows) - owner_rows
    my_starts = lax.dynamic_index_in_dim(row_starts.reshape(Z, QUAD), quad, 1, keepdims=False)
    my_counts = lax.dynamic_index_in_dim(owner_rows.reshape(Z, QUAD), quad, 1, keepdims=False)

    columns = rotation.T

    block_bf16 = jax.ShapeDtypeStruct((BANDS_DEV, ROWS), BF16)
    block_f32 = jax.ShapeDtypeStruct((BANDS_DEV, ROWS), F32)
    operator = jax.ShapeDtypeStruct((ROWS, ROWS), BF16)
    current = pl.pallas_call(
        mask_kernel,
        out_shape=block_bf16,
        in_specs=[SMEM, VMEM],
        out_specs=VMEM,
        compiler_params=params(4),
        name="mask",
    )(basis_count, start_bands)
    w_even, w_odd = pl.pallas_call(
        couple_kernel,
        out_shape=(operator, operator),
        in_specs=[SMEM, SMEM, SMEM, VMEM],
        out_specs=(VMEM, VMEM),
        compiler_params=params(16),
    )(neighbours, basis_count, parity, hamiltonian)
    earlier = None
    for step in range(DEGREE):
        scale = 0.5 if step == 0 else 1.0
        previous = [] if earlier is None else [earlier]
        from_far = lax.ppermute(current, "elem", far)
        pair = lax.all_gather(
            current, "elem", axis=0, tiled=True, axis_index_groups=near
        )
        partial = pl.pallas_call(
            lambda *refs, scale=scale, has_prev=bool(previous): inside_kernel(
                scale, has_prev, *refs
            ),
            out_shape=block_f32,
            in_specs=[SMEM, SMEM, SMEM, VMEM, VMEM] + [VMEM] * len(previous) + [VMEM, VMEM],
            out_specs=VMEM,
            scratch_shapes=[pltpu.VMEM((ELEMS_DEV, BANDS_DEV, NB), BF16)],
            compiler_params=params(8),
            name="inside",
        )(neighbours, basis_count, parity, current, pair, *previous, hamiltonian, w_even)
        if step == 0:
            other_columns = lax.ppermute(columns, "yl", [(0, 1), (1, 0)])
            other_columns, partial = lax.optimization_barrier((other_columns, partial))
            pieces = jnp.concatenate([columns, other_columns], axis=0)
            rotation_all = lax.all_gather(pieces, ("z", "c"), axis=0, tiled=True)
        following = pl.pallas_call(
            lambda *refs, scale=scale: far_kernel(scale, *refs),
            out_shape=block_bf16,
            in_specs=[VMEM] * 3,
            out_specs=VMEM,
            compiler_params=params(8),
            name="outside",
        )(partial, from_far, w_odd)
        earlier, current = current, following

    filtered, rotation_all = lax.optimization_barrier((current, rotation_all))
    bands_quad = lax.all_gather(filtered, ("yl", "c"), axis=0, tiled=True)
    sent = pl.pallas_call(
        pick_kernel,
        out_shape=jax.ShapeDtypeStruct((Z, CAP_PAD, QUAD * BANDS_DEV), BF16),
        in_specs=[SMEM, SMEM, VMEM],
        out_specs=VMEM,
        scratch_shapes=[pltpu.VMEM((ROWS + 48, QUAD * BANDS_DEV), F32)],
        compiler_params=params(4),
        name="pick",
    )(my_starts, my_counts, bands_quad)
    received = lax.all_to_all(sent, "z", split_axis=0, concat_axis=0, tiled=True)
    rotated = pl.pallas_call(
        rotate_kernel,
        out_shape=jax.ShapeDtypeStruct((CAP, rotation_all.shape[1]), BF16),
        in_specs=[SMEM, VMEM, VMEM],
        out_specs=VMEM,
        scratch_shapes=[pltpu.VMEM((CAP_PAD, rotation_all.shape[1]), BF16)],
        compiler_params=params(4),
        name="rotate",
    )(low, received, rotation_all)
    return current, rotated


def solution(mesh):
    fine = Mesh(mesh.devices.reshape(mesh.shape["elem"], Z, 2, 2), ("elem",) + BAND_AXES)
    placed = (
        P(BAND_AXES, "elem"),
        P("elem", None, None, None),
        P("elem", None),
        P("elem"),
        P(),
        P(None, BAND_AXES),
    )
    return jax.shard_map(
        per_device,
        mesh=fine,
        in_specs=placed,
        out_specs=(P(BAND_AXES, "elem"), P(("elem",) + BAND_AXES, None)),
        check_vma=False,
    )
```

time: 173 us -> 170 us (0.983)
  blocking collectives: 36.2 us -> 74.3 us
  waiting for transfers between devices: 25.1 us -> 4.13 us
  starting transfers between devices: 63.1 us -> 44.7 us
  local copies, waits for them, and re-layouts: 5.07 us -> 12.3 us
  Pallas kernels: 23.7 us -> 18.2 us
  between operations: 16.4 us -> 14.4 us
    all_gather x1 -> x9, blocking collectives: 5.79 us -> 44.1 us  [the longest x8 38.3 us: per_device(): lax.all_gather(current, 'elem', axis=0, tiled=True, axis_index_groups=near)]
    ppermute x8, waiting for transfers between devices: 22.3 us -> 4.11 us  [per_device(): from_far = lax.ppermute(current, 'elem', far)]
    ppermute x8 -> x0, starting transfers between devices: 17 us -> none  [per_device(): from_near = lax.ppermute(current, 'elem', near)]
    unnamed x24 -> x38, local copies, waits for them, and re-layouts: 3.16 us -> 11.8 us
    pallas_call x1, Pallas kernels: 8.23 us -> 3.04 us  [per_device(): pl.pallas_call(rotate_kernel, out_shape=jax.ShapeDtypeStruct((CAP, rotati...]
    ppermute x8 -> x0, waiting for transfers between devices: 2.75 us -> none  [per_device(): from_near = lax.ppermute(current, 'elem', near)]
    pallas_call x16 -> x17, Pallas kernels: 13.9 us -> 13.5 us  [the longest x8 9.59 us: per_device(): pl.pallas_call(lambda *refs, scale=scale, has_prev=bool(previous): inside...]
  transfers between devices with their start and end apart: 18 -> 10, of which waited for: 9 -> 3; matrix products, arithmetic and copies ran while one was open for 2% -> 0% of each run, Pallas kernels for 9% -> 9%
where the time goes in v3:
time: 170 us; the launch traced here: 169 us
  blocking collectives  74.3 us (44%)
  starting transfers between devices  44.7 us (26%)
  Pallas kernels  18.2 us (11%)
  between operations  14.4 us (8%)
  local copies, waits for them, and re-layouts  12.3 us (7%)
  waiting for transfers between devices  4.13 us (2%)
    ppermute x8, starting transfers between devices, per_device(): from_far = lax.ppermute(current, 'elem', far)  41.2 us
    all_gather x8, blocking collectives, per_device(): lax.all_gather(current, 'elem', axis=0, tiled=True, axis_index_groups=near)  38.3 us
    all_to_all x1, blocking collectives, per_device(): lax.all_to_all(sent, 'z', split_axis=0, concat_axis=0, tiled=True)  30.2 us
    unnamed x38, local copies, waits for them, and re-layouts  11.8 us
    pallas_call x8, Pallas kernels, per_device(): pl.pallas_call(lambda *refs, scale=scale, has_prev=bool(previous): inside...  9.59 us
    all_gather x1, blocking collectives, per_device(): bands_quad = lax.all_gather(filtered, ('yl', 'c'), axis=0, tiled=True)  5.79 us
    ppermute x8, waiting for transfers between devices, per_device(): from_far = lax.ppermute(current, 'elem', far)  4.11 us
    ppermute x1, starting transfers between devices, per_device(): other_columns = lax.ppermute(columns, 'yl', [(0, 1), (1, 0)])  3.49 us
  transfers between devices with their start and end apart: 10, of which 3 were waited for; matrix products, arithmetic and copies ran while one was open for 0% of the time, Pallas kernels for 9%

profile of v3, /device:TPU:32, one launch (start us, length us, event | category | flops | bytes accessed | tf_op | source)
XLA Modules:
  0.0 168.8 jit_solution(9680735602125231676)
XLA Ops:
  7.2 3.5 %collective-permute-start = (bf16[32,2048]{1,0:T(8,128)(2,1)}, bf16[32,2048]{1,0:T(8,128)(2,1)S(1)}, u32[]{:S(2)}, u32[]{:S(2)}) collective-permute-start(bf16[32,2048]{1,0:T(8,128)(2,1)} %bitcast.4), channel_id=1, source_target_pairs={{0,2},{2,0},{1,3},{3,1},{4,6},{6,4},{5,7},{7,5},{8,10},{10,8},{9,1... | collective-permute-start | bytes 393224 | tf_op jit(solution)/shard_map/ppermute | solution.py:169
  10.7 0.6 copy-done.13
  11.4 0.8 copy-done.16
  12.2 0.7 mask.1.refs_3_.refs_5_
  12.9 1.8 %copy-done = bf16[4,7,192,192]{3,2,1,0:T(8,128)(2,1)S(1)} copy-done((bf16[4,7,192,192]{3,2,1,0:T(8,128)(2,1)S(1)}, bf16[4,7,192,192]{3,2,1,0:T(8,128)(2,1)}, u32[]{:S(2)}) %copy-start) | copy-done | bytes 2064408
  14.6 0.7 copy-done.11
  15.3 0.7 copy-done.14
  16.0 0.9 shard_map.77
  16.9 4.9 %all_gather.30.refs_4_ = bf16[64,768]{1,0:T(8,128)(2,1)S(1)} all-gather(bf16[32,768]{1,0:T(8,128)(2,1)S(1)} %mask.1.refs_3_.refs_5_), channel_id=1, replica_groups={{0,64},{128,192},{256,320},{384,448},{1,65},{129,193},{257,321},{385,44..., dimensions={0}, use_global_device_ids=true | all-gather | bytes 147456 | tf_op jit(solution)/shard_map/all_gather | solution.py:154
  21.8 1.2 inside.8.refs_0_
  23.1 0.7 pad_maximum_fusion
  23.8 7.0 %collective-permute-start.1 = (bf16[32,768]{1,0:T(8,128)(2,1)S(1)}, bf16[32,768]{1,0:T(8,128)(2,1)S(1)}, u32[]{:S(2)}, u32[]{:S(2)}) collective-permute-start(bf16[32,768]{1,0:T(8,128)(2,1)S(1)} %mask.1.refs_3_.refs_5_), channel_id=1, source_target_pairs={{0,448},{64,128},{128,64},{192,256},{256,192},{320,384},{384,320},... | collective-permute-start | bytes 147464 | tf_op jit(solution)/shard_map/ppermute | solution.py:153
  30.8 2.6 %collective-permute-done.1.refs_1_ = bf16[32,768]{1,0:T(8,128)(2,1)S(1)} collective-permute-done((bf16[32,768]{1,0:T(8,128)(2,1)S(1)}, bf16[32,768]{1,0:T(8,128)(2,1)S(1)}, u32[]{:S(2)}, u32[]{:S(2)}) %collective-permute-start.1) | collective-permute-done | bytes 49184 | tf_op jit(solution)/shard_map/ppermute | solution.py:153
  33.4 1.3 copy-done.3
  34.7 0.3 outside.8.refs_3_.refs_5_
  35.0 7.1 %collective-permute-start.2 = (bf16[32,768]{1,0:T(8,128)(2,1)S(1)}, bf16[32,768]{1,0:T(8,128)(2,1)S(1)}, u32[]{:S(2)}, u32[]{:S(2)}) collective-permute-start(bf16[32,768]{1,0:T(8,128)(2,1)S(1)} %outside.8.refs_3_.refs_5_), channel_id=1, source_target_pairs={{0,448},{64,128},{128,64},{192,256},{256,192},{320,384},{384,320},... | collective-permute-start | bytes 147464 | tf_op jit(solution)/shard_map/ppermute | solution.py:153
  42.1 4.8 %all_gather.31.refs_4_ = bf16[64,768]{1,0:T(8,128)(2,1)S(1)} all-gather(bf16[32,768]{1,0:T(8,128)(2,1)S(1)} %outside.8.refs_3_.refs_5_), channel_id=1, replica_groups={{0,64},{128,192},{256,320},{384,448},{1,65},{129,193},{257,321},{385,44..., dimensions={0}, use_global_device_ids=true | all-gather | bytes 147456 | tf_op jit(solution)/shard_map/all_gather | solution.py:154
  46.9 1.3 copy-done.7
  48.2 1.2 inside.9.refs_0_
  49.4 0.3 outside.9.refs_3_.refs_5_
  49.8 2.4 %collective-permute-start.3 = (bf16[32,768]{1,0:T(8,128)(2,1)S(1)}, bf16[32,768]{1,0:T(8,128)(2,1)S(1)}, u32[]{:S(2)}, u32[]{:S(2)}) collective-permute-start(bf16[32,768]{1,0:T(8,128)(2,1)S(1)} %outside.9.refs_3_.refs_5_), channel_id=1, source_target_pairs={{0,448},{64,128},{128,64},{192,256},{256,192},{320,384},{384,320},... | collective-permute-start | bytes 147464 | tf_op jit(solution)/shard_map/ppermute | solution.py:153
  52.2 4.8 %all_gather.32.refs_4_ = bf16[64,768]{1,0:T(8,128)(2,1)S(1)} all-gather(bf16[32,768]{1,0:T(8,128)(2,1)S(1)} %outside.9.refs_3_.refs_5_), channel_id=1, replica_groups={{0,64},{128,192},{256,320},{384,448},{1,65},{129,193},{257,321},{385,44..., dimensions={0}, use_global_device_ids=true | all-gather | bytes 147456 | tf_op jit(solution)/shard_map/all_gather | solution.py:154
  57.0 1.2 inside.10.refs_0_
  58.2 1.2 collective-permute-done.3.refs_1_
  59.7 5.8 %collective-permute-start.4 = (bf16[32,768]{1,0:T(8,128)(2,1)S(1)}, bf16[32,768]{1,0:T(8,128)(2,1)S(1)}, u32[]{:S(2)}, u32[]{:S(2)}) collective-permute-start(bf16[32,768]{1,0:T(8,128)(2,1)S(1)} %outside.10.refs_3_.refs_5_), channel_id=1, source_target_pairs={{0,448},{64,128},{128,64},{192,256},{256,192},{320,384},{384,320},... | collective-permute-start | bytes 147464 | tf_op jit(solution)/shard_map/ppermute | solution.py:153
  65.5 4.8 %all_gather.33.refs_4_ = bf16[64,768]{1,0:T(8,128)(2,1)S(1)} all-gather(bf16[32,768]{1,0:T(8,128)(2,1)S(1)} %outside.10.refs_3_.refs_5_), channel_id=1, replica_groups={{0,64},{128,192},{256,320},{384,448},{1,65},{129,193},{257,321},{385,44..., dimensions={0}, use_global_device_ids=true | all-gather | bytes 147456 | tf_op jit(solution)/shard_map/all_gather | solution.py:154
  70.3 1.2 inside.11.refs_0_
  71.5 0.3 outside.11.refs_3_.refs_5_
  71.8 3.6 %collective-permute-start.5 = (bf16[32,768]{1,0:T(8,128)(2,1)S(1)}, bf16[32,768]{1,0:T(8,128)(2,1)S(1)}, u32[]{:S(2)}, u32[]{:S(2)}) collective-permute-start(bf16[32,768]{1,0:T(8,128)(2,1)S(1)} %outside.11.refs_3_.refs_5_), channel_id=1, source_target_pairs={{0,448},{64,128},{128,64},{192,256},{256,192},{320,384},{384,320},... | collective-permute-start | bytes 147464 | tf_op jit(solution)/shard_map/ppermute | solution.py:153
  75.4 4.8 %all_gather.34.refs_4_ = bf16[64,768]{1,0:T(8,128)(2,1)S(1)} all-gather(bf16[32,768]{1,0:T(8,128)(2,1)S(1)} %outside.11.refs_3_.refs_5_), channel_id=1, replica_groups={{0,64},{128,192},{256,320},{384,448},{1,65},{129,193},{257,321},{385,44..., dimensions={0}, use_global_device_ids=true | all-gather | bytes 147456 | tf_op jit(solution)/shard_map/all_gather | solution.py:154
  80.2 1.2 inside.12.refs_0_
  81.7 5.8 %collective-permute-start.6 = (bf16[32,768]{1,0:T(8,128)(2,1)S(1)}, bf16[32,768]{1,0:T(8,128)(2,1)S(1)}, u32[]{:S(2)}, u32[]{:S(2)}) collective-permute-start(bf16[32,768]{1,0:T(8,128)(2,1)S(1)} %outside.12.refs_3_.refs_5_), channel_id=1, source_target_pairs={{0,448},{64,128},{128,64},{192,256},{256,192},{320,384},{384,320},... | collective-permute-start | bytes 147464 | tf_op jit(solution)/shard_map/ppermute | solution.py:153
  87.6 4.8 %all_gather.35.refs_4_ = bf16[64,768]{1,0:T(8,128)(2,1)S(1)} all-gather(bf16[32,768]{1,0:T(8,128)(2,1)S(1)} %outside.12.refs_3_.refs_5_), channel_id=1, replica_groups={{0,64},{128,192},{256,320},{384,448},{1,65},{129,193},{257,321},{385,44..., dimensions={0}, use_global_device_ids=true | all-gather | bytes 147456 | tf_op jit(solution)/shard_map/all_gather | solution.py:154
  92.3 1.2 inside.13.refs_0_
  93.6 0.3 outside.13.refs_3_.refs_5_
  93.9 3.6 %collective-permute-start.7 = (bf16[32,768]{1,0:T(8,128)(2,1)S(1)}, bf16[32,768]{1,0:T(8,128)(2,1)S(1)}, u32[]{:S(2)}, u32[]{:S(2)}) collective-permute-start(bf16[32,768]{1,0:T(8,128)(2,1)S(1)} %outside.13.refs_3_.refs_5_), channel_id=1, source_target_pairs={{0,448},{64,128},{128,64},{192,256},{256,192},{320,384},{384,320},... | collective-permute-start | bytes 147464 | tf_op jit(solution)/shard_map/ppermute | solution.py:153
  97.5 4.8 %all_gather.36.refs_4_ = bf16[64,768]{1,0:T(8,128)(2,1)S(1)} all-gather(bf16[32,768]{1,0:T(8,128)(2,1)S(1)} %outside.13.refs_3_.refs_5_), channel_id=1, replica_groups={{0,64},{128,192},{256,320},{384,448},{1,65},{129,193},{257,321},{385,44..., dimensions={0}, use_global_device_ids=true | all-gather | bytes 147456 | tf_op jit(solution)/shard_map/all_gather | solution.py:154
  102.3 1.2 inside.14.refs_0_
  104.1 5.7 %collective-permute-start.8 = (bf16[32,768]{1,0:T(8,128)(2,1)S(1)}, bf16[32,768]{1,0:T(8,128)(2,1)S(1)}, u32[]{:S(2)}, u32[]{:S(2)}) collective-permute-start(bf16[32,768]{1,0:T(8,128)(2,1)S(1)} %outside.14.refs_3_), channel_id=1, source_target_pairs={{0,448},{64,128},{128,64},{192,256},{256,192},{320,384},{384,320},... | collective-permute-start | bytes 147464 | tf_op jit(solution)/shard_map/ppermute | solution.py:153
  110.6 4.9 %all_gather.37.refs_4_ = bf16[64,768]{1,0:T(8,128)(2,1)S(1)} all-gather(bf16[32,768]{1,0:T(8,128)(2,1)S(1)} %outside.14.refs_3_), channel_id=1, replica_groups={{0,64},{128,192},{256,320},{384,448},{1,65},{129,193},{257,321},{385,44..., dimensions={0}, use_global_device_ids=true | all-gather | bytes 147456 | tf_op jit(solution)/shard_map/all_gather | solution.py:154
  115.4 1.3 copy-done.9
  116.7 1.2 inside.15.refs_0_
  117.9 1.0 outside.15
  118.9 5.8 %all_gather.39.y_ref = bf16[128,768]{1,0:T(8,128)(2,1)S(1)} all-gather(bf16[32,768]{1,0:T(8,128)(2,1)} %outside.15), channel_id=1, replica_groups=mesh['elem'=8,'z'=16,'yl'=2,'c'=2] {'yl','c'}, dimensions={0}, use_global_device_ids=true | all-gather | bytes 245760 | tf_op jit(solution)/shard_map/all_gather | solution.py:184
  124.7 0.7 pick.1
  125.4 30.2 %all_to_all.5.x_ref = bf16[16,40,128]{2,1,0:T(8,128)(2,1)S(1)} all-to-all(bf16[16,40,128]{2,1,0:T(8,128)(2,1)S(1)} %pick.1), channel_id=1, replica_groups=mesh['elem'=8,'z'=16,'yl'=2,'c'=2] {'z'}, dimensions={0} | all-to-all | bytes 327680 | tf_op jit(solution)/shard_map/all_to_all | solution.py:194
  155.6 3.4 %copy-done.10 = bf16[2048,2048]{1,0:T(8,128)(2,1)S(1)} copy-done((bf16[2048,2048]{1,0:T(8,128)(2,1)S(1)}, bf16[2048,2048]{1,0:T(8,128)(2,1)}, u32[]{:S(2)}) %copy-start.10) | copy-done | bytes 8388632
  159.0 3.0 %rotate.1 = bf16[36,2048]{1,0:T(8,128)(2,1)} custom-call(s32[1]{0:T(128)} %bitcast.2.low, bf16[16,40,128]{2,1,0:T(8,128)(2,1)S(1)} %all_to_all.5.x_ref, bf16[2048,2048]{1,0:T(8,128)(2,1)S(1)} %copy-done.10), custom_call_target="tpu_custom_call" | custom-call | tf_op jit(solution)/shard_map/rotate/pallas_call | solution.py:195
  (49 shorter events, 2.1 us)
Async XLA Ops:
  7.2 111.7 %all-gather.2.cloned.1.call-start = ((), (), s32[]{:S(2)}) async-start(), calls=%async_computation.1 | async-start | bytes 8650752 | tf_op jit(solution)/shard_map/all_gather | solution.py:172
  7.2 15.8 %collective-permute-start = (bf16[32,2048]{1,0:T(8,128)(2,1)}, bf16[32,2048]{1,0:T(8,128)(2,1)S(1)}, u32[]{:S(2)}, u32[]{:S(2)}) collective-permute-start(bf16[32,2048]{1,0:T(8,128)(2,1)} %bitcast.4), channel_id=1, source_target_pairs={{0,2},{2,0},{1,3},{3,1},{4,6},{6,4},{5,7},{7,5},{8,10},{10,8},{9,1... | collective-permute-start | bytes 393224 | tf_op jit(solution)/shard_map/ppermute | solution.py:169
  10.7 0.7 copy-start.13
  11.4 0.8 copy-start.16
  12.9 1.8 %copy-start = (bf16[4,7,192,192]{3,2,1,0:T(8,128)(2,1)S(1)}, bf16[4,7,192,192]{3,2,1,0:T(8,128)(2,1)}, u32[]{:S(2)}) copy-start(bf16[4,7,192,192]{3,2,1,0:T(8,128)(2,1)} %refs_6_.13) | copy-start | bytes 6193156
  14.6 0.7 copy-start.11
  15.3 0.7 copy-start.14
  16.9 6.1 %copy-start.2 = (bf16[768,768]{1,0:T(8,128)(2,1)}, bf16[768,768]{1,0:T(8,128)(2,1)S(1)}, u32[]{:S(2)}) copy-start(bf16[768,768]{1,0:T(8,128)(2,1)S(1)} %get-tuple-element.10.refs_2_) | copy-start | bytes 3538948
  16.9 6.1 %copy-start.6 = (bf16[768,768]{1,0:T(8,128)(2,1)}, bf16[768,768]{1,0:T(8,128)(2,1)S(1)}, u32[]{:S(2)}) copy-start(bf16[768,768]{1,0:T(8,128)(2,1)S(1)} %get-tuple-element.8.refs_6_.refs_7_) | copy-start | bytes 3538948
  16.9 6.1 %copy-start.17 = (bf16[2048,32]{0,1:T(8,128)(2,1)S(1)}, bf16[2048,32]{0,1:T(8,128)(2,1)}, u32[]{:S(2)}) copy-start(bf16[2048,32]{0,1:T(8,128)(2,1)} %param.11) | copy-start | bytes 393220
  21.8 25.1 %copy-start.1 = (bf16[4,7,192,192]{3,2,1,0:T(8,128)(2,1)S(1)}, bf16[4,7,192,192]{3,2,1,0:T(8,128)(2,1)}, u32[]{:S(2)}) copy-start(bf16[4,7,192,192]{3,2,1,0:T(8,128)(2,1)} %refs_6_.13) | copy-start | bytes 6193156
  21.8 25.1 %copy-start.12 = (s32[4,6]{1,0:T(4,128)S(1)}, s32[4,6]{1,0:T(4,128)}, u32[]{:S(2)}) copy-start(s32[4,6]{1,0:T(4,128)} %refs_0_.15) | copy-start | bytes 292
  21.8 25.1 %copy-start.15 = (s32[4]{0:T(128)S(1)}, s32[4]{0:T(128)}, u32[]{:S(2)}) copy-start(s32[4]{0:T(128)} %refs_1_.15) | copy-start | bytes 52
  23.8 9.6 %collective-permute-start.1 = (bf16[32,768]{1,0:T(8,128)(2,1)S(1)}, bf16[32,768]{1,0:T(8,128)(2,1)S(1)}, u32[]{:S(2)}, u32[]{:S(2)}) collective-permute-start(bf16[32,768]{1,0:T(8,128)(2,1)S(1)} %mask.1.refs_3_.refs_5_), channel_id=1, source_target_pairs={{0,448},{64,128},{128,64},{192,256},{256,192},{320,384},{384,320},... | collective-permute-start | bytes 147464 | tf_op jit(solution)/shard_map/ppermute | solution.py:153
  33.4 1.3 copy-start.3
  34.7 14.7 %copy-start.4 = (bf16[768,768]{1,0:T(8,128)(2,1)S(1)}, bf16[768,768]{1,0:T(8,128)(2,1)}, u32[]{:S(2)}) copy-start(bf16[768,768]{1,0:T(8,128)(2,1)} %copy-done.2) | copy-start | bytes 3538948
  35.0 14.4 %collective-permute-start.2 = (bf16[32,768]{1,0:T(8,128)(2,1)S(1)}, bf16[32,768]{1,0:T(8,128)(2,1)S(1)}, u32[]{:S(2)}, u32[]{:S(2)}) collective-permute-start(bf16[32,768]{1,0:T(8,128)(2,1)S(1)} %outside.8.refs_3_.refs_5_), channel_id=1, source_target_pairs={{0,448},{64,128},{128,64},{192,256},{256,192},{320,384},{384,320},... | collective-permute-start | bytes 147464 | tf_op jit(solution)/shard_map/ppermute | solution.py:153
  46.9 1.3 copy-start.7
  48.2 8.7 %copy-start.8 = (bf16[768,768]{1,0:T(8,128)(2,1)S(1)}, bf16[768,768]{1,0:T(8,128)(2,1)}, u32[]{:S(2)}) copy-start(bf16[768,768]{1,0:T(8,128)(2,1)} %copy-done.6) | copy-start | bytes 3538948
  49.8 9.6 %collective-permute-start.3 = (bf16[32,768]{1,0:T(8,128)(2,1)S(1)}, bf16[32,768]{1,0:T(8,128)(2,1)S(1)}, u32[]{:S(2)}, u32[]{:S(2)}) collective-permute-start(bf16[32,768]{1,0:T(8,128)(2,1)S(1)} %outside.9.refs_3_.refs_5_), channel_id=1, source_target_pairs={{0,448},{64,128},{128,64},{192,256},{256,192},{320,384},{384,320},... | collective-permute-start | bytes 147464 | tf_op jit(solution)/shard_map/ppermute | solution.py:153
  59.7 11.8 %collective-permute-start.4 = (bf16[32,768]{1,0:T(8,128)(2,1)S(1)}, bf16[32,768]{1,0:T(8,128)(2,1)S(1)}, u32[]{:S(2)}, u32[]{:S(2)}) collective-permute-start(bf16[32,768]{1,0:T(8,128)(2,1)S(1)} %outside.10.refs_3_.refs_5_), channel_id=1, source_target_pairs={{0,448},{64,128},{128,64},{192,256},{256,192},{320,384},{384,320},... | collective-permute-start | bytes 147464 | tf_op jit(solution)/shard_map/ppermute | solution.py:153
  71.8 9.6 %collective-permute-start.5 = (bf16[32,768]{1,0:T(8,128)(2,1)S(1)}, bf16[32,768]{1,0:T(8,128)(2,1)S(1)}, u32[]{:S(2)}, u32[]{:S(2)}) collective-permute-start(bf16[32,768]{1,0:T(8,128)(2,1)S(1)} %outside.11.refs_3_.refs_5_), channel_id=1, source_target_pairs={{0,448},{64,128},{128,64},{192,256},{256,192},{320,384},{384,320},... | collective-permute-start | bytes 147464 | tf_op jit(solution)/shard_map/ppermute | solution.py:153
  81.7 11.8 %collective-permute-start.6 = (bf16[32,768]{1,0:T(8,128)(2,1)S(1)}, bf16[32,768]{1,0:T(8,128)(2,1)S(1)}, u32[]{:S(2)}, u32[]{:S(2)}) collective-permute-start(bf16[32,768]{1,0:T(8,128)(2,1)S(1)} %outside.12.refs_3_.refs_5_), channel_id=1, source_target_pairs={{0,448},{64,128},{128,64},{192,256},{256,192},{320,384},{384,320},... | collective-permute-start | bytes 147464 | tf_op jit(solution)/shard_map/ppermute | solution.py:153
  93.9 9.9 %collective-permute-start.7 = (bf16[32,768]{1,0:T(8,128)(2,1)S(1)}, bf16[32,768]{1,0:T(8,128)(2,1)S(1)}, u32[]{:S(2)}, u32[]{:S(2)}) collective-permute-start(bf16[32,768]{1,0:T(8,128)(2,1)S(1)} %outside.13.refs_3_.refs_5_), channel_id=1, source_target_pairs={{0,448},{64,128},{128,64},{192,256},{256,192},{320,384},{384,320},... | collective-permute-start | bytes 147464 | tf_op jit(solution)/shard_map/ppermute | solution.py:153
  102.3 7.6 %copy-start.18 = (s32[64]{0:T(128)S(1)}, s32[64]{0:T(128)}, u32[]{:S(2)}) copy-start(s32[64]{0:T(128)} %param.10) | copy-start | bytes 772
  104.1 13.8 %collective-permute-start.8 = (bf16[32,768]{1,0:T(8,128)(2,1)S(1)}, bf16[32,768]{1,0:T(8,128)(2,1)S(1)}, u32[]{:S(2)}, u32[]{:S(2)}) collective-permute-start(bf16[32,768]{1,0:T(8,128)(2,1)S(1)} %outside.14.refs_3_), channel_id=1, source_target_pairs={{0,448},{64,128},{128,64},{192,256},{256,192},{320,384},{384,320},... | collective-permute-start | bytes 147464 | tf_op jit(solution)/shard_map/ppermute | solution.py:153
  110.4 7.6 %copy-start.5 = (bf16[768,768]{1,0:T(8,128)(2,1)S(1)}, bf16[768,768]{1,0:T(8,128)(2,1)}, u32[]{:S(2)}) copy-start(bf16[768,768]{1,0:T(8,128)(2,1)} %copy-done.2) | copy-start | bytes 3538948
  115.4 1.3 copy-start.9
  155.6 3.4 %copy-start.10 = (bf16[2048,2048]{1,0:T(8,128)(2,1)S(1)}, bf16[2048,2048]{1,0:T(8,128)(2,1)}, u32[]{:S(2)}) copy-start(bf16[2048,2048]{1,0:T(8,128)(2,1)} %all-gather.2.cloned.1.call-done.r_ref) | copy-start | bytes 25165828
Sparse Core Ops, SparseCore 0:
  23.9 82.5 all-gather.1

commit v4 on v3

--- a/solution.py
+++ b/solution.py
@@ -21,6 +21,7 @@
 TILE = 256
 BAND_AXES = ("z", "yl", "c")
 
+COST = pl.CostEstimate(flops=1 << 20, bytes_accessed=16 << 20, transcendentals=0)
 VMEM = pl.BlockSpec(memory_space=pltpu.VMEM)
 SMEM = pl.BlockSpec(memory_space=pltpu.SMEM)
 
@@ -45,43 +46,47 @@
         )
 
 
-def couple_kernel(neighbours, counts, parity, h_ref, even_ref, odd_ref):
-    even_ref[...] = jnp.zeros_like(even_ref)
-    odd_ref[...] = jnp.zeros_like(odd_ref)
-    slot_even = 6 - parity[0]
-    slot_odd = 5 + parity[0]
+def couple_kernel(neighbours, counts, parity, h_ref, inner_ref, outer_ref, column):
+    inner_ref[ROWS:, :] = jnp.zeros((ROWS, ROWS), BF16)
+    outer_ref[...] = jnp.zeros_like(outer_ref)
+    slot_near = 6 - parity[0]
+    slot_far = 5 + parity[0]
     for i in range(ELEMS_DEV):
         keep = column_mask(counts[i], NB)
-        for slot, out_ref in ((slot_even, even_ref), (slot_odd, odd_ref)):
-            block = h_ref[i, slot]
-            block = jnp.where(keep, block, jnp.zeros_like(block))
-            source = neighbours[i, slot - 1]
-            out_ref[pl.ds(pl.multiple_of(source * NB, NB), NB), lanes(i)] = block
-
-
-def inside_kernel(scale, has_prev, neighbours, counts, parity, y_ref, pair_ref, *refs):
+
+        def block(slot, i=i, keep=keep):
+            value = h_ref[i, slot]
+            return jnp.where(keep, value, jnp.zeros_like(value))
+
+        def rows(source):
+            return pl.ds(pl.multiple_of(source * NB, NB), NB)
+
+        column[...] = jnp.zeros_like(column)
+        column[lanes(i), :] = block(0).astype(F32)
+        for slot in range(1, 5):
+            column[rows(neighbours[i, slot - 1]), :] += block(slot).astype(F32)
+        inner_ref[:ROWS, lanes(i)] = column[...].astype(BF16)
+        inner_ref[rows(ELEMS_DEV + neighbours[i, slot_near - 1]), lanes(i)] = block(slot_near)
+        outer_ref[rows(neighbours[i, slot_far - 1]), lanes(i)] = block(slot_far)
+
+
+def inside_kernel(scale, has_prev, y_ref, pair_ref, second_ref, *refs):
     if has_prev:
-        prev_ref, h_ref, w_ref, p_ref, split = refs
+        prev_ref, w_ref, p_ref = refs
     else:
-        h_ref, w_ref, p_ref, split = refs
-    other = pl.multiple_of(BANDS_DEV * (1 - parity[0]), BANDS_DEV)
-    near = jnp.dot(pair_ref[pl.ds(other, BANDS_DEV), :], w_ref[...], preferred_element_type=F32)
-    for i in range(ELEMS_DEV):
-        split[i] = y_ref[:, lanes(i)]
-    for i in range(ELEMS_DEV):
-        total = jnp.dot(split[i], h_ref[i, 0], preferred_element_type=F32)
-        for slot in range(4):
-            total += jnp.dot(
-                split[neighbours[i, slot]], h_ref[i, slot + 1], preferred_element_type=F32
-            )
-        total = jnp.where(column_mask(counts[i], BANDS_DEV), total, 0.0)
-        total = (total + near[:, lanes(i)]) * scale
-        if has_prev:
-            total = total - prev_ref[:, lanes(i)].astype(F32)
-        p_ref[:, lanes(i)] = total
-
-
-def far_kernel(scale, p_ref, far_ref, w_ref, y_ref):
+        w_ref, p_ref = refs
+    near = jnp.where(
+        second_ref[...] > 0.0, pair_ref[BANDS_DEV:, :].astype(F32), pair_ref[:BANDS_DEV, :].astype(F32)
+    ).astype(BF16)
+    total = jnp.dot(y_ref[...], w_ref[:ROWS, :], preferred_element_type=F32)
+    total += jnp.dot(near, w_ref[ROWS:, :], preferred_element_type=F32)
+    total = total * scale
+    if has_prev:
+        total = total - prev_ref[...].astype(F32)
+    p_ref[...] = total
+
+
+def outside_kernel(scale, p_ref, far_ref, w_ref, y_ref):
     total = jnp.dot(far_ref[...], w_ref[...], preferred_element_type=F32)
     y_ref[...] = (p_ref[...] + total * scale).astype(BF16)
 
@@ -120,6 +125,7 @@
     near = [[i, i + 1] for i in range(0, elem_size, 2)]
     far = [(i, (i + 1 if i % 2 else i - 1) % elem_size) for i in range(elem_size)]
     parity = (lax.axis_index("elem") % 2).astype(jnp.int32).reshape(1)
+    second = jnp.broadcast_to((1 - parity).astype(F32)[:, None], (1, ROWS))
     low = lax.axis_index("yl").astype(jnp.int32).reshape(1)
     quad = lax.axis_index("yl") * 2 + lax.axis_index("c")
     row_starts = jnp.cumsum(owner_rows) - owner_rows
@@ -130,7 +136,6 @@
 
     block_bf16 = jax.ShapeDtypeStruct((BANDS_DEV, ROWS), BF16)
     block_f32 = jax.ShapeDtypeStruct((BANDS_DEV, ROWS), F32)
-    operator = jax.ShapeDtypeStruct((ROWS, ROWS), BF16)
     current = pl.pallas_call(
         mask_kernel,
         out_shape=block_bf16,
@@ -139,49 +144,54 @@
         compiler_params=params(4),
         name="mask",
     )(basis_count, start_bands)
-    w_even, w_odd = pl.pallas_call(
+    w_inner, w_outer = pl.pallas_call(
         couple_kernel,
-        out_shape=(operator, operator),
+        out_shape=(
+            jax.ShapeDtypeStruct((2 * ROWS, ROWS), BF16),
+            jax.ShapeDtypeStruct((ROWS, ROWS), BF16),
+        ),
         in_specs=[SMEM, SMEM, SMEM, VMEM],
         out_specs=(VMEM, VMEM),
-        compiler_params=params(16),
+        scratch_shapes=[pltpu.VMEM((ROWS, NB), F32)],
+        compiler_params=params(12),
+        name="couple",
     )(neighbours, basis_count, parity, hamiltonian)
     earlier = None
     for step in range(DEGREE):
         scale = 0.5 if step == 0 else 1.0
         previous = [] if earlier is None else [earlier]
         from_far = lax.ppermute(current, "elem", far)
-        pair = lax.all_gather(
-            current, "elem", axis=0, tiled=True, axis_index_groups=near
-        )
+        mine = current
+        if step == 0:
+            other_columns = lax.ppermute(columns, "yl", [(0, 1), (1, 0)])
+            pieces = jnp.concatenate([columns, other_columns], axis=0)
+            pieces, mine, w_inner = lax.optimization_barrier((pieces, mine, w_inner))
+            rotation_all = lax.all_gather(pieces, ("z", "c"), axis=0, tiled=True)
+        pair = lax.all_gather(mine, "elem", axis=0, tiled=True, axis_index_groups=near)
         partial = pl.pallas_call(
             lambda *refs, scale=scale, has_prev=bool(previous): inside_kernel(
                 scale, has_prev, *refs
             ),
             out_shape=block_f32,
-            in_specs=[SMEM, SMEM, SMEM, VMEM, VMEM] + [VMEM] * len(previous) + [VMEM, VMEM],
+            in_specs=[VMEM] * (4 + len(previous)),
             out_specs=VMEM,
-            scratch_shapes=[pltpu.VMEM((ELEMS_DEV, BANDS_DEV, NB), BF16)],
-            compiler_params=params(8),
+            compiler_params=params(4),
+            cost_estimate=COST,
             name="inside",
-        )(neighbours, basis_count, parity, current, pair, *previous, hamiltonian, w_even)
-        if step == 0:
-            other_columns = lax.ppermute(columns, "yl", [(0, 1), (1, 0)])
-            other_columns, partial = lax.optimization_barrier((other_columns, partial))
-            pieces = jnp.concatenate([columns, other_columns], axis=0)
-            rotation_all = lax.all_gather(pieces, ("z", "c"), axis=0, tiled=True)
+        )(mine, pair, second, *previous, w_inner)
         following = pl.pallas_call(
-            lambda *refs, scale=scale: far_kernel(scale, *refs),
+            lambda *refs, scale=scale: outside_kernel(scale, *refs),
             out_shape=block_bf16,
             in_specs=[VMEM] * 3,
             out_specs=VMEM,
-            compiler_params=params(8),
+            compiler_params=params(4),
+            cost_estimate=COST,
             name="outside",
-        )(partial, from_far, w_odd)
+        )(partial, from_far, w_outer)
         earlier, current = current, following
 
-    filtered, rotation_all = lax.optimization_barrier((current, rotation_all))
-    bands_quad = lax.all_gather(filtered, ("yl", "c"), axis=0, tiled=True)
+    bands_quad = lax.all_gather(current, ("yl", "c"), axis=0, tiled=True)
+    bands_quad, rotation_all = lax.optimization_barrier((bands_quad, rotation_all))
     sent = pl.pallas_call(
         pick_kernel,
         out_shape=jax.ShapeDtypeStruct((Z, CAP_PAD, QUAD * BANDS_DEV), BF16),
@@ -189,6 +199,7 @@
         out_specs=VMEM,
         scratch_shapes=[pltpu.VMEM((ROWS + 48, QUAD * BANDS_DEV), F32)],
         compiler_params=params(4),
+        cost_estimate=COST,
         name="pick",
     )(my_starts, my_counts, bands_quad)
     received = lax.all_to_all(sent, "z", split_axis=0, concat_axis=0, tiled=True)

time: 170 us -> 166 us (0.976)
  waiting for transfers between devices: 4.13 us -> 0.97 us
  other arithmetic: 0.94 us -> 3.94 us
  Pallas kernels: 18.2 us -> 15.5 us
  starting transfers between devices: 44.7 us -> 42.5 us
    pallas_call x8, Pallas kernels: 9.59 us -> 4.75 us  [per_device(): pl.pallas_call(lambda *refs, scale=scale, has_prev=bool(previous): inside...]
    ppermute x8, waiting for transfers between devices: 4.11 us -> 0.95 us  [per_device(): from_far = lax.ppermute(current, 'elem', far)]
    ppermute x8, starting transfers between devices: 41.2 us -> 39 us  [per_device(): from_far = lax.ppermute(current, 'elem', far)]
    pallas_call x9, Pallas kernels: 4.13 us -> 6.36 us  [the longest x8 4.66 us: per_device(): pl.pallas_call(lambda *refs, scale=scale: outside_kernel(scale, *refs), o...]
    another operation x2, other arithmetic: 0.21 us -> 2.31 us
    unnamed x38 -> x26, local copies, waits for them, and re-layouts: 11.8 us -> 10.2 us
  transfers between devices with their start and end apart: 10 -> 10, of which waited for: 3 -> 1; matrix products, arithmetic and copies ran while one was open for 0% -> 3% of each run, Pallas kernels for 9% -> 7%
where the time goes in v4:
time: 166 us; the launch traced here: 165 us
  blocking collectives  74.5 us (45%)
  starting transfers between devices  42.5 us (26%)
  Pallas kernels  15.5 us (9%)
  between operations  14.3 us (9%)
  local copies, waits for them, and re-layouts  13.2 us (8%)
  other arithmetic  3.94 us (2%)
    ppermute x8, starting transfers between devices, per_device(): from_far = lax.ppermute(current, 'elem', far)  39 us
    all_gather x8, blocking collectives, per_device(): lax.all_gather(mine, 'elem', axis=0, tiled=True, axis_index_groups=near)  38.5 us
    all_to_all x1, blocking collectives, per_device(): lax.all_to_all(sent, 'z', split_axis=0, concat_axis=0, tiled=True)  30.3 us
    unnamed x26, local copies, waits for them, and re-layouts  10.2 us
    all_gather x1, blocking collectives, per_device(): bands_quad = lax.all_gather(current, ('yl', 'c'), axis=0, tiled=True)  5.79 us
    pallas_call x8, Pallas kernels, per_device(): pl.pallas_call(lambda *refs, scale=scale, has_prev=bool(previous): inside...  4.75 us
    pallas_call x8, Pallas kernels, per_device(): pl.pallas_call(lambda *refs, scale=scale: outside_kernel(scale, *refs), o...  4.66 us
    ppermute x1, starting transfers between devices, per_device(): other_columns = lax.ppermute(columns, 'yl', [(0, 1), (1, 0)])  3.49 us
  transfers between devices with their start and end apart: 10, of which 1 were waited for; matrix products, arithmetic and copies ran while one was open for 3% of the time, Pallas kernels for 7%

profile of v4, /device:TPU:32, one launch (start us, length us, event | category | flops | bytes accessed | tf_op | source)
XLA Modules:
  0.0 164.9 jit_solution(12009299492883384474)
XLA Ops:
  7.2 3.5 %collective-permute-start = (bf16[32,2048]{1,0:T(8,128)(2,1)}, bf16[32,2048]{1,0:T(8,128)(2,1)}, u32[]{:S(2)}, u32[]{:S(2)}) collective-permute-start(bf16[32,2048]{1,0:T(8,128)(2,1)} %bitcast.5), channel_id=1, source_target_pairs={{0,2},{2,0},{1,3},{3,1},{4,6},{6,4},{5,7},{7,5},{8,10},{10,8},{9,1... | collective-permute-start | bytes 393224 | tf_op jit(solution)/shard_map/ppermute | solution.py:166
  10.7 0.8 copy-done.7
  11.5 0.7 copy-done.8
  12.2 0.7 mask.1.refs_0_.refs_3_
  12.9 0.6 copy-done.4
  13.5 1.8 %copy-done.1 = bf16[4,7,192,192]{3,2,1,0:T(8,128)(2,1)S(1)} copy-done((bf16[4,7,192,192]{3,2,1,0:T(8,128)(2,1)S(1)}, bf16[4,7,192,192]{3,2,1,0:T(8,128)(2,1)}, u32[]{:S(2)}) %copy-start.1) | copy-done | bytes 2064408
  15.3 0.7 copy-done.9
  15.9 0.7 copy-done.10
  16.6 1.7 %couple.1 = (bf16[1536,768]{1,0:T(8,128)(2,1)S(1)}, bf16[768,768]{1,0:T(8,128)(2,1)S(1)}) custom-call(s32[4,6]{1,0:T(4,128)S(1)} %copy-done.10, s32[4]{0:T(128)S(1)} %copy-done.9, s32[1]{0:T(128)} %bitcast.1.parity, bf16[4,7,192,192]{3,2,1,0:T(8,128)(2,1)S(1)} %copy-done.1), custom_call_target="tpu_custom_call" | custom-call | tf_op jit(solution)/shard_map/couple/pallas_call | solution.py:147
  18.3 1.6 pad_maximum_fusion
  20.0 7.1 %collective-permute-start.1 = (bf16[32,768]{1,0:T(8,128)(2,1)}, bf16[32,768]{1,0:T(8,128)(2,1)S(1)}, u32[]{:S(2)}, u32[]{:S(2)}) collective-permute-start(bf16[32,768]{1,0:T(8,128)(2,1)} %copy-done.4), channel_id=1, source_target_pairs={{0,448},{64,128},{128,64},{192,256},{256,192},{320,384},{384,320},... | collective-permute-start | bytes 147464 | tf_op jit(solution)/shard_map/ppermute | solution.py:163
  27.1 5.0 %all_gather.30.refs_1_ = bf16[64,768]{1,0:T(8,128)(2,1)S(1)} all-gather(bf16[32,768]{1,0:T(8,128)(2,1)} %copy-done.4), channel_id=1, replica_groups={{0,64},{128,192},{256,320},{384,448},{1,65},{129,193},{257,321},{385,44..., dimensions={0}, use_global_device_ids=true | all-gather | bytes 147456 | tf_op jit(solution)/shard_map/all_gather | solution.py:170
  32.1 0.8 copy-done.5
  32.9 0.5 inside.8.refs_0_
  33.8 3.5 %collective-permute-start.2 = (bf16[32,768]{1,0:T(8,128)(2,1)S(1)}, bf16[32,768]{1,0:T(8,128)(2,1)S(1)}, u32[]{:S(2)}, u32[]{:S(2)}) collective-permute-start(bf16[32,768]{1,0:T(8,128)(2,1)S(1)} %outside.8.refs_0_.refs_3_), channel_id=1, source_target_pairs={{0,448},{64,128},{128,64},{192,256},{256,192},{320,384},{384,320},... | collective-permute-start | bytes 147464 | tf_op jit(solution)/shard_map/ppermute | solution.py:163
  37.3 4.8 %all_gather.31.refs_1_ = bf16[64,768]{1,0:T(8,128)(2,1)S(1)} all-gather(bf16[32,768]{1,0:T(8,128)(2,1)S(1)} %outside.8.refs_0_.refs_3_), channel_id=1, replica_groups={{0,64},{128,192},{256,320},{384,448},{1,65},{129,193},{257,321},{385,44..., dimensions={0}, use_global_device_ids=true | all-gather | bytes 147456 | tf_op jit(solution)/shard_map/all_gather | solution.py:170
  42.0 0.5 inside.9.refs_0_
  42.5 0.8 collective-permute-done.2.refs_1_
  43.7 5.1 %collective-permute-start.3 = (bf16[32,768]{1,0:T(8,128)(2,1)S(1)}, bf16[32,768]{1,0:T(8,128)(2,1)S(1)}, u32[]{:S(2)}, u32[]{:S(2)}) collective-permute-start(bf16[32,768]{1,0:T(8,128)(2,1)S(1)} %outside.9.refs_0_.refs_3_), channel_id=1, source_target_pairs={{0,448},{64,128},{128,64},{192,256},{256,192},{320,384},{384,320},... | collective-permute-start | bytes 147464 | tf_op jit(solution)/shard_map/ppermute | solution.py:163
  48.8 4.8 %all_gather.32.refs_1_ = bf16[64,768]{1,0:T(8,128)(2,1)S(1)} all-gather(bf16[32,768]{1,0:T(8,128)(2,1)S(1)} %outside.9.refs_0_.refs_3_), channel_id=1, replica_groups={{0,64},{128,192},{256,320},{384,448},{1,65},{129,193},{257,321},{385,44..., dimensions={0}, use_global_device_ids=true | all-gather | bytes 147456 | tf_op jit(solution)/shard_map/all_gather | solution.py:170
  54.4 4.3 %collective-permute-start.4 = (bf16[32,768]{1,0:T(8,128)(2,1)S(1)}, bf16[32,768]{1,0:T(8,128)(2,1)S(1)}, u32[]{:S(2)}, u32[]{:S(2)}) collective-permute-start(bf16[32,768]{1,0:T(8,128)(2,1)S(1)} %outside.10.refs_0_.refs_3_), channel_id=1, source_target_pairs={{0,448},{64,128},{128,64},{192,256},{256,192},{320,384},{384,320},... | collective-permute-start | bytes 147464 | tf_op jit(solution)/shard_map/ppermute | solution.py:163
  58.7 4.8 %all_gather.33.refs_1_ = bf16[64,768]{1,0:T(8,128)(2,1)S(1)} all-gather(bf16[32,768]{1,0:T(8,128)(2,1)S(1)} %outside.10.refs_0_.refs_3_), channel_id=1, replica_groups={{0,64},{128,192},{256,320},{384,448},{1,65},{129,193},{257,321},{385,44..., dimensions={0}, use_global_device_ids=true | all-gather | bytes 147456 | tf_op jit(solution)/shard_map/all_gather | solution.py:170
  64.3 5.1 %collective-permute-start.5 = (bf16[32,768]{1,0:T(8,128)(2,1)S(1)}, bf16[32,768]{1,0:T(8,128)(2,1)S(1)}, u32[]{:S(2)}, u32[]{:S(2)}) collective-permute-start(bf16[32,768]{1,0:T(8,128)(2,1)S(1)} %outside.11.refs_0_.refs_3_), channel_id=1, source_target_pairs={{0,448},{64,128},{128,64},{192,256},{256,192},{320,384},{384,320},... | collective-permute-start | bytes 147464 | tf_op jit(solution)/shard_map/ppermute | solution.py:163
  69.5 4.8 %all_gather.34.refs_1_ = bf16[64,768]{1,0:T(8,128)(2,1)S(1)} all-gather(bf16[32,768]{1,0:T(8,128)(2,1)S(1)} %outside.11.refs_0_.refs_3_), channel_id=1, replica_groups={{0,64},{128,192},{256,320},{384,448},{1,65},{129,193},{257,321},{385,44..., dimensions={0}, use_global_device_ids=true | all-gather | bytes 147456 | tf_op jit(solution)/shard_map/all_gather | solution.py:170
  74.2 0.5 inside.12.refs_0_
  75.1 4.3 %collective-permute-start.6 = (bf16[32,768]{1,0:T(8,128)(2,1)S(1)}, bf16[32,768]{1,0:T(8,128)(2,1)S(1)}, u32[]{:S(2)}, u32[]{:S(2)}) collective-permute-start(bf16[32,768]{1,0:T(8,128)(2,1)S(1)} %outside.12.refs_0_.refs_3_), channel_id=1, source_target_pairs={{0,448},{64,128},{128,64},{192,256},{256,192},{320,384},{384,320},... | collective-permute-start | bytes 147464 | tf_op jit(solution)/shard_map/ppermute | solution.py:163
  79.4 4.8 %all_gather.35.refs_1_ = bf16[64,768]{1,0:T(8,128)(2,1)S(1)} all-gather(bf16[32,768]{1,0:T(8,128)(2,1)S(1)} %outside.12.refs_0_.refs_3_), channel_id=1, replica_groups={{0,64},{128,192},{256,320},{384,448},{1,65},{129,193},{257,321},{385,44..., dimensions={0}, use_global_device_ids=true | all-gather | bytes 147456 | tf_op jit(solution)/shard_map/all_gather | solution.py:170
  84.2 0.5 inside.13.refs_0_
  85.0 5.1 %collective-permute-start.7 = (bf16[32,768]{1,0:T(8,128)(2,1)S(1)}, bf16[32,768]{1,0:T(8,128)(2,1)S(1)}, u32[]{:S(2)}, u32[]{:S(2)}) collective-permute-start(bf16[32,768]{1,0:T(8,128)(2,1)S(1)} %outside.13.refs_0_.refs_3_), channel_id=1, source_target_pairs={{0,448},{64,128},{128,64},{192,256},{256,192},{320,384},{384,320},... | collective-permute-start | bytes 147464 | tf_op jit(solution)/shard_map/ppermute | solution.py:163
  90.2 4.8 %all_gather.36.refs_1_ = bf16[64,768]{1,0:T(8,128)(2,1)S(1)} all-gather(bf16[32,768]{1,0:T(8,128)(2,1)S(1)} %outside.13.refs_0_.refs_3_), channel_id=1, replica_groups={{0,64},{128,192},{256,320},{384,448},{1,65},{129,193},{257,321},{385,44..., dimensions={0}, use_global_device_ids=true | all-gather | bytes 147456 | tf_op jit(solution)/shard_map/all_gather | solution.py:170
  94.9 0.5 inside.14.refs_0_
  95.4 1.0 outside.14.refs_0_
  96.4 4.3 %collective-permute-start.8 = (bf16[32,768]{1,0:T(8,128)(2,1)}, bf16[32,768]{1,0:T(8,128)(2,1)}, u32[]{:S(2)}, u32[]{:S(2)}) collective-permute-start(bf16[32,768]{1,0:T(8,128)(2,1)} %outside.14.refs_0_), channel_id=1, source_target_pairs={{0,448},{64,128},{128,64},{192,256},{256,192},{320,384},{384,320},... | collective-permute-start | bytes 147464 | tf_op jit(solution)/shard_map/ppermute | solution.py:163
  100.7 0.7 reshape.50
  101.4 0.7 copy.9
  102.1 1.4 reduce-window.9
  103.6 0.9 reduce
  104.4 0.7 reshape.49
  105.1 0.9 dynamic-slice_reduce_fusion
  106.0 5.0 %all_gather.37.refs_1_ = bf16[64,768]{1,0:T(8,128)(2,1)S(1)} all-gather(bf16[32,768]{1,0:T(8,128)(2,1)} %outside.14.refs_0_), channel_id=1, replica_groups={{0,64},{128,192},{256,320},{384,448},{1,65},{129,193},{257,321},{385,44..., dimensions={0}, use_global_device_ids=true | all-gather | bytes 147456 | tf_op jit(solution)/shard_map/all_gather | solution.py:170
  111.0 0.8 copy-done.3
  111.8 1.3 inside.15.refs_0_
  113.1 1.7 %outside.15 = bf16[32,768]{1,0:T(8,128)(2,1)} custom-call(f32[32,768]{1,0:T(8,128)S(1)} %inside.15.refs_0_, bf16[32,768]{1,0:T(8,128)(2,1)} %collective-permute-done.8.refs_1_, bf16[768,768]{1,0:T(8,128)(2,1)S(1)} %get-tuple-element.12.refs_2_), custom_call_target="tpu_custom_call" | custom-call | flops 1048576 | bytes 16777216 | tf_op jit(solution)/shard_map/outside/pallas_call | solution.py:182
  114.9 5.8 %all_gather.38.y_ref = bf16[128,768]{1,0:T(8,128)(2,1)S(1)} all-gather(bf16[32,768]{1,0:T(8,128)(2,1)} %outside.15), channel_id=1, replica_groups=mesh['elem'=8,'z'=16,'yl'=2,'c'=2] {'yl','c'}, dimensions={0}, use_global_device_ids=true | all-gather | bytes 245760 | tf_op jit(solution)/shard_map/all_gather | solution.py:193
  120.7 0.7 pick.1
  121.4 30.3 %all_to_all.5.x_ref = bf16[16,40,128]{2,1,0:T(8,128)(2,1)S(1)} all-to-all(bf16[16,40,128]{2,1,0:T(8,128)(2,1)S(1)} %pick.1), channel_id=1, replica_groups=mesh['elem'=8,'z'=16,'yl'=2,'c'=2] {'z'}, dimensions={0} | all-to-all | bytes 327680 | tf_op jit(solution)/shard_map/all_to_all | solution.py:205
  151.6 3.4 %copy-done = bf16[2048,2048]{1,0:T(8,128)(2,1)S(1)} copy-done((bf16[2048,2048]{1,0:T(8,128)(2,1)S(1)}, bf16[2048,2048]{1,0:T(8,128)(2,1)}, u32[]{:S(2)}) %copy-start) | copy-done | bytes 8388632
  155.0 3.0 %rotate.1 = bf16[36,2048]{1,0:T(8,128)(2,1)} custom-call(s32[1]{0:T(128)} %bitcast.3.low, bf16[16,40,128]{2,1,0:T(8,128)(2,1)S(1)} %all_to_all.5.x_ref, bf16[2048,2048]{1,0:T(8,128)(2,1)S(1)} %copy-done), custom_call_target="tpu_custom_call" | custom-call | tf_op jit(solution)/shard_map/rotate/pallas_call | solution.py:206
  (38 shorter events, 3.2 us)
Async XLA Ops:
  7.2 113.5 %all-gather.2.cloned.1.call-start = ((), (), s32[]{:S(2)}) async-start(), calls=%async_computation.1 | async-start | bytes 8650752 | tf_op jit(solution)/shard_map/all_gather | solution.py:169
  7.2 11.1 %collective-permute-start = (bf16[32,2048]{1,0:T(8,128)(2,1)}, bf16[32,2048]{1,0:T(8,128)(2,1)}, u32[]{:S(2)}, u32[]{:S(2)}) collective-permute-start(bf16[32,2048]{1,0:T(8,128)(2,1)} %bitcast.5), channel_id=1, source_target_pairs={{0,2},{2,0},{1,3},{3,1},{4,6},{6,4},{5,7},{7,5},{8,10},{10,8},{9,1... | collective-permute-start | bytes 393224 | tf_op jit(solution)/shard_map/ppermute | solution.py:166
  10.7 0.8 copy-start.7
  11.5 0.7 copy-start.8
  12.9 0.6 copy-start.4
  13.5 1.8 %copy-start.1 = (bf16[4,7,192,192]{3,2,1,0:T(8,128)(2,1)S(1)}, bf16[4,7,192,192]{3,2,1,0:T(8,128)(2,1)}, u32[]{:S(2)}) copy-start(bf16[4,7,192,192]{3,2,1,0:T(8,128)(2,1)} %h_ref.1) | copy-start | bytes 6193156
  15.3 0.7 copy-start.9
  15.9 0.7 copy-start.10
  16.6 1.7 %copy-start.11 = (bf16[2048,32]{0,1:T(8,128)(2,1)S(1)}, bf16[2048,32]{0,1:T(8,128)(2,1)}, u32[]{:S(2)}) copy-start(bf16[2048,32]{0,1:T(8,128)(2,1)} %param.11) | copy-start | bytes 393220
  20.0 22.0 %copy-start.6 = (bf16[32,768]{1,0:T(8,128)(2,1)S(1)}, bf16[32,768]{1,0:T(8,128)(2,1)}, u32[]{:S(2)}) copy-start(bf16[32,768]{1,0:T(8,128)(2,1)} %copy-done.4) | copy-start | bytes 147460
  20.0 13.4 %collective-permute-start.1 = (bf16[32,768]{1,0:T(8,128)(2,1)}, bf16[32,768]{1,0:T(8,128)(2,1)S(1)}, u32[]{:S(2)}, u32[]{:S(2)}) collective-permute-start(bf16[32,768]{1,0:T(8,128)(2,1)} %copy-done.4), channel_id=1, source_target_pairs={{0,448},{64,128},{128,64},{192,256},{256,192},{320,384},{384,320},... | collective-permute-start | bytes 147464 | tf_op jit(solution)/shard_map/ppermute | solution.py:163
  32.1 0.8 copy-start.5
  33.8 9.6 %collective-permute-start.2 = (bf16[32,768]{1,0:T(8,128)(2,1)S(1)}, bf16[32,768]{1,0:T(8,128)(2,1)S(1)}, u32[]{:S(2)}, u32[]{:S(2)}) collective-permute-start(bf16[32,768]{1,0:T(8,128)(2,1)S(1)} %outside.8.refs_0_.refs_3_), channel_id=1, source_target_pairs={{0,448},{64,128},{128,64},{192,256},{256,192},{320,384},{384,320},... | collective-permute-start | bytes 147464 | tf_op jit(solution)/shard_map/ppermute | solution.py:163
  43.7 10.4 %collective-permute-start.3 = (bf16[32,768]{1,0:T(8,128)(2,1)S(1)}, bf16[32,768]{1,0:T(8,128)(2,1)S(1)}, u32[]{:S(2)}, u32[]{:S(2)}) collective-permute-start(bf16[32,768]{1,0:T(8,128)(2,1)S(1)} %outside.9.refs_0_.refs_3_), channel_id=1, source_target_pairs={{0,448},{64,128},{128,64},{192,256},{256,192},{320,384},{384,320},... | collective-permute-start | bytes 147464 | tf_op jit(solution)/shard_map/ppermute | solution.py:163
  54.4 9.6 %collective-permute-start.4 = (bf16[32,768]{1,0:T(8,128)(2,1)S(1)}, bf16[32,768]{1,0:T(8,128)(2,1)S(1)}, u32[]{:S(2)}, u32[]{:S(2)}) collective-permute-start(bf16[32,768]{1,0:T(8,128)(2,1)S(1)} %outside.10.refs_0_.refs_3_), channel_id=1, source_target_pairs={{0,448},{64,128},{128,64},{192,256},{256,192},{320,384},{384,320},... | collective-permute-start | bytes 147464 | tf_op jit(solution)/shard_map/ppermute | solution.py:163
  64.3 10.4 %collective-permute-start.5 = (bf16[32,768]{1,0:T(8,128)(2,1)S(1)}, bf16[32,768]{1,0:T(8,128)(2,1)S(1)}, u32[]{:S(2)}, u32[]{:S(2)}) collective-permute-start(bf16[32,768]{1,0:T(8,128)(2,1)S(1)} %outside.11.refs_0_.refs_3_), channel_id=1, source_target_pairs={{0,448},{64,128},{128,64},{192,256},{256,192},{320,384},{384,320},... | collective-permute-start | bytes 147464 | tf_op jit(solution)/shard_map/ppermute | solution.py:163
  75.1 9.6 %collective-permute-start.6 = (bf16[32,768]{1,0:T(8,128)(2,1)S(1)}, bf16[32,768]{1,0:T(8,128)(2,1)S(1)}, u32[]{:S(2)}, u32[]{:S(2)}) collective-permute-start(bf16[32,768]{1,0:T(8,128)(2,1)S(1)} %outside.12.refs_0_.refs_3_), channel_id=1, source_target_pairs={{0,448},{64,128},{128,64},{192,256},{256,192},{320,384},{384,320},... | collective-permute-start | bytes 147464 | tf_op jit(solution)/shard_map/ppermute | solution.py:163
  84.7 16.1 %copy-start.12 = (s32[64]{0:T(128)S(1)}, s32[64]{0:T(128)}, u32[]{:S(2)}) copy-start(s32[64]{0:T(128)} %param.10) | copy-start | bytes 772
  85.0 9.9 %copy-start.2 = (bf16[32,768]{1,0:T(8,128)(2,1)}, bf16[32,768]{1,0:T(8,128)(2,1)S(1)}, u32[]{:S(2)}) copy-start(bf16[32,768]{1,0:T(8,128)(2,1)S(1)} %outside.13.refs_0_.refs_3_) | copy-start | bytes 147460
  85.0 10.4 %collective-permute-start.7 = (bf16[32,768]{1,0:T(8,128)(2,1)S(1)}, bf16[32,768]{1,0:T(8,128)(2,1)S(1)}, u32[]{:S(2)}, u32[]{:S(2)}) collective-permute-start(bf16[32,768]{1,0:T(8,128)(2,1)S(1)} %outside.13.refs_0_.refs_3_), channel_id=1, source_target_pairs={{0,448},{64,128},{128,64},{192,256},{256,192},{320,384},{384,320},... | collective-permute-start | bytes 147464 | tf_op jit(solution)/shard_map/ppermute | solution.py:163
  96.4 16.7 %collective-permute-start.8 = (bf16[32,768]{1,0:T(8,128)(2,1)}, bf16[32,768]{1,0:T(8,128)(2,1)}, u32[]{:S(2)}, u32[]{:S(2)}) collective-permute-start(bf16[32,768]{1,0:T(8,128)(2,1)} %outside.14.refs_0_), channel_id=1, source_target_pairs={{0,448},{64,128},{128,64},{192,256},{256,192},{320,384},{384,320},... | collective-permute-start | bytes 147464 | tf_op jit(solution)/shard_map/ppermute | solution.py:163
  111.0 0.8 copy-start.3
  151.6 3.4 %copy-start = (bf16[2048,2048]{1,0:T(8,128)(2,1)S(1)}, bf16[2048,2048]{1,0:T(8,128)(2,1)}, u32[]{:S(2)}) copy-start(bf16[2048,2048]{1,0:T(8,128)(2,1)} %all-gather.2.cloned.1.call-done.r_ref) | copy-start | bytes 25165828
Sparse Core Ops, SparseCore 0:
  20.1 82.0 all-gather.1

commit v5 on v4

--- a/solution.py
+++ b/solution.py
@@ -18,10 +18,10 @@
 QUAD = 4
 BF16 = jnp.bfloat16
 F32 = jnp.float32
-TILE = 256
+TILE = 1024
 BAND_AXES = ("z", "yl", "c")
 
-COST = pl.CostEstimate(flops=1 << 20, bytes_accessed=16 << 20, transcendentals=0)
+COST = pl.CostEstimate(flops=3 * 10**8, bytes_accessed=3 << 20, transcendentals=0)
 VMEM = pl.BlockSpec(memory_space=pltpu.VMEM)
 SMEM = pl.BlockSpec(memory_space=pltpu.SMEM)
 
@@ -91,33 +91,48 @@
     y_ref[...] = (p_ref[...] + total * scale).astype(BF16)
 
 
-def pick_kernel(starts, counts, y_ref, out_ref, turned):
+def pick_kernel(owner_rows, quad, y_ref, out_ref, turned):
     for block in range(ROWS // 128):
         part = y_ref[:, 128 * block : 128 * (block + 1)].astype(F32)
         turned[128 * block : 128 * (block + 1), :] = part.T
     slot = lax.broadcasted_iota(jnp.int32, (CAP_PAD, QUAD * BANDS_DEV), 0)
+    first = jnp.int32(0)
     for z in range(Z):
-        rows = turned[pl.ds(starts[z], CAP_PAD), :]
-        out_ref[z] = jnp.where(slot < counts[z], rows, 0.0).astype(BF16)
-
-
-def rotate_kernel(low, x_ref, r_ref, out_ref, gathered):
-    for z in range(Z):
-        gathered[:, 128 * z : 128 * (z + 1)] = x_ref[z]
-    mine = low[0]
-    for n in range(r_ref.shape[0] // TILE):
-        pieces = []
-        for block in range(TILE // 128):
-            for y, core in ((0, 0), (0, 1), (1, 0), (1, 1)):
-                first = n * TILE + 128 * block + 64 * core + 32 * (y ^ mine)
-                pieces.append(r_ref[pl.ds(pl.multiple_of(first, 32), 32), :])
-        product = lax.dot_general(
-            jnp.concatenate(pieces, axis=0),
-            gathered[...],
-            (((1,), (1,)), ((), ())),
-            preferred_element_type=F32,
-        )
-        out_ref[:, TILE * n : TILE * (n + 1)] = product.T[:CAP].astype(BF16)
+        counts = [owner_rows[QUAD * z + q] for q in range(QUAD)]
+        start, count = first, counts[0]
+        for q in range(1, QUAD):
+            first = first + counts[q - 1]
+            start = jnp.where(quad[0] == q, first, start)
+            count = jnp.where(quad[0] == q, counts[q], count)
+        first = first + counts[QUAD - 1]
+        rows = turned[pl.ds(start, CAP_PAD), :]
+        out_ref[z] = jnp.where(slot < count, rows, 0.0).astype(BF16)
+
+
+def join_kernel(low, own_ref, other_ref, out_ref):
+    half = own_ref.shape[0]
+    out_ref[pl.ds(pl.multiple_of(half * low[0], half), half), :] = own_ref[...]
+    out_ref[pl.ds(pl.multiple_of(half * (1 - low[0]), half), half), :] = other_ref[...]
+
+
+def rotate_kernel(x_ref, r_ref, out_ref, gathered):
+    @pl.when(pl.program_id(0) == 0)
+    def _():
+        for z in range(Z):
+            gathered[:, 128 * z : 128 * (z + 1)] = x_ref[z]
+
+    pieces = []
+    for block in range(TILE // 128):
+        for piece in (0, 2, 1, 3):
+            first = 128 * block + 32 * piece
+            pieces.append(r_ref[first : first + 32, :])
+    product = lax.dot_general(
+        jnp.concatenate(pieces, axis=0),
+        gathered[...],
+        (((1,), (1,)), ((), ())),
+        preferred_element_type=F32,
+    )
+    out_ref[...] = product.T[:CAP].astype(BF16)
 
 
 def per_device(start_bands, hamiltonian, neighbours, basis_count, owner_rows, rotation):
@@ -127,10 +142,7 @@
     parity = (lax.axis_index("elem") % 2).astype(jnp.int32).reshape(1)
     second = jnp.broadcast_to((1 - parity).astype(F32)[:, None], (1, ROWS))
     low = lax.axis_index("yl").astype(jnp.int32).reshape(1)
-    quad = lax.axis_index("yl") * 2 + lax.axis_index("c")
-    row_starts = jnp.cumsum(owner_rows) - owner_rows
-    my_starts = lax.dynamic_index_in_dim(row_starts.reshape(Z, QUAD), quad, 1, keepdims=False)
-    my_counts = lax.dynamic_index_in_dim(owner_rows.reshape(Z, QUAD), quad, 1, keepdims=False)
+    quad = (lax.axis_index("yl") * 2 + lax.axis_index("c")).astype(jnp.int32).reshape(1)
 
     columns = rotation.T
 
@@ -141,33 +153,42 @@
         out_shape=block_bf16,
         in_specs=[SMEM, VMEM],
         out_specs=VMEM,
-        compiler_params=params(4),
+        compiler_params=params(8),
+        cost_estimate=COST,
         name="mask",
     )(basis_count, start_bands)
-    w_inner, w_outer = pl.pallas_call(
-        couple_kernel,
-        out_shape=(
-            jax.ShapeDtypeStruct((2 * ROWS, ROWS), BF16),
-            jax.ShapeDtypeStruct((ROWS, ROWS), BF16),
-        ),
-        in_specs=[SMEM, SMEM, SMEM, VMEM],
-        out_specs=(VMEM, VMEM),
-        scratch_shapes=[pltpu.VMEM((ROWS, NB), F32)],
-        compiler_params=params(12),
-        name="couple",
-    )(neighbours, basis_count, parity, hamiltonian)
     earlier = None
     for step in range(DEGREE):
         scale = 0.5 if step == 0 else 1.0
         previous = [] if earlier is None else [earlier]
         from_far = lax.ppermute(current, "elem", far)
-        mine = current
+        pair = lax.all_gather(current, "elem", axis=0, tiled=True, axis_index_groups=near)
         if step == 0:
             other_columns = lax.ppermute(columns, "yl", [(0, 1), (1, 0)])
-            pieces = jnp.concatenate([columns, other_columns], axis=0)
-            pieces, mine, w_inner = lax.optimization_barrier((pieces, mine, w_inner))
+            other_columns, pair = lax.optimization_barrier((other_columns, pair))
+            pieces = pl.pallas_call(
+                join_kernel,
+                out_shape=jax.ShapeDtypeStruct((2 * BANDS_DEV, columns.shape[1]), BF16),
+                in_specs=[SMEM, VMEM, VMEM],
+                out_specs=VMEM,
+                compiler_params=params(8),
+                cost_estimate=COST,
+                name="join",
+            )(low, columns, other_columns)
+            pieces, parity, second, quad = lax.optimization_barrier((pieces, parity, second, quad))
             rotation_all = lax.all_gather(pieces, ("z", "c"), axis=0, tiled=True)
-        pair = lax.all_gather(mine, "elem", axis=0, tiled=True, axis_index_groups=near)
+            w_inner, w_outer = pl.pallas_call(
+                couple_kernel,
+                out_shape=(
+                    jax.ShapeDtypeStruct((2 * ROWS, ROWS), BF16),
+                    jax.ShapeDtypeStruct((ROWS, ROWS), BF16),
+                ),
+                in_specs=[SMEM, SMEM, SMEM, VMEM],
+                out_specs=(VMEM, VMEM),
+                scratch_shapes=[pltpu.VMEM((ROWS, NB), F32)],
+                compiler_params=params(12),
+                name="couple",
+            )(neighbours, basis_count, parity, hamiltonian)
         partial = pl.pallas_call(
             lambda *refs, scale=scale, has_prev=bool(previous): inside_kernel(
                 scale, has_prev, *refs
@@ -175,43 +196,46 @@
             out_shape=block_f32,
             in_specs=[VMEM] * (4 + len(previous)),
             out_specs=VMEM,
-            compiler_params=params(4),
+            compiler_params=params(8),
             cost_estimate=COST,
             name="inside",
-        )(mine, pair, second, *previous, w_inner)
+        )(current, pair, second, *previous, w_inner)
         following = pl.pallas_call(
             lambda *refs, scale=scale: outside_kernel(scale, *refs),
             out_shape=block_bf16,
             in_specs=[VMEM] * 3,
             out_specs=VMEM,
-            compiler_params=params(4),
+            compiler_params=params(8),
             cost_estimate=COST,
             name="outside",
         )(partial, from_far, w_outer)
         earlier, current = current, following
 
     bands_quad = lax.all_gather(current, ("yl", "c"), axis=0, tiled=True)
-    bands_quad, rotation_all = lax.optimization_barrier((bands_quad, rotation_all))
     sent = pl.pallas_call(
         pick_kernel,
         out_shape=jax.ShapeDtypeStruct((Z, CAP_PAD, QUAD * BANDS_DEV), BF16),
         in_specs=[SMEM, SMEM, VMEM],
         out_specs=VMEM,
         scratch_shapes=[pltpu.VMEM((ROWS + 48, QUAD * BANDS_DEV), F32)],
-        compiler_params=params(4),
+        compiler_params=params(8),
         cost_estimate=COST,
         name="pick",
-    )(my_starts, my_counts, bands_quad)
+    )(owner_rows, quad, bands_quad)
     received = lax.all_to_all(sent, "z", split_axis=0, concat_axis=0, tiled=True)
     rotated = pl.pallas_call(
         rotate_kernel,
         out_shape=jax.ShapeDtypeStruct((CAP, rotation_all.shape[1]), BF16),
-        in_specs=[SMEM, VMEM, VMEM],
-        out_specs=VMEM,
+        grid=(rotation_all.shape[0] // TILE,),
+        in_specs=[
+            pl.BlockSpec(received.shape, lambda n: (0, 0, 0)),
+            pl.BlockSpec((TILE, rotation_all.shape[1]), lambda n: (n, 0)),
+        ],
+        out_specs=pl.BlockSpec((CAP, TILE), lambda n: (0, n)),
         scratch_shapes=[pltpu.VMEM((CAP_PAD, rotation_all.shape[1]), BF16)],
-        compiler_params=params(4),
+        compiler_params=params(58),
         name="rotate",
-    )(low, received, rotation_all)
+    )(received, rotation_all)
     return current, rotated
 
 

time: 166 us -> 154 us (0.928)
  local copies, waits for them, and re-layouts: 13.2 us -> 5.47 us
  other arithmetic: 3.94 us -> 0 us
    unnamed x26 -> x14, local copies, waits for them, and re-layouts: 10.2 us -> 5.47 us
    pallas_call x1, Pallas kernels: 3.03 us -> 5.44 us  [per_device(): pl.pallas_call(rotate_kernel, out_shape=jax.ShapeDtypeStruct((CAP, rotati...]
    another operation x2 -> x0, other arithmetic: 2.31 us -> none
  transfers between devices with their start and end apart: 10 -> 10, of which waited for: 1 -> 2; matrix products, arithmetic and copies ran while one was open for 3% -> 0% of each run, Pallas kernels for 7% -> 7%
where the time goes in v5:
time: 154 us
  blocking collectives  74.4 us (48%)
  starting transfers between devices  42.8 us (28%)
  Pallas kernels  16.5 us (11%)
  between operations  14.2 us (9%)
  local copies, waits for them, and re-layouts  5.47 us (4%)
    ppermute x8, starting transfers between devices, per_device(): from_far = lax.ppermute(current, 'elem', far)  39.3 us
    all_gather x8, blocking collectives, per_device(): lax.all_gather(current, 'elem', axis=0, tiled=True, axis_index_groups=near)  38.5 us
    all_to_all x1, blocking collectives, per_device(): lax.all_to_all(sent, 'z', split_axis=0, concat_axis=0, tiled=True)  30.1 us
    all_gather x1, blocking collectives, per_device(): bands_quad = lax.all_gather(current, ('yl', 'c'), axis=0, tiled=True)  5.79 us
    unnamed x14, local copies, waits for them, and re-layouts  5.47 us
    pallas_call x1, Pallas kernels, per_device(): pl.pallas_call(rotate_kernel, out_shape=jax.ShapeDtypeStruct((CAP, rotati...  5.44 us
    pallas_call x8, Pallas kernels, per_device(): pl.pallas_call(lambda *refs, scale=scale, has_prev=bool(previous): inside...  3.96 us
    ppermute x1, starting transfers between devices, per_device(): other_columns = lax.ppermute(columns, 'yl', [(0, 1), (1, 0)])  3.49 us
  transfers between devices with their start and end apart: 10, of which 2 were waited for; matrix products, arithmetic and copies ran while one was open for 0% of the time, Pallas kernels for 7%

profile of v5, /device:TPU:32, one launch (start us, length us, event | category | flops | bytes accessed | tf_op | source)
XLA Modules:
  0.0 153.9 jit_solution(9945863716077063823)
XLA Ops:
  7.2 3.5 %collective-permute-start = (bf16[32,2048]{1,0:T(8,128)(2,1)}, bf16[32,2048]{1,0:T(8,128)(2,1)S(1)}, u32[]{:S(2)}, u32[]{:S(2)}) collective-permute-start(bf16[32,2048]{1,0:T(8,128)(2,1)} %bitcast.5), channel_id=1, source_target_pairs={{0,2},{2,0},{1,3},{3,1},{4,6},{6,4},{5,7},{7,5},{8,10},{10,8},{9,1... | collective-permute-start | bytes 393224 | tf_op jit(solution)/shard_map/ppermute | solution.py:167
  10.7 0.6 copy-done.2
  11.4 0.8 copy-done.5
  12.2 0.7 mask.1.refs_0_.refs_3_
  12.9 4.7 %all_gather.30.refs_1_ = bf16[64,768]{1,0:T(8,128)(2,1)S(1)} all-gather(bf16[32,768]{1,0:T(8,128)(2,1)S(1)} %mask.1.refs_0_.refs_3_), channel_id=1, replica_groups={{0,64},{128,192},{256,320},{384,448},{1,65},{129,193},{257,321},{385,44..., dimensions={0}, use_global_device_ids=true | all-gather | bytes 147456 | tf_op jit(solution)/shard_map/all_gather | solution.py:165
  17.6 0.9 copy-done.4
  18.5 0.7 join.1
  19.3 7.0 %collective-permute-start.1 = (bf16[32,768]{1,0:T(8,128)(2,1)S(1)}, bf16[32,768]{1,0:T(8,128)(2,1)S(1)}, u32[]{:S(2)}, u32[]{:S(2)}) collective-permute-start(bf16[32,768]{1,0:T(8,128)(2,1)S(1)} %mask.1.refs_0_.refs_3_), channel_id=1, source_target_pairs={{0,448},{64,128},{128,64},{192,256},{256,192},{320,384},{384,320},... | collective-permute-start | bytes 147464 | tf_op jit(solution)/shard_map/ppermute | solution.py:164
  26.3 1.8 %copy-done = bf16[4,7,192,192]{3,2,1,0:T(8,128)(2,1)S(1)} copy-done((bf16[4,7,192,192]{3,2,1,0:T(8,128)(2,1)S(1)}, bf16[4,7,192,192]{3,2,1,0:T(8,128)(2,1)}, u32[]{:S(2)}) %copy-start) | copy-done | bytes 2064408
  28.1 0.7 copy-done.1
  28.8 0.7 copy-done.3
  29.4 1.7 %couple.1 = (bf16[1536,768]{1,0:T(8,128)(2,1)S(1)}, bf16[768,768]{1,0:T(8,128)(2,1)S(1)}) custom-call(s32[4,6]{1,0:T(4,128)S(1)} %copy-done.1, s32[4]{0:T(128)S(1)} %copy-done.3, s32[1]{0:T(128)} %bitcast.2.parity, bf16[4,7,192,192]{3,2,1,0:T(8,128)(2,1)S(1)} %copy-done), custom_call_target="tpu_custom_call" | custom-call | tf_op jit(solution)/shard_map/couple/pallas_call | solution.py:180
  31.1 0.5 inside.8.refs_0_
  31.6 0.3 outside.8.refs_0_.refs_3_
  32.0 4.2 %collective-permute-start.2 = (bf16[32,768]{1,0:T(8,128)(2,1)S(1)}, bf16[32,768]{1,0:T(8,128)(2,1)S(1)}, u32[]{:S(2)}, u32[]{:S(2)}) collective-permute-start(bf16[32,768]{1,0:T(8,128)(2,1)S(1)} %outside.8.refs_0_.refs_3_), channel_id=1, source_target_pairs={{0,448},{64,128},{128,64},{192,256},{256,192},{320,384},{384,320},... | collective-permute-start | bytes 147464 | tf_op jit(solution)/shard_map/ppermute | solution.py:164
  36.2 4.8 %all_gather.31.refs_1_ = bf16[64,768]{1,0:T(8,128)(2,1)S(1)} all-gather(bf16[32,768]{1,0:T(8,128)(2,1)S(1)} %outside.8.refs_0_.refs_3_), channel_id=1, replica_groups={{0,64},{128,192},{256,320},{384,448},{1,65},{129,193},{257,321},{385,44..., dimensions={0}, use_global_device_ids=true | all-gather | bytes 147456 | tf_op jit(solution)/shard_map/all_gather | solution.py:165
  41.0 0.5 inside.9.refs_0_
  41.5 0.1 collective-permute-done.2.refs_1_
  41.5 0.3 outside.9.refs_0_.refs_3_
  41.9 5.1 %collective-permute-start.3 = (bf16[32,768]{1,0:T(8,128)(2,1)S(1)}, bf16[32,768]{1,0:T(8,128)(2,1)S(1)}, u32[]{:S(2)}, u32[]{:S(2)}) collective-permute-start(bf16[32,768]{1,0:T(8,128)(2,1)S(1)} %outside.9.refs_0_.refs_3_), channel_id=1, source_target_pairs={{0,448},{64,128},{128,64},{192,256},{256,192},{320,384},{384,320},... | collective-permute-start | bytes 147464 | tf_op jit(solution)/shard_map/ppermute | solution.py:164
  47.0 4.8 %all_gather.32.refs_1_ = bf16[64,768]{1,0:T(8,128)(2,1)S(1)} all-gather(bf16[32,768]{1,0:T(8,128)(2,1)S(1)} %outside.9.refs_0_.refs_3_), channel_id=1, replica_groups={{0,64},{128,192},{256,320},{384,448},{1,65},{129,193},{257,321},{385,44..., dimensions={0}, use_global_device_ids=true | all-gather | bytes 147456 | tf_op jit(solution)/shard_map/all_gather | solution.py:165
  51.8 0.5 inside.10.refs_0_
  52.3 0.3 outside.10.refs_0_.refs_3_
  52.6 4.3 %collective-permute-start.4 = (bf16[32,768]{1,0:T(8,128)(2,1)S(1)}, bf16[32,768]{1,0:T(8,128)(2,1)S(1)}, u32[]{:S(2)}, u32[]{:S(2)}) collective-permute-start(bf16[32,768]{1,0:T(8,128)(2,1)S(1)} %outside.10.refs_0_.refs_3_), channel_id=1, source_target_pairs={{0,448},{64,128},{128,64},{192,256},{256,192},{320,384},{384,320},... | collective-permute-start | bytes 147464 | tf_op jit(solution)/shard_map/ppermute | solution.py:164
  56.9 4.8 %all_gather.33.refs_1_ = bf16[64,768]{1,0:T(8,128)(2,1)S(1)} all-gather(bf16[32,768]{1,0:T(8,128)(2,1)S(1)} %outside.10.refs_0_.refs_3_), channel_id=1, replica_groups={{0,64},{128,192},{256,320},{384,448},{1,65},{129,193},{257,321},{385,44..., dimensions={0}, use_global_device_ids=true | all-gather | bytes 147456 | tf_op jit(solution)/shard_map/all_gather | solution.py:165
  61.7 0.5 inside.11.refs_0_
  62.2 0.3 outside.11.refs_0_.refs_3_
  62.5 5.1 %collective-permute-start.5 = (bf16[32,768]{1,0:T(8,128)(2,1)S(1)}, bf16[32,768]{1,0:T(8,128)(2,1)S(1)}, u32[]{:S(2)}, u32[]{:S(2)}) collective-permute-start(bf16[32,768]{1,0:T(8,128)(2,1)S(1)} %outside.11.refs_0_.refs_3_), channel_id=1, source_target_pairs={{0,448},{64,128},{128,64},{192,256},{256,192},{320,384},{384,320},... | collective-permute-start | bytes 147464 | tf_op jit(solution)/shard_map/ppermute | solution.py:164
  67.7 4.8 %all_gather.34.refs_1_ = bf16[64,768]{1,0:T(8,128)(2,1)S(1)} all-gather(bf16[32,768]{1,0:T(8,128)(2,1)S(1)} %outside.11.refs_0_.refs_3_), channel_id=1, replica_groups={{0,64},{128,192},{256,320},{384,448},{1,65},{129,193},{257,321},{385,44..., dimensions={0}, use_global_device_ids=true | all-gather | bytes 147456 | tf_op jit(solution)/shard_map/all_gather | solution.py:165
  72.5 0.5 inside.12.refs_0_
  73.0 0.3 outside.12.refs_0_.refs_3_
  73.3 4.3 %collective-permute-start.6 = (bf16[32,768]{1,0:T(8,128)(2,1)S(1)}, bf16[32,768]{1,0:T(8,128)(2,1)S(1)}, u32[]{:S(2)}, u32[]{:S(2)}) collective-permute-start(bf16[32,768]{1,0:T(8,128)(2,1)S(1)} %outside.12.refs_0_.refs_3_), channel_id=1, source_target_pairs={{0,448},{64,128},{128,64},{192,256},{256,192},{320,384},{384,320},... | collective-permute-start | bytes 147464 | tf_op jit(solution)/shard_map/ppermute | solution.py:164
  77.6 4.8 %all_gather.35.refs_1_ = bf16[64,768]{1,0:T(8,128)(2,1)S(1)} all-gather(bf16[32,768]{1,0:T(8,128)(2,1)S(1)} %outside.12.refs_0_.refs_3_), channel_id=1, replica_groups={{0,64},{128,192},{256,320},{384,448},{1,65},{129,193},{257,321},{385,44..., dimensions={0}, use_global_device_ids=true | all-gather | bytes 147456 | tf_op jit(solution)/shard_map/all_gather | solution.py:165
  82.4 0.5 inside.13.refs_0_
  82.9 0.3 outside.13.refs_0_.refs_3_
  83.2 5.1 %collective-permute-start.7 = (bf16[32,768]{1,0:T(8,128)(2,1)S(1)}, bf16[32,768]{1,0:T(8,128)(2,1)S(1)}, u32[]{:S(2)}, u32[]{:S(2)}) collective-permute-start(bf16[32,768]{1,0:T(8,128)(2,1)S(1)} %outside.13.refs_0_.refs_3_), channel_id=1, source_target_pairs={{0,448},{64,128},{128,64},{192,256},{256,192},{320,384},{384,320},... | collective-permute-start | bytes 147464 | tf_op jit(solution)/shard_map/ppermute | solution.py:164
  88.4 5.2 %all_gather.36.refs_1_ = bf16[64,768]{1,0:T(8,128)(2,1)S(1)} all-gather(bf16[32,768]{1,0:T(8,128)(2,1)S(1)} %outside.13.refs_0_.refs_3_), channel_id=1, replica_groups={{0,64},{128,192},{256,320},{384,448},{1,65},{129,193},{257,321},{385,44..., dimensions={0}, use_global_device_ids=true | all-gather | bytes 147456 | tf_op jit(solution)/shard_map/all_gather | solution.py:165
  93.6 0.5 inside.14.refs_0_
  94.1 0.3 outside.14.refs_0_
  94.4 4.0 %collective-permute-start.8 = (bf16[32,768]{1,0:T(8,128)(2,1)S(1)}, bf16[32,768]{1,0:T(8,128)(2,1)S(1)}, u32[]{:S(2)}, u32[]{:S(2)}) collective-permute-start(bf16[32,768]{1,0:T(8,128)(2,1)S(1)} %outside.14.refs_0_), channel_id=1, source_target_pairs={{0,448},{64,128},{128,64},{192,256},{256,192},{320,384},{384,320},... | collective-permute-start | bytes 147464 | tf_op jit(solution)/shard_map/ppermute | solution.py:164
  98.4 4.8 %all_gather.37.refs_1_ = bf16[64,768]{1,0:T(8,128)(2,1)S(1)} all-gather(bf16[32,768]{1,0:T(8,128)(2,1)S(1)} %outside.14.refs_0_), channel_id=1, replica_groups={{0,64},{128,192},{256,320},{384,448},{1,65},{129,193},{257,321},{385,44..., dimensions={0}, use_global_device_ids=true | all-gather | bytes 147456 | tf_op jit(solution)/shard_map/all_gather | solution.py:165
  103.2 0.5 inside.15.refs_0_
  103.7 0.3 collective-permute-done.8.refs_1_
  104.0 1.0 outside.15
  105.0 5.8 %all_gather.38.y_ref = bf16[128,768]{1,0:T(8,128)(2,1)S(1)} all-gather(bf16[32,768]{1,0:T(8,128)(2,1)} %outside.15), channel_id=1, replica_groups=mesh['elem'=8,'z'=16,'yl'=2,'c'=2] {'yl','c'}, dimensions={0}, use_global_device_ids=true | all-gather | bytes 245760 | tf_op jit(solution)/shard_map/all_gather | solution.py:214
  110.8 0.7 pick.1
  111.5 30.1 %all_to_all.5.x_ref = bf16[16,40,128]{2,1,0:T(8,128)(2,1)} all-to-all(bf16[16,40,128]{2,1,0:T(8,128)(2,1)S(1)} %pick.1), channel_id=1, replica_groups=mesh['elem'=8,'z'=16,'yl'=2,'c'=2] {'z'}, dimensions={0} | all-to-all | bytes 327680 | tf_op jit(solution)/shard_map/all_to_all | solution.py:225
  141.6 5.4 %rotate.1 = bf16[36,2048]{1,0:T(8,128)(2,1)} custom-call(bf16[16,40,128]{2,1,0:T(8,128)(2,1)} %all_to_all.5.x_ref, bf16[2048,2048]{1,0:T(8,128)(2,1)} %all-gather.2.cloned.1.call-done.r_ref), custom_call_target="tpu_custom_call" | custom-call | tf_op jit(solution)/shard_map/rotate/pallas_call | solution.py:226
  (19 shorter events, 0.2 us)
Async XLA Ops:
  7.2 134.4 %all-gather.2.cloned.1.call-start = ((), (), s32[]{:S(2)}) async-start(), calls=%async_computation.1 | async-start | bytes 8650752 | tf_op jit(solution)/shard_map/all_gather | solution.py:179
  7.2 10.4 %collective-permute-start = (bf16[32,2048]{1,0:T(8,128)(2,1)}, bf16[32,2048]{1,0:T(8,128)(2,1)S(1)}, u32[]{:S(2)}, u32[]{:S(2)}) collective-permute-start(bf16[32,2048]{1,0:T(8,128)(2,1)} %bitcast.5), channel_id=1, source_target_pairs={{0,2},{2,0},{1,3},{3,1},{4,6},{6,4},{5,7},{7,5},{8,10},{10,8},{9,1... | collective-permute-start | bytes 393224 | tf_op jit(solution)/shard_map/ppermute | solution.py:167
  10.7 0.7 copy-start.2
  11.4 0.8 copy-start.5
  17.6 0.9 copy-start.4
  19.3 12.3 %collective-permute-start.1 = (bf16[32,768]{1,0:T(8,128)(2,1)S(1)}, bf16[32,768]{1,0:T(8,128)(2,1)S(1)}, u32[]{:S(2)}, u32[]{:S(2)}) collective-permute-start(bf16[32,768]{1,0:T(8,128)(2,1)S(1)} %mask.1.refs_0_.refs_3_), channel_id=1, source_target_pairs={{0,448},{64,128},{128,64},{192,256},{256,192},{320,384},{384,320},... | collective-permute-start | bytes 147464 | tf_op jit(solution)/shard_map/ppermute | solution.py:164
  26.3 1.8 %copy-start = (bf16[4,7,192,192]{3,2,1,0:T(8,128)(2,1)S(1)}, bf16[4,7,192,192]{3,2,1,0:T(8,128)(2,1)}, u32[]{:S(2)}) copy-start(bf16[4,7,192,192]{3,2,1,0:T(8,128)(2,1)} %h_ref.1) | copy-start | bytes 6193156
  28.1 0.7 copy-start.1
  28.8 0.7 copy-start.3
  32.0 9.6 %collective-permute-start.2 = (bf16[32,768]{1,0:T(8,128)(2,1)S(1)}, bf16[32,768]{1,0:T(8,128)(2,1)S(1)}, u32[]{:S(2)}, u32[]{:S(2)}) collective-permute-start(bf16[32,768]{1,0:T(8,128)(2,1)S(1)} %outside.8.refs_0_.refs_3_), channel_id=1, source_target_pairs={{0,448},{64,128},{128,64},{192,256},{256,192},{320,384},{384,320},... | collective-permute-start | bytes 147464 | tf_op jit(solution)/shard_map/ppermute | solution.py:164
  41.9 10.4 %collective-permute-start.3 = (bf16[32,768]{1,0:T(8,128)(2,1)S(1)}, bf16[32,768]{1,0:T(8,128)(2,1)S(1)}, u32[]{:S(2)}, u32[]{:S(2)}) collective-permute-start(bf16[32,768]{1,0:T(8,128)(2,1)S(1)} %outside.9.refs_0_.refs_3_), channel_id=1, source_target_pairs={{0,448},{64,128},{128,64},{192,256},{256,192},{320,384},{384,320},... | collective-permute-start | bytes 147464 | tf_op jit(solution)/shard_map/ppermute | solution.py:164
  52.6 9.6 %collective-permute-start.4 = (bf16[32,768]{1,0:T(8,128)(2,1)S(1)}, bf16[32,768]{1,0:T(8,128)(2,1)S(1)}, u32[]{:S(2)}, u32[]{:S(2)}) collective-permute-start(bf16[32,768]{1,0:T(8,128)(2,1)S(1)} %outside.10.refs_0_.refs_3_), channel_id=1, source_target_pairs={{0,448},{64,128},{128,64},{192,256},{256,192},{320,384},{384,320},... | collective-permute-start | bytes 147464 | tf_op jit(solution)/shard_map/ppermute | solution.py:164
  62.5 10.4 %collective-permute-start.5 = (bf16[32,768]{1,0:T(8,128)(2,1)S(1)}, bf16[32,768]{1,0:T(8,128)(2,1)S(1)}, u32[]{:S(2)}, u32[]{:S(2)}) collective-permute-start(bf16[32,768]{1,0:T(8,128)(2,1)S(1)} %outside.11.refs_0_.refs_3_), channel_id=1, source_target_pairs={{0,448},{64,128},{128,64},{192,256},{256,192},{320,384},{384,320},... | collective-permute-start | bytes 147464 | tf_op jit(solution)/shard_map/ppermute | solution.py:164
  73.3 9.6 %collective-permute-start.6 = (bf16[32,768]{1,0:T(8,128)(2,1)S(1)}, bf16[32,768]{1,0:T(8,128)(2,1)S(1)}, u32[]{:S(2)}, u32[]{:S(2)}) collective-permute-start(bf16[32,768]{1,0:T(8,128)(2,1)S(1)} %outside.12.refs_0_.refs_3_), channel_id=1, source_target_pairs={{0,448},{64,128},{128,64},{192,256},{256,192},{320,384},{384,320},... | collective-permute-start | bytes 147464 | tf_op jit(solution)/shard_map/ppermute | solution.py:164
  83.2 10.9 %collective-permute-start.7 = (bf16[32,768]{1,0:T(8,128)(2,1)S(1)}, bf16[32,768]{1,0:T(8,128)(2,1)S(1)}, u32[]{:S(2)}, u32[]{:S(2)}) collective-permute-start(bf16[32,768]{1,0:T(8,128)(2,1)S(1)} %outside.13.refs_0_.refs_3_), channel_id=1, source_target_pairs={{0,448},{64,128},{128,64},{192,256},{256,192},{320,384},{384,320},... | collective-permute-start | bytes 147464 | tf_op jit(solution)/shard_map/ppermute | solution.py:164
  94.1 16.7 %copy-start.6 = (s32[64]{0:T(128)S(1)}, s32[64]{0:T(128)}, u32[]{:S(2)}) copy-start(s32[64]{0:T(128)} %owner_rows.1) | copy-start | bytes 772
  94.4 9.6 %collective-permute-start.8 = (bf16[32,768]{1,0:T(8,128)(2,1)S(1)}, bf16[32,768]{1,0:T(8,128)(2,1)S(1)}, u32[]{:S(2)}, u32[]{:S(2)}) collective-permute-start(bf16[32,768]{1,0:T(8,128)(2,1)S(1)} %outside.14.refs_0_), channel_id=1, source_target_pairs={{0,448},{64,128},{128,64},{192,256},{256,192},{320,384},{384,320},... | collective-permute-start | bytes 147464 | tf_op jit(solution)/shard_map/ppermute | solution.py:164
Sparse Core Ops, SparseCore 0:
  19.4 82.5 all-gather.1

commit v6 on v5

--- a/solution.py
+++ b/solution.py
@@ -107,6 +107,10 @@
         first = first + counts[QUAD - 1]
         rows = turned[pl.ds(start, CAP_PAD), :]
         out_ref[z] = jnp.where(slot < count, rows, 0.0).astype(BF16)
+
+
+def emit_kernel(y_ref, out_ref):
+    out_ref[...] = y_ref[...]
 
 
 def join_kernel(low, own_ref, other_ref, out_ref):
@@ -222,6 +226,15 @@
         cost_estimate=COST,
         name="pick",
     )(owner_rows, quad, bands_quad)
+    filtered = pl.pallas_call(
+        emit_kernel,
+        out_shape=block_bf16,
+        in_specs=[VMEM],
+        out_specs=VMEM,
+        compiler_params=params(8),
+        cost_estimate=COST,
+        name="emit",
+    )(current)
     received = lax.all_to_all(sent, "z", split_axis=0, concat_axis=0, tiled=True)
     rotated = pl.pallas_call(
         rotate_kernel,
@@ -236,7 +249,7 @@
         compiler_params=params(58),
         name="rotate",
     )(received, rotation_all)
-    return current, rotated
+    return filtered, rotated
 
 
 def solution(mesh):

time: 154 us -> 155 us (level)
  blocking collectives: 74.4 us -> 44.1 us
  starting transfers between devices: 42.8 us -> 57.6 us
  waiting for transfers between devices: 0.52 us -> 15.2 us
    all_to_all x1 -> x0, blocking collectives: 30.1 us -> none  [per_device(): lax.all_to_all(sent, 'z', split_axis=0, concat_axis=0, tiled=True)]
    all_to_all x0 -> x1, starting transfers between devices: none -> 14.8 us  [per_device(): lax.all_to_all(sent, 'z', split_axis=0, concat_axis=0, tiled=True)]
    all_to_all x0 -> x1, waiting for transfers between devices: none -> 14.6 us  [per_device(): lax.all_to_all(sent, 'z', split_axis=0, concat_axis=0, tiled=True)]
    unnamed x14 -> x16, local copies, waits for them, and re-layouts: 5.47 us -> 6.13 us
  transfers between devices with their start and end apart: 10 -> 11, of which waited for: 2 -> 3; matrix products, arithmetic and copies ran while one was open for 0% -> 0% of each run, Pallas kernels for 7% -> 7%
where the time goes in v6:
time: 155 us; the launch traced here: 154 us
  starting transfers between devices  57.6 us (37%)
  blocking collectives  44.1 us (28%)
  Pallas kernels  17.2 us (11%)
  waiting for transfers between devices  15.2 us (10%)
  between operations  14.2 us (9%)
  local copies, waits for them, and re-layouts  6.13 us (4%)
    ppermute x8, starting transfers between devices, per_device(): from_far = lax.ppermute(current, 'elem', far)  39.3 us
    all_gather x8, blocking collectives, per_device(): lax.all_gather(current, 'elem', axis=0, tiled=True, axis_index_groups=near)  38.5 us
    all_to_all x1, starting transfers between devices, per_device(): lax.all_to_all(sent, 'z', split_axis=0, concat_axis=0, tiled=True)  14.8 us
    all_to_all x1, waiting for transfers between devices, per_device(): lax.all_to_all(sent, 'z', split_axis=0, concat_axis=0, tiled=True)  14.6 us
    unnamed x16, local copies, waits for them, and re-layouts  6.13 us
    all_gather x1, blocking collectives, per_device(): bands_quad = lax.all_gather(current, ('yl', 'c'), axis=0, tiled=True)  5.59 us
    pallas_call x1, Pallas kernels, per_device(): pl.pallas_call(rotate_kernel, out_shape=jax.ShapeDtypeStruct((CAP, rotati...  5.44 us
    pallas_call x8, Pallas kernels, per_device(): pl.pallas_call(lambda *refs, scale=scale, has_prev=bool(previous): inside...  3.99 us
  transfers between devices with their start and end apart: 11, of which 3 were waited for; matrix products, arithmetic and copies ran while one was open for 0% of the time, Pallas kernels for 7%

profile of v6, /device:TPU:32, one launch (start us, length us, event | category | flops | bytes accessed | tf_op | source)
XLA Modules:
  0.0 154.4 jit_solution(11226736067555866169)
XLA Ops:
  7.2 3.5 %collective-permute-start = (bf16[32,2048]{1,0:T(8,128)(2,1)}, bf16[32,2048]{1,0:T(8,128)(2,1)S(1)}, u32[]{:S(2)}, u32[]{:S(2)}) collective-permute-start(bf16[32,2048]{1,0:T(8,128)(2,1)} %bitcast.5), channel_id=1, source_target_pairs={{0,2},{2,0},{1,3},{3,1},{4,6},{6,4},{5,7},{7,5},{8,10},{10,8},{9,1... | collective-permute-start | bytes 393224 | tf_op jit(solution)/shard_map/ppermute | solution.py:171
  10.7 0.6 copy-done.2
  11.4 0.8 copy-done.5
  12.2 0.7 mask.1.refs_0_.refs_3_
  12.9 4.7 %all_gather.30.refs_1_ = bf16[64,768]{1,0:T(8,128)(2,1)S(1)} all-gather(bf16[32,768]{1,0:T(8,128)(2,1)S(1)} %mask.1.refs_0_.refs_3_), channel_id=1, replica_groups={{0,64},{128,192},{256,320},{384,448},{1,65},{129,193},{257,321},{385,44..., dimensions={0}, use_global_device_ids=true | all-gather | bytes 147456 | tf_op jit(solution)/shard_map/all_gather | solution.py:169
  17.6 0.9 copy-done.4
  18.5 0.7 join.1
  19.3 7.0 %collective-permute-start.1 = (bf16[32,768]{1,0:T(8,128)(2,1)S(1)}, bf16[32,768]{1,0:T(8,128)(2,1)S(1)}, u32[]{:S(2)}, u32[]{:S(2)}) collective-permute-start(bf16[32,768]{1,0:T(8,128)(2,1)S(1)} %mask.1.refs_0_.refs_3_), channel_id=1, source_target_pairs={{0,448},{64,128},{128,64},{192,256},{256,192},{320,384},{384,320},... | collective-permute-start | bytes 147464 | tf_op jit(solution)/shard_map/ppermute | solution.py:168
  26.3 1.8 %copy-done = bf16[4,7,192,192]{3,2,1,0:T(8,128)(2,1)S(1)} copy-done((bf16[4,7,192,192]{3,2,1,0:T(8,128)(2,1)S(1)}, bf16[4,7,192,192]{3,2,1,0:T(8,128)(2,1)}, u32[]{:S(2)}) %copy-start) | copy-done | bytes 2064408
  28.1 0.7 copy-done.1
  28.8 0.7 copy-done.3
  29.4 1.7 %couple.1 = (bf16[1536,768]{1,0:T(8,128)(2,1)S(1)}, bf16[768,768]{1,0:T(8,128)(2,1)S(1)}) custom-call(s32[4,6]{1,0:T(4,128)S(1)} %copy-done.1, s32[4]{0:T(128)S(1)} %copy-done.3, s32[1]{0:T(128)} %bitcast.2.parity, bf16[4,7,192,192]{3,2,1,0:T(8,128)(2,1)S(1)} %copy-done), custom_call_target="tpu_custom_call" | custom-call | tf_op jit(solution)/shard_map/couple/pallas_call | solution.py:184
  31.1 0.5 inside.8.refs_0_
  31.7 0.3 outside.8.refs_0_.refs_3_
  32.0 4.2 %collective-permute-start.2 = (bf16[32,768]{1,0:T(8,128)(2,1)S(1)}, bf16[32,768]{1,0:T(8,128)(2,1)S(1)}, u32[]{:S(2)}, u32[]{:S(2)}) collective-permute-start(bf16[32,768]{1,0:T(8,128)(2,1)S(1)} %outside.8.refs_0_.refs_3_), channel_id=1, source_target_pairs={{0,448},{64,128},{128,64},{192,256},{256,192},{320,384},{384,320},... | collective-permute-start | bytes 147464 | tf_op jit(solution)/shard_map/ppermute | solution.py:168
  36.2 4.8 %all_gather.31.refs_1_ = bf16[64,768]{1,0:T(8,128)(2,1)S(1)} all-gather(bf16[32,768]{1,0:T(8,128)(2,1)S(1)} %outside.8.refs_0_.refs_3_), channel_id=1, replica_groups={{0,64},{128,192},{256,320},{384,448},{1,65},{129,193},{257,321},{385,44..., dimensions={0}, use_global_device_ids=true | all-gather | bytes 147456 | tf_op jit(solution)/shard_map/all_gather | solution.py:169
  41.0 0.5 inside.9.refs_0_
  41.6 0.3 outside.9.refs_0_.refs_3_
  41.9 5.1 %collective-permute-start.3 = (bf16[32,768]{1,0:T(8,128)(2,1)S(1)}, bf16[32,768]{1,0:T(8,128)(2,1)S(1)}, u32[]{:S(2)}, u32[]{:S(2)}) collective-permute-start(bf16[32,768]{1,0:T(8,128)(2,1)S(1)} %outside.9.refs_0_.refs_3_), channel_id=1, source_target_pairs={{0,448},{64,128},{128,64},{192,256},{256,192},{320,384},{384,320},... | collective-permute-start | bytes 147464 | tf_op jit(solution)/shard_map/ppermute | solution.py:168
  47.1 4.8 %all_gather.32.refs_1_ = bf16[64,768]{1,0:T(8,128)(2,1)S(1)} all-gather(bf16[32,768]{1,0:T(8,128)(2,1)S(1)} %outside.9.refs_0_.refs_3_), channel_id=1, replica_groups={{0,64},{128,192},{256,320},{384,448},{1,65},{129,193},{257,321},{385,44..., dimensions={0}, use_global_device_ids=true | all-gather | bytes 147456 | tf_op jit(solution)/shard_map/all_gather | solution.py:169
  51.8 0.5 inside.10.refs_0_
  52.3 0.3 outside.10.refs_0_.refs_3_
  52.7 4.3 %collective-permute-start.4 = (bf16[32,768]{1,0:T(8,128)(2,1)S(1)}, bf16[32,768]{1,0:T(8,128)(2,1)S(1)}, u32[]{:S(2)}, u32[]{:S(2)}) collective-permute-start(bf16[32,768]{1,0:T(8,128)(2,1)S(1)} %outside.10.refs_0_.refs_3_), channel_id=1, source_target_pairs={{0,448},{64,128},{128,64},{192,256},{256,192},{320,384},{384,320},... | collective-permute-start | bytes 147464 | tf_op jit(solution)/shard_map/ppermute | solution.py:168
  57.0 4.8 %all_gather.33.refs_1_ = bf16[64,768]{1,0:T(8,128)(2,1)S(1)} all-gather(bf16[32,768]{1,0:T(8,128)(2,1)S(1)} %outside.10.refs_0_.refs_3_), channel_id=1, replica_groups={{0,64},{128,192},{256,320},{384,448},{1,65},{129,193},{257,321},{385,44..., dimensions={0}, use_global_device_ids=true | all-gather | bytes 147456 | tf_op jit(solution)/shard_map/all_gather | solution.py:169
  61.7 0.5 inside.11.refs_0_
  62.3 0.3 outside.11.refs_0_.refs_3_
  62.6 5.1 %collective-permute-start.5 = (bf16[32,768]{1,0:T(8,128)(2,1)S(1)}, bf16[32,768]{1,0:T(8,128)(2,1)S(1)}, u32[]{:S(2)}, u32[]{:S(2)}) collective-permute-start(bf16[32,768]{1,0:T(8,128)(2,1)S(1)} %outside.11.refs_0_.refs_3_), channel_id=1, source_target_pairs={{0,448},{64,128},{128,64},{192,256},{256,192},{320,384},{384,320},... | collective-permute-start | bytes 147464 | tf_op jit(solution)/shard_map/ppermute | solution.py:168
  67.7 4.8 %all_gather.34.refs_1_ = bf16[64,768]{1,0:T(8,128)(2,1)S(1)} all-gather(bf16[32,768]{1,0:T(8,128)(2,1)S(1)} %outside.11.refs_0_.refs_3_), channel_id=1, replica_groups={{0,64},{128,192},{256,320},{384,448},{1,65},{129,193},{257,321},{385,44..., dimensions={0}, use_global_device_ids=true | all-gather | bytes 147456 | tf_op jit(solution)/shard_map/all_gather | solution.py:169
  72.5 0.5 inside.12.refs_0_
  73.0 0.3 outside.12.refs_0_.refs_3_
  73.4 4.3 %collective-permute-start.6 = (bf16[32,768]{1,0:T(8,128)(2,1)S(1)}, bf16[32,768]{1,0:T(8,128)(2,1)S(1)}, u32[]{:S(2)}, u32[]{:S(2)}) collective-permute-start(bf16[32,768]{1,0:T(8,128)(2,1)S(1)} %outside.12.refs_0_.refs_3_), channel_id=1, source_target_pairs={{0,448},{64,128},{128,64},{192,256},{256,192},{320,384},{384,320},... | collective-permute-start | bytes 147464 | tf_op jit(solution)/shard_map/ppermute | solution.py:168
  77.7 4.8 %all_gather.35.refs_1_ = bf16[64,768]{1,0:T(8,128)(2,1)S(1)} all-gather(bf16[32,768]{1,0:T(8,128)(2,1)S(1)} %outside.12.refs_0_.refs_3_), channel_id=1, replica_groups={{0,64},{128,192},{256,320},{384,448},{1,65},{129,193},{257,321},{385,44..., dimensions={0}, use_global_device_ids=true | all-gather | bytes 147456 | tf_op jit(solution)/shard_map/all_gather | solution.py:169
  82.4 0.5 inside.13.refs_0_
  82.9 0.3 outside.13.refs_0_.refs_3_
  83.3 5.1 %collective-permute-start.7 = (bf16[32,768]{1,0:T(8,128)(2,1)S(1)}, bf16[32,768]{1,0:T(8,128)(2,1)S(1)}, u32[]{:S(2)}, u32[]{:S(2)}) collective-permute-start(bf16[32,768]{1,0:T(8,128)(2,1)S(1)} %outside.13.refs_0_.refs_3_), channel_id=1, source_target_pairs={{0,448},{64,128},{128,64},{192,256},{256,192},{320,384},{384,320},... | collective-permute-start | bytes 147464 | tf_op jit(solution)/shard_map/ppermute | solution.py:168
  88.4 5.2 %all_gather.36.refs_1_ = bf16[64,768]{1,0:T(8,128)(2,1)S(1)} all-gather(bf16[32,768]{1,0:T(8,128)(2,1)S(1)} %outside.13.refs_0_.refs_3_), channel_id=1, replica_groups={{0,64},{128,192},{256,320},{384,448},{1,65},{129,193},{257,321},{385,44..., dimensions={0}, use_global_device_ids=true | all-gather | bytes 147456 | tf_op jit(solution)/shard_map/all_gather | solution.py:169
  93.6 0.5 inside.14.refs_0_
  94.2 0.3 outside.14.refs_0_
  94.5 4.0 %collective-permute-start.8 = (bf16[32,768]{1,0:T(8,128)(2,1)S(1)}, bf16[32,768]{1,0:T(8,128)(2,1)S(1)}, u32[]{:S(2)}, u32[]{:S(2)}) collective-permute-start(bf16[32,768]{1,0:T(8,128)(2,1)S(1)} %outside.14.refs_0_), channel_id=1, source_target_pairs={{0,448},{64,128},{128,64},{192,256},{256,192},{320,384},{384,320},... | collective-permute-start | bytes 147464 | tf_op jit(solution)/shard_map/ppermute | solution.py:168
  98.5 4.8 %all_gather.37.refs_1_ = bf16[64,768]{1,0:T(8,128)(2,1)S(1)} all-gather(bf16[32,768]{1,0:T(8,128)(2,1)S(1)} %outside.14.refs_0_), channel_id=1, replica_groups={{0,64},{128,192},{256,320},{384,448},{1,65},{129,193},{257,321},{385,44..., dimensions={0}, use_global_device_ids=true | all-gather | bytes 147456 | tf_op jit(solution)/shard_map/all_gather | solution.py:169
  103.3 0.5 inside.15.refs_0_
  104.4 5.6 %all_gather.38.y_ref = bf16[128,768]{1,0:T(8,128)(2,1)S(1)} all-gather(bf16[32,768]{1,0:T(8,128)(2,1)S(1)} %outside.15.y_ref), channel_id=1, replica_groups=mesh['elem'=8,'z'=16,'yl'=2,'c'=2] {'yl','c'}, dimensions={0}, use_global_device_ids=true | all-gather | bytes 245760 | tf_op jit(solution)/shard_map/all_gather | solution.py:218
  110.0 1.4 pick.1
  111.4 14.8 %all-to-all-start = ((bf16[16,40,128]{2,1,0:T(8,128)(2,1)}), bf16[16,40,128]{2,1,0:T(8,128)(2,1)S(1)}, u32[]{:S(2)}, u32[]{:S(2)}) async-start(bf16[16,40,128]{2,1,0:T(8,128)(2,1)} %pick.1), calls=%async_computation | async-start | bytes 327680 | tf_op jit(solution)/shard_map/all_to_all | solution.py:238
  126.2 0.6 emit.1
  126.8 14.6 %all-to-all-done.x_ref = bf16[16,40,128]{2,1,0:T(8,128)(2,1)S(1)} async-done(((bf16[16,40,128]{2,1,0:T(8,128)(2,1)}), bf16[16,40,128]{2,1,0:T(8,128)(2,1)S(1)}, u32[]{:S(2)}, u32[]{:S(2)}) %all-to-all-start) | async-done | bytes 163872 | tf_op jit(solution)/shard_map/all_to_all | solution.py:238
  141.5 0.7 copy-done.7
  142.1 5.4 %rotate.1 = bf16[36,2048]{1,0:T(8,128)(2,1)} custom-call(bf16[16,40,128]{2,1,0:T(8,128)(2,1)} %copy-done.7, bf16[2048,2048]{1,0:T(8,128)(2,1)} %all-gather.2.cloned.1.call-done.r_ref), custom_call_target="tpu_custom_call" | custom-call | tf_op jit(solution)/shard_map/rotate/pallas_call | solution.py:239
  (23 shorter events, 0.9 us)
Async XLA Ops:
  7.2 134.3 %all-gather.2.cloned.1.call-start = ((), (), s32[]{:S(2)}) async-start(), calls=%async_computation.1 | async-start | bytes 8650752 | tf_op jit(solution)/shard_map/all_gather | solution.py:183
  7.2 10.4 %collective-permute-start = (bf16[32,2048]{1,0:T(8,128)(2,1)}, bf16[32,2048]{1,0:T(8,128)(2,1)S(1)}, u32[]{:S(2)}, u32[]{:S(2)}) collective-permute-start(bf16[32,2048]{1,0:T(8,128)(2,1)} %bitcast.5), channel_id=1, source_target_pairs={{0,2},{2,0},{1,3},{3,1},{4,6},{6,4},{5,7},{7,5},{8,10},{10,8},{9,1... | collective-permute-start | bytes 393224 | tf_op jit(solution)/shard_map/ppermute | solution.py:171
  10.7 0.7 copy-start.2
  11.4 0.8 copy-start.5
  17.6 0.9 copy-start.4
  19.3 12.4 %collective-permute-start.1 = (bf16[32,768]{1,0:T(8,128)(2,1)S(1)}, bf16[32,768]{1,0:T(8,128)(2,1)S(1)}, u32[]{:S(2)}, u32[]{:S(2)}) collective-permute-start(bf16[32,768]{1,0:T(8,128)(2,1)S(1)} %mask.1.refs_0_.refs_3_), channel_id=1, source_target_pairs={{0,448},{64,128},{128,64},{192,256},{256,192},{320,384},{384,320},... | collective-permute-start | bytes 147464 | tf_op jit(solution)/shard_map/ppermute | solution.py:168
  26.3 1.8 %copy-start = (bf16[4,7,192,192]{3,2,1,0:T(8,128)(2,1)S(1)}, bf16[4,7,192,192]{3,2,1,0:T(8,128)(2,1)}, u32[]{:S(2)}) copy-start(bf16[4,7,192,192]{3,2,1,0:T(8,128)(2,1)} %h_ref.1) | copy-start | bytes 6193156
  28.1 0.7 copy-start.1
  28.8 0.7 copy-start.3
  32.0 9.6 %collective-permute-start.2 = (bf16[32,768]{1,0:T(8,128)(2,1)S(1)}, bf16[32,768]{1,0:T(8,128)(2,1)S(1)}, u32[]{:S(2)}, u32[]{:S(2)}) collective-permute-start(bf16[32,768]{1,0:T(8,128)(2,1)S(1)} %outside.8.refs_0_.refs_3_), channel_id=1, source_target_pairs={{0,448},{64,128},{128,64},{192,256},{256,192},{320,384},{384,320},... | collective-permute-start | bytes 147464 | tf_op jit(solution)/shard_map/ppermute | solution.py:168
  41.9 10.4 %collective-permute-start.3 = (bf16[32,768]{1,0:T(8,128)(2,1)S(1)}, bf16[32,768]{1,0:T(8,128)(2,1)S(1)}, u32[]{:S(2)}, u32[]{:S(2)}) collective-permute-start(bf16[32,768]{1,0:T(8,128)(2,1)S(1)} %outside.9.refs_0_.refs_3_), channel_id=1, source_target_pairs={{0,448},{64,128},{128,64},{192,256},{256,192},{320,384},{384,320},... | collective-permute-start | bytes 147464 | tf_op jit(solution)/shard_map/ppermute | solution.py:168
  52.7 9.6 %collective-permute-start.4 = (bf16[32,768]{1,0:T(8,128)(2,1)S(1)}, bf16[32,768]{1,0:T(8,128)(2,1)S(1)}, u32[]{:S(2)}, u32[]{:S(2)}) collective-permute-start(bf16[32,768]{1,0:T(8,128)(2,1)S(1)} %outside.10.refs_0_.refs_3_), channel_id=1, source_target_pairs={{0,448},{64,128},{128,64},{192,256},{256,192},{320,384},{384,320},... | collective-permute-start | bytes 147464 | tf_op jit(solution)/shard_map/ppermute | solution.py:168
  62.6 10.4 %collective-permute-start.5 = (bf16[32,768]{1,0:T(8,128)(2,1)S(1)}, bf16[32,768]{1,0:T(8,128)(2,1)S(1)}, u32[]{:S(2)}, u32[]{:S(2)}) collective-permute-start(bf16[32,768]{1,0:T(8,128)(2,1)S(1)} %outside.11.refs_0_.refs_3_), channel_id=1, source_target_pairs={{0,448},{64,128},{128,64},{192,256},{256,192},{320,384},{384,320},... | collective-permute-start | bytes 147464 | tf_op jit(solution)/shard_map/ppermute | solution.py:168
  73.4 9.6 %collective-permute-start.6 = (bf16[32,768]{1,0:T(8,128)(2,1)S(1)}, bf16[32,768]{1,0:T(8,128)(2,1)S(1)}, u32[]{:S(2)}, u32[]{:S(2)}) collective-permute-start(bf16[32,768]{1,0:T(8,128)(2,1)S(1)} %outside.12.refs_0_.refs_3_), channel_id=1, source_target_pairs={{0,448},{64,128},{128,64},{192,256},{256,192},{320,384},{384,320},... | collective-permute-start | bytes 147464 | tf_op jit(solution)/shard_map/ppermute | solution.py:168
  83.3 10.9 %collective-permute-start.7 = (bf16[32,768]{1,0:T(8,128)(2,1)S(1)}, bf16[32,768]{1,0:T(8,128)(2,1)S(1)}, u32[]{:S(2)}, u32[]{:S(2)}) collective-permute-start(bf16[32,768]{1,0:T(8,128)(2,1)S(1)} %outside.13.refs_0_.refs_3_), channel_id=1, source_target_pairs={{0,448},{64,128},{128,64},{192,256},{256,192},{320,384},{384,320},... | collective-permute-start | bytes 147464 | tf_op jit(solution)/shard_map/ppermute | solution.py:168
  94.1 15.9 %copy-start.6 = (s32[64]{0:T(128)S(1)}, s32[64]{0:T(128)}, u32[]{:S(2)}) copy-start(s32[64]{0:T(128)} %owner_rows.1) | copy-start | bytes 772
  94.5 9.6 %collective-permute-start.8 = (bf16[32,768]{1,0:T(8,128)(2,1)S(1)}, bf16[32,768]{1,0:T(8,128)(2,1)S(1)}, u32[]{:S(2)}, u32[]{:S(2)}) collective-permute-start(bf16[32,768]{1,0:T(8,128)(2,1)S(1)} %outside.14.refs_0_), channel_id=1, source_target_pairs={{0,448},{64,128},{128,64},{192,256},{256,192},{320,384},{384,320},... | collective-permute-start | bytes 147464 | tf_op jit(solution)/shard_map/ppermute | solution.py:168
  111.4 30.1 %all-to-all-start = ((bf16[16,40,128]{2,1,0:T(8,128)(2,1)}), bf16[16,40,128]{2,1,0:T(8,128)(2,1)S(1)}, u32[]{:S(2)}, u32[]{:S(2)}) async-start(bf16[16,40,128]{2,1,0:T(8,128)(2,1)} %pick.1), calls=%async_computation | async-start | bytes 327680 | tf_op jit(solution)/shard_map/all_to_all | solution.py:238
  141.5 0.7 copy-start.7
Sparse Core Ops, SparseCore 0:
  19.4 82.5 all-gather.1

commit v7 on v5

--- a/solution.py
+++ b/solution.py
@@ -24,6 +24,11 @@
 COST = pl.CostEstimate(flops=3 * 10**8, bytes_accessed=3 << 20, transcendentals=0)
 VMEM = pl.BlockSpec(memory_space=pltpu.VMEM)
 SMEM = pl.BlockSpec(memory_space=pltpu.SMEM)
+HBM = pl.BlockSpec(memory_space=pltpu.HBM)
+
+
+def in_hbm(value):
+    return pltpu.with_memory_space_constraint(value, pltpu.HBM)
 
 
 def params(mib):
@@ -38,21 +43,41 @@
     return lax.broadcasted_iota(jnp.int32, (rows, NB), 1) < count
 
 
-def mask_kernel(counts, start_ref, y_ref):
+def mask_kernel(counts_hbm, start_hbm, y_ref, counts, start, sems):
+    small = pltpu.make_async_copy(counts_hbm, counts, sems.at[0])
+    large = pltpu.make_async_copy(start_hbm, start, sems.at[1])
+    small.start()
+    large.start()
+    small.wait()
+    large.wait()
     for i in range(ELEMS_DEV):
-        block = start_ref[:, lanes(i)]
+        block = start[:, lanes(i)]
         y_ref[:, lanes(i)] = jnp.where(
             column_mask(counts[i], BANDS_DEV), block, jnp.zeros_like(block)
         )
 
 
-def couple_kernel(neighbours, counts, parity, h_ref, inner_ref, outer_ref, column):
+def couple_kernel(
+    neighbours_hbm, counts_hbm, parity, h_hbm, inner_ref, outer_ref, column, h_ref, neighbours, counts, sems
+):
+    copies = [
+        pltpu.make_async_copy(h_hbm.at[i], h_ref.at[i], sems.at[i]) for i in range(ELEMS_DEV)
+    ]
+    tables = [
+        pltpu.make_async_copy(neighbours_hbm, neighbours, sems.at[ELEMS_DEV]),
+        pltpu.make_async_copy(counts_hbm, counts, sems.at[ELEMS_DEV + 1]),
+    ]
+    for copy in tables + copies:
+        copy.start()
     inner_ref[ROWS:, :] = jnp.zeros((ROWS, ROWS), BF16)
     outer_ref[...] = jnp.zeros_like(outer_ref)
+    for copy in tables:
+        copy.wait()
     slot_near = 6 - parity[0]
     slot_far = 5 + parity[0]
     for i in range(ELEMS_DEV):
         keep = column_mask(counts[i], NB)
+        copies[i].wait()
 
         def block(slot, i=i, keep=keep):
             value = h_ref[i, slot]
@@ -109,10 +134,13 @@
         out_ref[z] = jnp.where(slot < count, rows, 0.0).astype(BF16)
 
 
-def join_kernel(low, own_ref, other_ref, out_ref):
-    half = own_ref.shape[0]
-    out_ref[pl.ds(pl.multiple_of(half * low[0], half), half), :] = own_ref[...]
+def join_kernel(low, own_hbm, other_ref, out_ref, own, sem):
+    copy = pltpu.make_async_copy(own_hbm, own, sem)
+    copy.start()
+    half = other_ref.shape[0]
     out_ref[pl.ds(pl.multiple_of(half * (1 - low[0]), half), half), :] = other_ref[...]
+    copy.wait()
+    out_ref[pl.ds(pl.multiple_of(half * low[0], half), half), :] = own[...]
 
 
 def rotate_kernel(x_ref, r_ref, out_ref, gathered):
@@ -151,12 +179,17 @@
     current = pl.pallas_call(
         mask_kernel,
         out_shape=block_bf16,
-        in_specs=[SMEM, VMEM],
+        in_specs=[HBM, HBM],
         out_specs=VMEM,
+        scratch_shapes=[
+            pltpu.SMEM(basis_count.shape, jnp.int32),
+            pltpu.VMEM(start_bands.shape, BF16),
+            pltpu.SemaphoreType.DMA((2,)),
+        ],
         compiler_params=params(8),
         cost_estimate=COST,
         name="mask",
-    )(basis_count, start_bands)
+    )(in_hbm(basis_count), in_hbm(start_bands))
     earlier = None
     for step in range(DEGREE):
         scale = 0.5 if step == 0 else 1.0
@@ -169,12 +202,13 @@
             pieces = pl.pallas_call(
                 join_kernel,
                 out_shape=jax.ShapeDtypeStruct((2 * BANDS_DEV, columns.shape[1]), BF16),
-                in_specs=[SMEM, VMEM, VMEM],
+                in_specs=[SMEM, HBM, VMEM],
                 out_specs=VMEM,
+                scratch_shapes=[pltpu.VMEM(columns.shape, BF16), pltpu.SemaphoreType.DMA],
                 compiler_params=params(8),
                 cost_estimate=COST,
                 name="join",
-            )(low, columns, other_columns)
+            )(low, in_hbm(columns), other_columns)
             pieces, parity, second, quad = lax.optimization_barrier((pieces, parity, second, quad))
             rotation_all = lax.all_gather(pieces, ("z", "c"), axis=0, tiled=True)
             w_inner, w_outer = pl.pallas_call(
@@ -183,12 +217,18 @@
                     jax.ShapeDtypeStruct((2 * ROWS, ROWS), BF16),
                     jax.ShapeDtypeStruct((ROWS, ROWS), BF16),
                 ),
-                in_specs=[SMEM, SMEM, SMEM, VMEM],
+                in_specs=[HBM, HBM, SMEM, HBM],
                 out_specs=(VMEM, VMEM),
-                scratch_shapes=[pltpu.VMEM((ROWS, NB), F32)],
+                scratch_shapes=[
+                pltpu.VMEM((ROWS, NB), F32),
+                pltpu.VMEM(hamiltonian.shape, BF16),
+                pltpu.SMEM(neighbours.shape, jnp.int32),
+                pltpu.SMEM(basis_count.shape, jnp.int32),
+                pltpu.SemaphoreType.DMA((ELEMS_DEV + 2,)),
+            ],
                 compiler_params=params(12),
                 name="couple",
-            )(neighbours, basis_count, parity, hamiltonian)
+            )(in_hbm(neighbours), in_hbm(basis_count), parity, in_hbm(hamiltonian))
         partial = pl.pallas_call(
             lambda *refs, scale=scale, has_prev=bool(previous): inside_kernel(
                 scale, has_prev, *refs
@@ -233,9 +273,9 @@
         ],
         out_specs=pl.BlockSpec((CAP, TILE), lambda n: (0, n)),
         scratch_shapes=[pltpu.VMEM((CAP_PAD, rotation_all.shape[1]), BF16)],
-        compiler_params=params(58),
+        compiler_params=params(24),
         name="rotate",
-    )(received, rotation_all)
+    )(received, in_hbm(rotation_all))
     return current, rotated
 
 

time: 154 us -> 153 us (level)
  local copies, waits for them, and re-layouts: 5.47 us -> 0.01 us
  starting transfers between devices: 42.8 us -> 45.4 us
  Pallas kernels: 16.5 us -> 18.2 us
    unnamed x14 -> x2, local copies, waits for them, and re-layouts: 5.47 us -> 0.01 us
    ppermute x8, starting transfers between devices: 39.3 us -> 41.9 us  [per_device(): from_far = lax.ppermute(current, 'elem', far)]
  transfers between devices with their start and end apart: 10 -> 10, of which waited for: 2 -> 0; matrix products, arithmetic and copies ran while one was open for 0% -> 0% of each run, Pallas kernels for 7% -> 7%
where the time goes in v7:
time: 153 us
  blocking collectives  74.5 us (49%)
  starting transfers between devices  45.4 us (30%)
  Pallas kernels  18.2 us (12%)
  between operations  14.2 us (9%)
    ppermute x8, starting transfers between devices, per_device(): from_far = lax.ppermute(current, 'elem', far)  41.9 us
    all_gather x8, blocking collectives, per_device(): lax.all_gather(current, 'elem', axis=0, tiled=True, axis_index_groups=near)  38.4 us
    all_to_all x1, blocking collectives, per_device(): lax.all_to_all(sent, 'z', split_axis=0, concat_axis=0, tiled=True)  30.3 us
    all_gather x1, blocking collectives, per_device(): bands_quad = lax.all_gather(current, ('yl', 'c'), axis=0, tiled=True)  5.79 us
    pallas_call x1, Pallas kernels, per_device(): pl.pallas_call(rotate_kernel, out_shape=jax.ShapeDtypeStruct((CAP, rotati...  5.41 us
    pallas_call x8, Pallas kernels, per_device(): pl.pallas_call(lambda *refs, scale=scale, has_prev=bool(previous): inside...  3.96 us
    ppermute x1, starting transfers between devices, per_device(): other_columns = lax.ppermute(columns, 'yl', [(0, 1), (1, 0)])  3.49 us
    pallas_call x8, Pallas kernels, per_device(): pl.pallas_call(lambda *refs, scale=scale: outside_kernel(scale, *refs), o...  3.24 us
  transfers between devices with their start and end apart: 10, of which 0 were waited for; matrix products, arithmetic and copies ran while one was open for 0% of the time, Pallas kernels for 7%

profile of v7, /device:TPU:32, one launch (start us, length us, event | category | flops | bytes accessed | tf_op | source)
XLA Modules:
  0.0 152.5 jit_solution(13539072994949735230)
XLA Ops:
  7.2 0.0 all-gather.2.cloned.1.call-start
  7.2 3.5 %collective-permute-start = (bf16[32,2048]{1,0:T(8,128)(2,1)}, bf16[32,2048]{1,0:T(8,128)(2,1)S(1)}, u32[]{:S(2)}, u32[]{:S(2)}) collective-permute-start(bf16[32,2048]{1,0:T(8,128)(2,1)} %bitcast.5), channel_id=1, source_target_pairs={{0,2},{2,0},{1,3},{3,1},{4,6},{6,4},{5,7},{7,5},{8,10},{10,8},{9,1... | collective-permute-start | bytes 393224 | tf_op jit(solution)/shard_map/ppermute | solution.py:200
  10.7 1.0 mask.1.refs_0_.refs_3_
  11.7 4.8 %all_gather.30.refs_1_ = bf16[64,768]{1,0:T(8,128)(2,1)S(1)} all-gather(bf16[32,768]{1,0:T(8,128)(2,1)S(1)} %mask.1.refs_0_.refs_3_), channel_id=1, replica_groups={{0,64},{128,192},{256,320},{384,448},{1,65},{129,193},{257,321},{385,44..., dimensions={0}, use_global_device_ids=true | all-gather | bytes 147456 | tf_op jit(solution)/shard_map/all_gather | solution.py:198
  16.5 1.7 %join.1 = bf16[64,2048]{1,0:T(8,128)(2,1)} custom-call(s32[1]{0:T(128)} %bitcast.1.low, bf16[32,2048]{1,0:T(8,128)(2,1)} %bitcast.6, bf16[32,2048]{1,0:T(8,128)(2,1)S(1)} %collective-permute-done.other_ref), custom_call_target="tpu_custom_call" | custom-call | flops 300000000 | bytes 3145728 | tf_op jit(solution)/shard_map/join/pallas_call | solution.py:202
  18.1 0.0 all-gather.2.cloned.1.call-update
  18.2 7.0 %collective-permute-start.1 = (bf16[32,768]{1,0:T(8,128)(2,1)S(1)}, bf16[32,768]{1,0:T(8,128)(2,1)S(1)}, u32[]{:S(2)}, u32[]{:S(2)}) collective-permute-start(bf16[32,768]{1,0:T(8,128)(2,1)S(1)} %mask.1.refs_0_.refs_3_), channel_id=1, source_target_pairs={{0,448},{64,128},{128,64},{192,256},{256,192},{320,384},{384,320},... | collective-permute-start | bytes 147464 | tf_op jit(solution)/shard_map/ppermute | solution.py:197
  25.2 2.2 %couple.1 = (bf16[1536,768]{1,0:T(8,128)(2,1)S(1)}, bf16[768,768]{1,0:T(8,128)(2,1)S(1)}) custom-call(s32[4,6]{1,0:T(4,128)} %neighbours_hbm.1, s32[4]{0:T(128)} %counts_hbm.3, s32[1]{0:T(128)} %bitcast.2.parity, bf16[4,7,192,192]{3,2,1,0:T(8,128)(2,1)} %h_hbm.1), custom_call_target="tpu_custom_call" | custom-call | tf_op jit(solution)/shard_map/couple/pallas_call | solution.py:214
  27.4 0.5 inside.8.refs_0_
  27.9 0.0 collective-permute-done.1.refs_1_
  27.9 0.3 outside.8.refs_0_.refs_3_
  28.3 6.8 %collective-permute-start.2 = (bf16[32,768]{1,0:T(8,128)(2,1)S(1)}, bf16[32,768]{1,0:T(8,128)(2,1)S(1)}, u32[]{:S(2)}, u32[]{:S(2)}) collective-permute-start(bf16[32,768]{1,0:T(8,128)(2,1)S(1)} %outside.8.refs_0_.refs_3_), channel_id=1, source_target_pairs={{0,448},{64,128},{128,64},{192,256},{256,192},{320,384},{384,320},... | collective-permute-start | bytes 147464 | tf_op jit(solution)/shard_map/ppermute | solution.py:197
  35.1 4.8 %all_gather.31.refs_1_ = bf16[64,768]{1,0:T(8,128)(2,1)S(1)} all-gather(bf16[32,768]{1,0:T(8,128)(2,1)S(1)} %outside.8.refs_0_.refs_3_), channel_id=1, replica_groups={{0,64},{128,192},{256,320},{384,448},{1,65},{129,193},{257,321},{385,44..., dimensions={0}, use_global_device_ids=true | all-gather | bytes 147456 | tf_op jit(solution)/shard_map/all_gather | solution.py:198
  39.8 0.5 inside.9.refs_0_
  40.3 0.0 collective-permute-done.2.refs_1_
  40.4 0.3 outside.9.refs_0_.refs_3_
  40.7 4.3 %collective-permute-start.3 = (bf16[32,768]{1,0:T(8,128)(2,1)S(1)}, bf16[32,768]{1,0:T(8,128)(2,1)S(1)}, u32[]{:S(2)}, u32[]{:S(2)}) collective-permute-start(bf16[32,768]{1,0:T(8,128)(2,1)S(1)} %outside.9.refs_0_.refs_3_), channel_id=1, source_target_pairs={{0,448},{64,128},{128,64},{192,256},{256,192},{320,384},{384,320},... | collective-permute-start | bytes 147464 | tf_op jit(solution)/shard_map/ppermute | solution.py:197
  45.0 4.8 %all_gather.32.refs_1_ = bf16[64,768]{1,0:T(8,128)(2,1)S(1)} all-gather(bf16[32,768]{1,0:T(8,128)(2,1)S(1)} %outside.9.refs_0_.refs_3_), channel_id=1, replica_groups={{0,64},{128,192},{256,320},{384,448},{1,65},{129,193},{257,321},{385,44..., dimensions={0}, use_global_device_ids=true | all-gather | bytes 147456 | tf_op jit(solution)/shard_map/all_gather | solution.py:198
  49.8 0.5 inside.10.refs_0_
  50.3 0.0 collective-permute-done.3.refs_1_
  50.3 0.3 outside.10.refs_0_.refs_3_
  50.6 5.1 %collective-permute-start.4 = (bf16[32,768]{1,0:T(8,128)(2,1)S(1)}, bf16[32,768]{1,0:T(8,128)(2,1)S(1)}, u32[]{:S(2)}, u32[]{:S(2)}) collective-permute-start(bf16[32,768]{1,0:T(8,128)(2,1)S(1)} %outside.10.refs_0_.refs_3_), channel_id=1, source_target_pairs={{0,448},{64,128},{128,64},{192,256},{256,192},{320,384},{384,320},... | collective-permute-start | bytes 147464 | tf_op jit(solution)/shard_map/ppermute | solution.py:197
  55.8 4.8 %all_gather.33.refs_1_ = bf16[64,768]{1,0:T(8,128)(2,1)S(1)} all-gather(bf16[32,768]{1,0:T(8,128)(2,1)S(1)} %outside.10.refs_0_.refs_3_), channel_id=1, replica_groups={{0,64},{128,192},{256,320},{384,448},{1,65},{129,193},{257,321},{385,44..., dimensions={0}, use_global_device_ids=true | all-gather | bytes 147456 | tf_op jit(solution)/shard_map/all_gather | solution.py:198
  60.5 0.5 inside.11.refs_0_
  61.0 0.3 outside.11.refs_0_.refs_3_
  61.4 4.3 %collective-permute-start.5 = (bf16[32,768]{1,0:T(8,128)(2,1)S(1)}, bf16[32,768]{1,0:T(8,128)(2,1)S(1)}, u32[]{:S(2)}, u32[]{:S(2)}) collective-permute-start(bf16[32,768]{1,0:T(8,128)(2,1)S(1)} %outside.11.refs_0_.refs_3_), channel_id=1, source_target_pairs={{0,448},{64,128},{128,64},{192,256},{256,192},{320,384},{384,320},... | collective-permute-start | bytes 147464 | tf_op jit(solution)/shard_map/ppermute | solution.py:197
  65.7 4.8 %all_gather.34.refs_1_ = bf16[64,768]{1,0:T(8,128)(2,1)S(1)} all-gather(bf16[32,768]{1,0:T(8,128)(2,1)S(1)} %outside.11.refs_0_.refs_3_), channel_id=1, replica_groups={{0,64},{128,192},{256,320},{384,448},{1,65},{129,193},{257,321},{385,44..., dimensions={0}, use_global_device_ids=true | all-gather | bytes 147456 | tf_op jit(solution)/shard_map/all_gather | solution.py:198
  70.4 0.5 inside.12.refs_0_
  70.9 0.0 collective-permute-done.5.refs_1_
  71.0 0.3 outside.12.refs_0_.refs_3_
  71.3 5.1 %collective-permute-start.6 = (bf16[32,768]{1,0:T(8,128)(2,1)S(1)}, bf16[32,768]{1,0:T(8,128)(2,1)S(1)}, u32[]{:S(2)}, u32[]{:S(2)}) collective-permute-start(bf16[32,768]{1,0:T(8,128)(2,1)S(1)} %outside.12.refs_0_.refs_3_), channel_id=1, source_target_pairs={{0,448},{64,128},{128,64},{192,256},{256,192},{320,384},{384,320},... | collective-permute-start | bytes 147464 | tf_op jit(solution)/shard_map/ppermute | solution.py:197
  76.4 4.8 %all_gather.35.refs_1_ = bf16[64,768]{1,0:T(8,128)(2,1)S(1)} all-gather(bf16[32,768]{1,0:T(8,128)(2,1)S(1)} %outside.12.refs_0_.refs_3_), channel_id=1, replica_groups={{0,64},{128,192},{256,320},{384,448},{1,65},{129,193},{257,321},{385,44..., dimensions={0}, use_global_device_ids=true | all-gather | bytes 147456 | tf_op jit(solution)/shard_map/all_gather | solution.py:198
  81.2 0.5 inside.13.refs_0_
  81.7 0.3 outside.13.refs_0_.refs_3_
  82.0 4.3 %collective-permute-start.7 = (bf16[32,768]{1,0:T(8,128)(2,1)S(1)}, bf16[32,768]{1,0:T(8,128)(2,1)S(1)}, u32[]{:S(2)}, u32[]{:S(2)}) collective-permute-start(bf16[32,768]{1,0:T(8,128)(2,1)S(1)} %outside.13.refs_0_.refs_3_), channel_id=1, source_target_pairs={{0,448},{64,128},{128,64},{192,256},{256,192},{320,384},{384,320},... | collective-permute-start | bytes 147464 | tf_op jit(solution)/shard_map/ppermute | solution.py:197
  86.3 5.1 %all_gather.36.refs_1_ = bf16[64,768]{1,0:T(8,128)(2,1)S(1)} all-gather(bf16[32,768]{1,0:T(8,128)(2,1)S(1)} %outside.13.refs_0_.refs_3_), channel_id=1, replica_groups={{0,64},{128,192},{256,320},{384,448},{1,65},{129,193},{257,321},{385,44..., dimensions={0}, use_global_device_ids=true | all-gather | bytes 147456 | tf_op jit(solution)/shard_map/all_gather | solution.py:198
  91.5 0.5 inside.14.refs_0_
  92.0 0.0 collective-permute-done.7.refs_1_
  92.0 0.3 outside.14.refs_0_
  92.3 4.9 %collective-permute-start.8 = (bf16[32,768]{1,0:T(8,128)(2,1)S(1)}, bf16[32,768]{1,0:T(8,128)(2,1)S(1)}, u32[]{:S(2)}, u32[]{:S(2)}) collective-permute-start(bf16[32,768]{1,0:T(8,128)(2,1)S(1)} %outside.14.refs_0_), channel_id=1, source_target_pairs={{0,448},{64,128},{128,64},{192,256},{256,192},{320,384},{384,320},... | collective-permute-start | bytes 147464 | tf_op jit(solution)/shard_map/ppermute | solution.py:197
  97.2 4.8 %all_gather.37.refs_1_ = bf16[64,768]{1,0:T(8,128)(2,1)S(1)} all-gather(bf16[32,768]{1,0:T(8,128)(2,1)S(1)} %outside.14.refs_0_), channel_id=1, replica_groups={{0,64},{128,192},{256,320},{384,448},{1,65},{129,193},{257,321},{385,44..., dimensions={0}, use_global_device_ids=true | all-gather | bytes 147456 | tf_op jit(solution)/shard_map/all_gather | solution.py:198
  102.0 0.5 inside.15.refs_0_
  102.5 0.0 collective-permute-done.8.refs_1_
  102.5 1.0 outside.15
  103.4 5.8 %all_gather.38.y_ref = bf16[128,768]{1,0:T(8,128)(2,1)S(1)} all-gather(bf16[32,768]{1,0:T(8,128)(2,1)} %outside.15), channel_id=1, replica_groups=mesh['elem'=8,'z'=16,'yl'=2,'c'=2] {'yl','c'}, dimensions={0}, use_global_device_ids=true | all-gather | bytes 245760 | tf_op jit(solution)/shard_map/all_gather | solution.py:254
  109.2 0.7 pick.1
  110.0 30.3 %all_to_all.5.x_ref = bf16[16,40,128]{2,1,0:T(8,128)(2,1)S(1)} all-to-all(bf16[16,40,128]{2,1,0:T(8,128)(2,1)S(1)} %pick.1), channel_id=1, replica_groups=mesh['elem'=8,'z'=16,'yl'=2,'c'=2] {'z'}, dimensions={0} | all-to-all | bytes 327680 | tf_op jit(solution)/shard_map/all_to_all | solution.py:265
  140.2 5.4 %rotate.1 = bf16[36,2048]{1,0:T(8,128)(2,1)} custom-call(bf16[16,40,128]{2,1,0:T(8,128)(2,1)S(1)} %all_to_all.5.x_ref, bf16[2048,2048]{1,0:T(8,128)(2,1)} %all-gather.2.cloned.1.call-done.r_ref), custom_call_target="tpu_custom_call" | custom-call | tf_op jit(solution)/shard_map/rotate/pallas_call | solution.py:266
  (7 shorter events, 0.0 us)
Async XLA Ops:
  7.2 133.1 %all-gather.2.cloned.1.call-start = ((), (), s32[]{:S(2)}) async-start(), calls=%async_computation.1 | async-start | bytes 8650752 | tf_op jit(solution)/shard_map/all_gather | solution.py:213
  7.2 9.3 %collective-permute-start = (bf16[32,2048]{1,0:T(8,128)(2,1)}, bf16[32,2048]{1,0:T(8,128)(2,1)S(1)}, u32[]{:S(2)}, u32[]{:S(2)}) collective-permute-start(bf16[32,2048]{1,0:T(8,128)(2,1)} %bitcast.5), channel_id=1, source_target_pairs={{0,2},{2,0},{1,3},{3,1},{4,6},{6,4},{5,7},{7,5},{8,10},{10,8},{9,1... | collective-permute-start | bytes 393224 | tf_op jit(solution)/shard_map/ppermute | solution.py:200
  18.2 9.8 %collective-permute-start.1 = (bf16[32,768]{1,0:T(8,128)(2,1)S(1)}, bf16[32,768]{1,0:T(8,128)(2,1)S(1)}, u32[]{:S(2)}, u32[]{:S(2)}) collective-permute-start(bf16[32,768]{1,0:T(8,128)(2,1)S(1)} %mask.1.refs_0_.refs_3_), channel_id=1, source_target_pairs={{0,448},{64,128},{128,64},{192,256},{256,192},{320,384},{384,320},... | collective-permute-start | bytes 147464 | tf_op jit(solution)/shard_map/ppermute | solution.py:197
  28.3 12.1 %collective-permute-start.2 = (bf16[32,768]{1,0:T(8,128)(2,1)S(1)}, bf16[32,768]{1,0:T(8,128)(2,1)S(1)}, u32[]{:S(2)}, u32[]{:S(2)}) collective-permute-start(bf16[32,768]{1,0:T(8,128)(2,1)S(1)} %outside.8.refs_0_.refs_3_), channel_id=1, source_target_pairs={{0,448},{64,128},{128,64},{192,256},{256,192},{320,384},{384,320},... | collective-permute-start | bytes 147464 | tf_op jit(solution)/shard_map/ppermute | solution.py:197
  40.7 9.6 %collective-permute-start.3 = (bf16[32,768]{1,0:T(8,128)(2,1)S(1)}, bf16[32,768]{1,0:T(8,128)(2,1)S(1)}, u32[]{:S(2)}, u32[]{:S(2)}) collective-permute-start(bf16[32,768]{1,0:T(8,128)(2,1)S(1)} %outside.9.refs_0_.refs_3_), channel_id=1, source_target_pairs={{0,448},{64,128},{128,64},{192,256},{256,192},{320,384},{384,320},... | collective-permute-start | bytes 147464 | tf_op jit(solution)/shard_map/ppermute | solution.py:197
  50.6 10.4 %collective-permute-start.4 = (bf16[32,768]{1,0:T(8,128)(2,1)S(1)}, bf16[32,768]{1,0:T(8,128)(2,1)S(1)}, u32[]{:S(2)}, u32[]{:S(2)}) collective-permute-start(bf16[32,768]{1,0:T(8,128)(2,1)S(1)} %outside.10.refs_0_.refs_3_), channel_id=1, source_target_pairs={{0,448},{64,128},{128,64},{192,256},{256,192},{320,384},{384,320},... | collective-permute-start | bytes 147464 | tf_op jit(solution)/shard_map/ppermute | solution.py:197
  61.4 9.6 %collective-permute-start.5 = (bf16[32,768]{1,0:T(8,128)(2,1)S(1)}, bf16[32,768]{1,0:T(8,128)(2,1)S(1)}, u32[]{:S(2)}, u32[]{:S(2)}) collective-permute-start(bf16[32,768]{1,0:T(8,128)(2,1)S(1)} %outside.11.refs_0_.refs_3_), channel_id=1, source_target_pairs={{0,448},{64,128},{128,64},{192,256},{256,192},{320,384},{384,320},... | collective-permute-start | bytes 147464 | tf_op jit(solution)/shard_map/ppermute | solution.py:197
  71.3 10.4 %collective-permute-start.6 = (bf16[32,768]{1,0:T(8,128)(2,1)S(1)}, bf16[32,768]{1,0:T(8,128)(2,1)S(1)}, u32[]{:S(2)}, u32[]{:S(2)}) collective-permute-start(bf16[32,768]{1,0:T(8,128)(2,1)S(1)} %outside.12.refs_0_.refs_3_), channel_id=1, source_target_pairs={{0,448},{64,128},{128,64},{192,256},{256,192},{320,384},{384,320},... | collective-permute-start | bytes 147464 | tf_op jit(solution)/shard_map/ppermute | solution.py:197
  82.0 10.0 %collective-permute-start.7 = (bf16[32,768]{1,0:T(8,128)(2,1)S(1)}, bf16[32,768]{1,0:T(8,128)(2,1)S(1)}, u32[]{:S(2)}, u32[]{:S(2)}) collective-permute-start(bf16[32,768]{1,0:T(8,128)(2,1)S(1)} %outside.13.refs_0_.refs_3_), channel_id=1, source_target_pairs={{0,448},{64,128},{128,64},{192,256},{256,192},{320,384},{384,320},... | collective-permute-start | bytes 147464 | tf_op jit(solution)/shard_map/ppermute | solution.py:197
  92.0 17.3 %copy-start = (s32[64]{0:T(128)S(1)}, s32[64]{0:T(128)}, u32[]{:S(2)}) copy-start(s32[64]{0:T(128)} %owner_rows.1) | copy-start | bytes 772
  92.3 10.1 %collective-permute-start.8 = (bf16[32,768]{1,0:T(8,128)(2,1)S(1)}, bf16[32,768]{1,0:T(8,128)(2,1)S(1)}, u32[]{:S(2)}, u32[]{:S(2)}) collective-permute-start(bf16[32,768]{1,0:T(8,128)(2,1)S(1)} %outside.14.refs_0_), channel_id=1, source_target_pairs={{0,448},{64,128},{128,64},{192,256},{256,192},{320,384},{384,320},... | collective-permute-start | bytes 147464 | tf_op jit(solution)/shard_map/ppermute | solution.py:197
Sparse Core Ops, SparseCore 0:
  18.3 82.6 all-gather.1

commit v8 on v7

--- a/solution.py
+++ b/solution.py
@@ -116,7 +116,8 @@
     y_ref[...] = (p_ref[...] + total * scale).astype(BF16)
 
 
-def pick_kernel(owner_rows, quad, y_ref, out_ref, turned):
+def pick_kernel(owner_rows, quad, y_ref, out_ref, own_ref, turned):
+    own_ref[...] = y_ref[pl.ds(pl.multiple_of(BANDS_DEV * quad[0], BANDS_DEV), BANDS_DEV), :]
     for block in range(ROWS // 128):
         part = y_ref[:, 128 * block : 128 * (block + 1)].astype(F32)
         turned[128 * block : 128 * (block + 1), :] = part.T
@@ -134,13 +135,21 @@
         out_ref[z] = jnp.where(slot < count, rows, 0.0).astype(BF16)
 
 
-def join_kernel(low, own_hbm, other_ref, out_ref, own, sem):
-    copy = pltpu.make_async_copy(own_hbm, own, sem)
-    copy.start()
+def join_kernel(low, own_hbm, other_ref, out_hbm, own, sems):
     half = other_ref.shape[0]
-    out_ref[pl.ds(pl.multiple_of(half * (1 - low[0]), half), half), :] = other_ref[...]
-    copy.wait()
-    out_ref[pl.ds(pl.multiple_of(half * low[0], half), half), :] = own[...]
+
+    def rows(place):
+        return out_hbm.at[pl.ds(pl.multiple_of(half * place, half), half)]
+
+    load = pltpu.make_async_copy(own_hbm, own, sems.at[0])
+    load.start()
+    other = pltpu.make_async_copy(other_ref, rows(1 - low[0]), sems.at[1])
+    other.start()
+    load.wait()
+    store = pltpu.make_async_copy(own, rows(low[0]), sems.at[2])
+    store.start()
+    other.wait()
+    store.wait()
 
 
 def rotate_kernel(x_ref, r_ref, out_ref, gathered):
@@ -203,8 +212,11 @@
                 join_kernel,
                 out_shape=jax.ShapeDtypeStruct((2 * BANDS_DEV, columns.shape[1]), BF16),
                 in_specs=[SMEM, HBM, VMEM],
-                out_specs=VMEM,
-                scratch_shapes=[pltpu.VMEM(columns.shape, BF16), pltpu.SemaphoreType.DMA],
+                out_specs=HBM,
+                scratch_shapes=[
+                    pltpu.VMEM(columns.shape, BF16),
+                    pltpu.SemaphoreType.DMA((3,)),
+                ],
                 compiler_params=params(8),
                 cost_estimate=COST,
                 name="join",
@@ -252,11 +264,11 @@
         earlier, current = current, following
 
     bands_quad = lax.all_gather(current, ("yl", "c"), axis=0, tiled=True)
-    sent = pl.pallas_call(
+    sent, filtered = pl.pallas_call(
         pick_kernel,
-        out_shape=jax.ShapeDtypeStruct((Z, CAP_PAD, QUAD * BANDS_DEV), BF16),
+        out_shape=(jax.ShapeDtypeStruct((Z, CAP_PAD, QUAD * BANDS_DEV), BF16), block_bf16),
         in_specs=[SMEM, SMEM, VMEM],
-        out_specs=VMEM,
+        out_specs=(VMEM, VMEM),
         scratch_shapes=[pltpu.VMEM((ROWS + 48, QUAD * BANDS_DEV), F32)],
         compiler_params=params(8),
         cost_estimate=COST,
@@ -276,7 +288,7 @@
         compiler_params=params(24),
         name="rotate",
     )(received, in_hbm(rotation_all))
-    return current, rotated
+    return filtered, rotated
 
 
 def solution(mesh):

time: 153 us -> 153 us (level)
  no operation moved by 1% of the time
where the time goes in v8:
time: 153 us; the launch traced here: 152 us
  blocking collectives  74.4 us (49%)
  starting transfers between devices  45.4 us (30%)
  Pallas kernels  18.1 us (12%)
  between operations  14.2 us (9%)
    ppermute x8, starting transfers between devices, per_device(): from_far = lax.ppermute(current, 'elem', far)  41.9 us
    all_gather x8, blocking collectives, per_device(): lax.all_gather(current, 'elem', axis=0, tiled=True, axis_index_groups=near)  38.4 us
    all_to_all x1, blocking collectives, per_device(): lax.all_to_all(sent, 'z', split_axis=0, concat_axis=0, tiled=True)  30.3 us
    all_gather x1, blocking collectives, per_device(): bands_quad = lax.all_gather(current, ('yl', 'c'), axis=0, tiled=True)  5.59 us
    pallas_call x1, Pallas kernels, per_device(): pl.pallas_call(rotate_kernel, out_shape=jax.ShapeDtypeStruct((CAP, rotati...  5.41 us
    pallas_call x8, Pallas kernels, per_device(): pl.pallas_call(lambda *refs, scale=scale, has_prev=bool(previous): inside...  3.96 us
    ppermute x1, starting transfers between devices, per_device(): other_columns = lax.ppermute(columns, 'yl', [(0, 1), (1, 0)])  3.49 us
  transfers between devices with their start and end apart: 10, of which 0 were waited for; matrix products, arithmetic and copies ran while one was open for 0% of the time, Pallas kernels for 7%

profile of v8, /device:TPU:32, one launch (start us, length us, event | category | flops | bytes accessed | tf_op | source)
XLA Modules:
  0.0 152.2 jit_solution(2663099950700402927)
XLA Ops:
  7.2 0.0 all-gather.2.cloned.1.call-start
  7.2 3.5 %collective-permute-start = (bf16[32,2048]{1,0:T(8,128)(2,1)}, bf16[32,2048]{1,0:T(8,128)(2,1)S(1)}, u32[]{:S(2)}, u32[]{:S(2)}) collective-permute-start(bf16[32,2048]{1,0:T(8,128)(2,1)} %bitcast.5), channel_id=1, source_target_pairs={{0,2},{2,0},{1,3},{3,1},{4,6},{6,4},{5,7},{7,5},{8,10},{10,8},{9,1... | collective-permute-start | bytes 393224 | tf_op jit(solution)/shard_map/ppermute | solution.py:209
  10.7 1.0 mask.1.refs_0_.refs_3_
  11.7 4.8 %all_gather.30.refs_1_ = bf16[64,768]{1,0:T(8,128)(2,1)S(1)} all-gather(bf16[32,768]{1,0:T(8,128)(2,1)S(1)} %mask.1.refs_0_.refs_3_), channel_id=1, replica_groups={{0,64},{128,192},{256,320},{384,448},{1,65},{129,193},{257,321},{385,44..., dimensions={0}, use_global_device_ids=true | all-gather | bytes 147456 | tf_op jit(solution)/shard_map/all_gather | solution.py:207
  16.5 1.6 %join.1 = bf16[64,2048]{1,0:T(8,128)(2,1)} custom-call(s32[1]{0:T(128)} %bitcast.low, bf16[32,2048]{1,0:T(8,128)(2,1)} %bitcast.6, bf16[32,2048]{1,0:T(8,128)(2,1)S(1)} %collective-permute-done.other_ref), custom_call_target="tpu_custom_call" | custom-call | flops 300000000 | bytes 3145728 | tf_op jit(solution)/shard_map/join/pallas_call | solution.py:211
  18.1 0.0 all-gather.2.cloned.1.call-update
  18.1 7.0 %collective-permute-start.1 = (bf16[32,768]{1,0:T(8,128)(2,1)S(1)}, bf16[32,768]{1,0:T(8,128)(2,1)S(1)}, u32[]{:S(2)}, u32[]{:S(2)}) collective-permute-start(bf16[32,768]{1,0:T(8,128)(2,1)S(1)} %mask.1.refs_0_.refs_3_), channel_id=1, source_target_pairs={{0,448},{64,128},{128,64},{192,256},{256,192},{320,384},{384,320},... | collective-permute-start | bytes 147464 | tf_op jit(solution)/shard_map/ppermute | solution.py:206
  25.1 2.2 %couple.1 = (bf16[1536,768]{1,0:T(8,128)(2,1)S(1)}, bf16[768,768]{1,0:T(8,128)(2,1)S(1)}) custom-call(s32[4,6]{1,0:T(4,128)} %neighbours_hbm.1, s32[4]{0:T(128)} %counts_hbm.3, s32[1]{0:T(128)} %bitcast.2.parity, bf16[4,7,192,192]{3,2,1,0:T(8,128)(2,1)} %h_hbm.1), custom_call_target="tpu_custom_call" | custom-call | tf_op jit(solution)/shard_map/couple/pallas_call | solution.py:226
  27.4 0.5 inside.8.refs_0_
  27.9 0.0 collective-permute-done.1.refs_1_
  27.9 0.3 outside.8.refs_0_.refs_3_
  28.3 6.8 %collective-permute-start.2 = (bf16[32,768]{1,0:T(8,128)(2,1)S(1)}, bf16[32,768]{1,0:T(8,128)(2,1)S(1)}, u32[]{:S(2)}, u32[]{:S(2)}) collective-permute-start(bf16[32,768]{1,0:T(8,128)(2,1)S(1)} %outside.8.refs_0_.refs_3_), channel_id=1, source_target_pairs={{0,448},{64,128},{128,64},{192,256},{256,192},{320,384},{384,320},... | collective-permute-start | bytes 147464 | tf_op jit(solution)/shard_map/ppermute | solution.py:206
  35.1 4.8 %all_gather.31.refs_1_ = bf16[64,768]{1,0:T(8,128)(2,1)S(1)} all-gather(bf16[32,768]{1,0:T(8,128)(2,1)S(1)} %outside.8.refs_0_.refs_3_), channel_id=1, replica_groups={{0,64},{128,192},{256,320},{384,448},{1,65},{129,193},{257,321},{385,44..., dimensions={0}, use_global_device_ids=true | all-gather | bytes 147456 | tf_op jit(solution)/shard_map/all_gather | solution.py:207
  39.8 0.5 inside.9.refs_0_
  40.3 0.0 collective-permute-done.2.refs_1_
  40.3 0.3 outside.9.refs_0_.refs_3_
  40.7 4.3 %collective-permute-start.3 = (bf16[32,768]{1,0:T(8,128)(2,1)S(1)}, bf16[32,768]{1,0:T(8,128)(2,1)S(1)}, u32[]{:S(2)}, u32[]{:S(2)}) collective-permute-start(bf16[32,768]{1,0:T(8,128)(2,1)S(1)} %outside.9.refs_0_.refs_3_), channel_id=1, source_target_pairs={{0,448},{64,128},{128,64},{192,256},{256,192},{320,384},{384,320},... | collective-permute-start | bytes 147464 | tf_op jit(solution)/shard_map/ppermute | solution.py:206
  45.0 4.8 %all_gather.32.refs_1_ = bf16[64,768]{1,0:T(8,128)(2,1)S(1)} all-gather(bf16[32,768]{1,0:T(8,128)(2,1)S(1)} %outside.9.refs_0_.refs_3_), channel_id=1, replica_groups={{0,64},{128,192},{256,320},{384,448},{1,65},{129,193},{257,321},{385,44..., dimensions={0}, use_global_device_ids=true | all-gather | bytes 147456 | tf_op jit(solution)/shard_map/all_gather | solution.py:207
  49.7 0.5 inside.10.refs_0_
  50.2 0.0 collective-permute-done.3.refs_1_
  50.3 0.3 outside.10.refs_0_.refs_3_
  50.6 5.1 %collective-permute-start.4 = (bf16[32,768]{1,0:T(8,128)(2,1)S(1)}, bf16[32,768]{1,0:T(8,128)(2,1)S(1)}, u32[]{:S(2)}, u32[]{:S(2)}) collective-permute-start(bf16[32,768]{1,0:T(8,128)(2,1)S(1)} %outside.10.refs_0_.refs_3_), channel_id=1, source_target_pairs={{0,448},{64,128},{128,64},{192,256},{256,192},{320,384},{384,320},... | collective-permute-start | bytes 147464 | tf_op jit(solution)/shard_map/ppermute | solution.py:206
  55.7 4.8 %all_gather.33.refs_1_ = bf16[64,768]{1,0:T(8,128)(2,1)S(1)} all-gather(bf16[32,768]{1,0:T(8,128)(2,1)S(1)} %outside.10.refs_0_.refs_3_), channel_id=1, replica_groups={{0,64},{128,192},{256,320},{384,448},{1,65},{129,193},{257,321},{385,44..., dimensions={0}, use_global_device_ids=true | all-gather | bytes 147456 | tf_op jit(solution)/shard_map/all_gather | solution.py:207
  60.5 0.5 inside.11.refs_0_
  61.0 0.0 collective-permute-done.4.refs_1_
  61.0 0.3 outside.11.refs_0_.refs_3_
  61.3 4.3 %collective-permute-start.5 = (bf16[32,768]{1,0:T(8,128)(2,1)S(1)}, bf16[32,768]{1,0:T(8,128)(2,1)S(1)}, u32[]{:S(2)}, u32[]{:S(2)}) collective-permute-start(bf16[32,768]{1,0:T(8,128)(2,1)S(1)} %outside.11.refs_0_.refs_3_), channel_id=1, source_target_pairs={{0,448},{64,128},{128,64},{192,256},{256,192},{320,384},{384,320},... | collective-permute-start | bytes 147464 | tf_op jit(solution)/shard_map/ppermute | solution.py:206
  65.7 4.8 %all_gather.34.refs_1_ = bf16[64,768]{1,0:T(8,128)(2,1)S(1)} all-gather(bf16[32,768]{1,0:T(8,128)(2,1)S(1)} %outside.11.refs_0_.refs_3_), channel_id=1, replica_groups={{0,64},{128,192},{256,320},{384,448},{1,65},{129,193},{257,321},{385,44..., dimensions={0}, use_global_device_ids=true | all-gather | bytes 147456 | tf_op jit(solution)/shard_map/all_gather | solution.py:207
  70.4 0.5 inside.12.refs_0_
  70.9 0.0 collective-permute-done.5.refs_1_
  70.9 0.3 outside.12.refs_0_.refs_3_
  71.3 5.1 %collective-permute-start.6 = (bf16[32,768]{1,0:T(8,128)(2,1)S(1)}, bf16[32,768]{1,0:T(8,128)(2,1)S(1)}, u32[]{:S(2)}, u32[]{:S(2)}) collective-permute-start(bf16[32,768]{1,0:T(8,128)(2,1)S(1)} %outside.12.refs_0_.refs_3_), channel_id=1, source_target_pairs={{0,448},{64,128},{128,64},{192,256},{256,192},{320,384},{384,320},... | collective-permute-start | bytes 147464 | tf_op jit(solution)/shard_map/ppermute | solution.py:206
  76.4 4.8 %all_gather.35.refs_1_ = bf16[64,768]{1,0:T(8,128)(2,1)S(1)} all-gather(bf16[32,768]{1,0:T(8,128)(2,1)S(1)} %outside.12.refs_0_.refs_3_), channel_id=1, replica_groups={{0,64},{128,192},{256,320},{384,448},{1,65},{129,193},{257,321},{385,44..., dimensions={0}, use_global_device_ids=true | all-gather | bytes 147456 | tf_op jit(solution)/shard_map/all_gather | solution.py:207
  81.2 0.5 inside.13.refs_0_
  81.7 0.0 collective-permute-done.6.refs_1_
  81.7 0.3 outside.13.refs_0_.refs_3_
  82.0 4.3 %collective-permute-start.7 = (bf16[32,768]{1,0:T(8,128)(2,1)S(1)}, bf16[32,768]{1,0:T(8,128)(2,1)S(1)}, u32[]{:S(2)}, u32[]{:S(2)}) collective-permute-start(bf16[32,768]{1,0:T(8,128)(2,1)S(1)} %outside.13.refs_0_.refs_3_), channel_id=1, source_target_pairs={{0,448},{64,128},{128,64},{192,256},{256,192},{320,384},{384,320},... | collective-permute-start | bytes 147464 | tf_op jit(solution)/shard_map/ppermute | solution.py:206
  86.3 5.1 %all_gather.36.refs_1_ = bf16[64,768]{1,0:T(8,128)(2,1)S(1)} all-gather(bf16[32,768]{1,0:T(8,128)(2,1)S(1)} %outside.13.refs_0_.refs_3_), channel_id=1, replica_groups={{0,64},{128,192},{256,320},{384,448},{1,65},{129,193},{257,321},{385,44..., dimensions={0}, use_global_device_ids=true | all-gather | bytes 147456 | tf_op jit(solution)/shard_map/all_gather | solution.py:207
  91.5 0.5 inside.14.refs_0_
  92.0 0.3 outside.14.refs_0_
  92.3 4.9 %collective-permute-start.8 = (bf16[32,768]{1,0:T(8,128)(2,1)S(1)}, bf16[32,768]{1,0:T(8,128)(2,1)S(1)}, u32[]{:S(2)}, u32[]{:S(2)}) collective-permute-start(bf16[32,768]{1,0:T(8,128)(2,1)S(1)} %outside.14.refs_0_), channel_id=1, source_target_pairs={{0,448},{64,128},{128,64},{192,256},{256,192},{320,384},{384,320},... | collective-permute-start | bytes 147464 | tf_op jit(solution)/shard_map/ppermute | solution.py:206
  97.2 4.8 %all_gather.37.refs_1_ = bf16[64,768]{1,0:T(8,128)(2,1)S(1)} all-gather(bf16[32,768]{1,0:T(8,128)(2,1)S(1)} %outside.14.refs_0_), channel_id=1, replica_groups={{0,64},{128,192},{256,320},{384,448},{1,65},{129,193},{257,321},{385,44..., dimensions={0}, use_global_device_ids=true | all-gather | bytes 147456 | tf_op jit(solution)/shard_map/all_gather | solution.py:207
  101.9 0.5 inside.15.refs_0_
  102.4 0.3 outside.15
  102.8 5.6 %all_gather.38.y_ref = bf16[128,768]{1,0:T(8,128)(2,1)S(1)} all-gather(bf16[32,768]{1,0:T(8,128)(2,1)S(1)} %outside.15), channel_id=1, replica_groups=mesh['elem'=8,'z'=16,'yl'=2,'c'=2] {'yl','c'}, dimensions={0}, use_global_device_ids=true | all-gather | bytes 245760 | tf_op jit(solution)/shard_map/all_gather | solution.py:266
  108.4 1.3 pick.1
  109.6 30.3 %all_to_all.5.x_ref = bf16[16,40,128]{2,1,0:T(8,128)(2,1)S(1)} all-to-all(bf16[16,40,128]{2,1,0:T(8,128)(2,1)S(1)} %get-tuple-element.20), channel_id=1, replica_groups=mesh['elem'=8,'z'=16,'yl'=2,'c'=2] {'z'}, dimensions={0} | all-to-all | bytes 327680 | tf_op jit(solution)/shard_map/all_to_all | solution.py:277
  140.0 5.4 %rotate.1 = bf16[36,2048]{1,0:T(8,128)(2,1)} custom-call(bf16[16,40,128]{2,1,0:T(8,128)(2,1)S(1)} %all_to_all.5.x_ref, bf16[2048,2048]{1,0:T(8,128)(2,1)} %all-gather.2.cloned.1.call-done.r_ref), custom_call_target="tpu_custom_call" | custom-call | tf_op jit(solution)/shard_map/rotate/pallas_call | solution.py:278
  (7 shorter events, 0.0 us)
Async XLA Ops:
  7.2 132.8 %all-gather.2.cloned.1.call-start = ((), (), s32[]{:S(2)}) async-start(), calls=%async_computation.1 | async-start | bytes 8650752 | tf_op jit(solution)/shard_map/all_gather | solution.py:225
  7.2 9.3 %collective-permute-start = (bf16[32,2048]{1,0:T(8,128)(2,1)}, bf16[32,2048]{1,0:T(8,128)(2,1)S(1)}, u32[]{:S(2)}, u32[]{:S(2)}) collective-permute-start(bf16[32,2048]{1,0:T(8,128)(2,1)} %bitcast.5), channel_id=1, source_target_pairs={{0,2},{2,0},{1,3},{3,1},{4,6},{6,4},{5,7},{7,5},{8,10},{10,8},{9,1... | collective-permute-start | bytes 393224 | tf_op jit(solution)/shard_map/ppermute | solution.py:209
  18.1 9.8 %collective-permute-start.1 = (bf16[32,768]{1,0:T(8,128)(2,1)S(1)}, bf16[32,768]{1,0:T(8,128)(2,1)S(1)}, u32[]{:S(2)}, u32[]{:S(2)}) collective-permute-start(bf16[32,768]{1,0:T(8,128)(2,1)S(1)} %mask.1.refs_0_.refs_3_), channel_id=1, source_target_pairs={{0,448},{64,128},{128,64},{192,256},{256,192},{320,384},{384,320},... | collective-permute-start | bytes 147464 | tf_op jit(solution)/shard_map/ppermute | solution.py:206
  28.3 12.1 %collective-permute-start.2 = (bf16[32,768]{1,0:T(8,128)(2,1)S(1)}, bf16[32,768]{1,0:T(8,128)(2,1)S(1)}, u32[]{:S(2)}, u32[]{:S(2)}) collective-permute-start(bf16[32,768]{1,0:T(8,128)(2,1)S(1)} %outside.8.refs_0_.refs_3_), channel_id=1, source_target_pairs={{0,448},{64,128},{128,64},{192,256},{256,192},{320,384},{384,320},... | collective-permute-start | bytes 147464 | tf_op jit(solution)/shard_map/ppermute | solution.py:206
  40.7 9.6 %collective-permute-start.3 = (bf16[32,768]{1,0:T(8,128)(2,1)S(1)}, bf16[32,768]{1,0:T(8,128)(2,1)S(1)}, u32[]{:S(2)}, u32[]{:S(2)}) collective-permute-start(bf16[32,768]{1,0:T(8,128)(2,1)S(1)} %outside.9.refs_0_.refs_3_), channel_id=1, source_target_pairs={{0,448},{64,128},{128,64},{192,256},{256,192},{320,384},{384,320},... | collective-permute-start | bytes 147464 | tf_op jit(solution)/shard_map/ppermute | solution.py:206
  50.6 10.4 %collective-permute-start.4 = (bf16[32,768]{1,0:T(8,128)(2,1)S(1)}, bf16[32,768]{1,0:T(8,128)(2,1)S(1)}, u32[]{:S(2)}, u32[]{:S(2)}) collective-permute-start(bf16[32,768]{1,0:T(8,128)(2,1)S(1)} %outside.10.refs_0_.refs_3_), channel_id=1, source_target_pairs={{0,448},{64,128},{128,64},{192,256},{256,192},{320,384},{384,320},... | collective-permute-start | bytes 147464 | tf_op jit(solution)/shard_map/ppermute | solution.py:206
  61.3 9.6 %collective-permute-start.5 = (bf16[32,768]{1,0:T(8,128)(2,1)S(1)}, bf16[32,768]{1,0:T(8,128)(2,1)S(1)}, u32[]{:S(2)}, u32[]{:S(2)}) collective-permute-start(bf16[32,768]{1,0:T(8,128)(2,1)S(1)} %outside.11.refs_0_.refs_3_), channel_id=1, source_target_pairs={{0,448},{64,128},{128,64},{192,256},{256,192},{320,384},{384,320},... | collective-permute-start | bytes 147464 | tf_op jit(solution)/shard_map/ppermute | solution.py:206
  71.3 10.4 %collective-permute-start.6 = (bf16[32,768]{1,0:T(8,128)(2,1)S(1)}, bf16[32,768]{1,0:T(8,128)(2,1)S(1)}, u32[]{:S(2)}, u32[]{:S(2)}) collective-permute-start(bf16[32,768]{1,0:T(8,128)(2,1)S(1)} %outside.12.refs_0_.refs_3_), channel_id=1, source_target_pairs={{0,448},{64,128},{128,64},{192,256},{256,192},{320,384},{384,320},... | collective-permute-start | bytes 147464 | tf_op jit(solution)/shard_map/ppermute | solution.py:206
  82.0 10.0 %collective-permute-start.7 = (bf16[32,768]{1,0:T(8,128)(2,1)S(1)}, bf16[32,768]{1,0:T(8,128)(2,1)S(1)}, u32[]{:S(2)}, u32[]{:S(2)}) collective-permute-start(bf16[32,768]{1,0:T(8,128)(2,1)S(1)} %outside.13.refs_0_.refs_3_), channel_id=1, source_target_pairs={{0,448},{64,128},{128,64},{192,256},{256,192},{320,384},{384,320},... | collective-permute-start | bytes 147464 | tf_op jit(solution)/shard_map/ppermute | solution.py:206
  92.0 16.4 %copy-start = (s32[64]{0:T(128)S(1)}, s32[64]{0:T(128)}, u32[]{:S(2)}) copy-start(s32[64]{0:T(128)} %owner_rows.1) | copy-start | bytes 772
  92.3 10.1 %collective-permute-start.8 = (bf16[32,768]{1,0:T(8,128)(2,1)S(1)}, bf16[32,768]{1,0:T(8,128)(2,1)S(1)}, u32[]{:S(2)}, u32[]{:S(2)}) collective-permute-start(bf16[32,768]{1,0:T(8,128)(2,1)S(1)} %outside.14.refs_0_), channel_id=1, source_target_pairs={{0,448},{64,128},{128,64},{192,256},{256,192},{320,384},{384,320},... | collective-permute-start | bytes 147464 | tf_op jit(solution)/shard_map/ppermute | solution.py:206
Sparse Core Ops, SparseCore 0:
  18.3 82.5 all-gather.1

commit v9 on v8

--- a/solution.py
+++ b/solution.py
@@ -116,8 +116,10 @@
     y_ref[...] = (p_ref[...] + total * scale).astype(BF16)
 
 
-def pick_kernel(owner_rows, quad, y_ref, out_ref, own_ref, turned):
-    own_ref[...] = y_ref[pl.ds(pl.multiple_of(BANDS_DEV * quad[0], BANDS_DEV), BANDS_DEV), :]
+def pick_kernel(owner_rows, quad, y_ref, out_ref, own_hbm, turned, sem):
+    mine = pl.ds(pl.multiple_of(BANDS_DEV * quad[0], BANDS_DEV), BANDS_DEV)
+    store = pltpu.make_async_copy(y_ref.at[mine], own_hbm, sem)
+    store.start()
     for block in range(ROWS // 128):
         part = y_ref[:, 128 * block : 128 * (block + 1)].astype(F32)
         turned[128 * block : 128 * (block + 1), :] = part.T
@@ -133,6 +135,7 @@
         first = first + counts[QUAD - 1]
         rows = turned[pl.ds(start, CAP_PAD), :]
         out_ref[z] = jnp.where(slot < count, rows, 0.0).astype(BF16)
+    store.wait()
 
 
 def join_kernel(low, own_hbm, other_ref, out_hbm, own, sems):
@@ -268,8 +271,11 @@
         pick_kernel,
         out_shape=(jax.ShapeDtypeStruct((Z, CAP_PAD, QUAD * BANDS_DEV), BF16), block_bf16),
         in_specs=[SMEM, SMEM, VMEM],
-        out_specs=(VMEM, VMEM),
-        scratch_shapes=[pltpu.VMEM((ROWS + 48, QUAD * BANDS_DEV), F32)],
+        out_specs=(VMEM, HBM),
+        scratch_shapes=[
+            pltpu.VMEM((ROWS + 48, QUAD * BANDS_DEV), F32),
+            pltpu.SemaphoreType.DMA,
+        ],
         compiler_params=params(8),
         cost_estimate=COST,
         name="pick",

time: 153 us -> 153 us (level)
  no operation moved by 1% of the time
where the time goes in v9:
time: 153 us; the launch traced here: 152 us
  blocking collectives  74.4 us (49%)
  starting transfers between devices  45.4 us (30%)
  Pallas kernels  18.1 us (12%)
  between operations  14.2 us (9%)
    ppermute x8, starting transfers between devices, per_device(): from_far = lax.ppermute(current, 'elem', far)  41.9 us
    all_gather x8, blocking collectives, per_device(): lax.all_gather(current, 'elem', axis=0, tiled=True, axis_index_groups=near)  38.4 us
    all_to_all x1, blocking collectives, per_device(): lax.all_to_all(sent, 'z', split_axis=0, concat_axis=0, tiled=True)  30.4 us
    all_gather x1, blocking collectives, per_device(): bands_quad = lax.all_gather(current, ('yl', 'c'), axis=0, tiled=True)  5.59 us
    pallas_call x1, Pallas kernels, per_device(): pl.pallas_call(rotate_kernel, out_shape=jax.ShapeDtypeStruct((CAP, rotati...  5.41 us
    pallas_call x8, Pallas kernels, per_device(): pl.pallas_call(lambda *refs, scale=scale, has_prev=bool(previous): inside...  3.96 us
    ppermute x1, starting transfers between devices, per_device(): other_columns = lax.ppermute(columns, 'yl', [(0, 1), (1, 0)])  3.49 us
  transfers between devices with their start and end apart: 10, of which 0 were waited for; matrix products, arithmetic and copies ran while one was open for 0% of the time, Pallas kernels for 7%

profile of v9, /device:TPU:32, one launch (start us, length us, event | category | flops | bytes accessed | tf_op | source)
XLA Modules:
  0.0 152.3 jit_solution(11433416752420696304)
XLA Ops:
  7.2 0.0 all-gather.2.cloned.1.call-start
  7.2 3.5 %collective-permute-start = (bf16[32,2048]{1,0:T(8,128)(2,1)}, bf16[32,2048]{1,0:T(8,128)(2,1)S(1)}, u32[]{:S(2)}, u32[]{:S(2)}) collective-permute-start(bf16[32,2048]{1,0:T(8,128)(2,1)} %bitcast.5), channel_id=1, source_target_pairs={{0,2},{2,0},{1,3},{3,1},{4,6},{6,4},{5,7},{7,5},{8,10},{10,8},{9,1... | collective-permute-start | bytes 393224 | tf_op jit(solution)/shard_map/ppermute | solution.py:212
  10.7 1.0 mask.1.refs_0_.refs_3_
  11.7 4.8 %all_gather.30.refs_1_ = bf16[64,768]{1,0:T(8,128)(2,1)S(1)} all-gather(bf16[32,768]{1,0:T(8,128)(2,1)S(1)} %mask.1.refs_0_.refs_3_), channel_id=1, replica_groups={{0,64},{128,192},{256,320},{384,448},{1,65},{129,193},{257,321},{385,44..., dimensions={0}, use_global_device_ids=true | all-gather | bytes 147456 | tf_op jit(solution)/shard_map/all_gather | solution.py:210
  16.5 1.6 %join.1 = bf16[64,2048]{1,0:T(8,128)(2,1)} custom-call(s32[1]{0:T(128)} %bitcast.low, bf16[32,2048]{1,0:T(8,128)(2,1)} %bitcast.6, bf16[32,2048]{1,0:T(8,128)(2,1)S(1)} %collective-permute-done.other_ref), custom_call_target="tpu_custom_call" | custom-call | flops 300000000 | bytes 3145728 | tf_op jit(solution)/shard_map/join/pallas_call | solution.py:214
  18.1 0.0 all-gather.2.cloned.1.call-update
  18.1 7.0 %collective-permute-start.1 = (bf16[32,768]{1,0:T(8,128)(2,1)S(1)}, bf16[32,768]{1,0:T(8,128)(2,1)S(1)}, u32[]{:S(2)}, u32[]{:S(2)}) collective-permute-start(bf16[32,768]{1,0:T(8,128)(2,1)S(1)} %mask.1.refs_0_.refs_3_), channel_id=1, source_target_pairs={{0,448},{64,128},{128,64},{192,256},{256,192},{320,384},{384,320},... | collective-permute-start | bytes 147464 | tf_op jit(solution)/shard_map/ppermute | solution.py:209
  25.1 2.2 %couple.1 = (bf16[1536,768]{1,0:T(8,128)(2,1)S(1)}, bf16[768,768]{1,0:T(8,128)(2,1)S(1)}) custom-call(s32[4,6]{1,0:T(4,128)} %neighbours_hbm.1, s32[4]{0:T(128)} %counts_hbm.3, s32[1]{0:T(128)} %bitcast.2.parity, bf16[4,7,192,192]{3,2,1,0:T(8,128)(2,1)} %h_hbm.1), custom_call_target="tpu_custom_call" | custom-call | tf_op jit(solution)/shard_map/couple/pallas_call | solution.py:229
  27.4 0.5 inside.8.refs_0_
  27.9 0.0 collective-permute-done.1.refs_1_
  27.9 0.3 outside.8.refs_0_.refs_3_
  28.3 6.8 %collective-permute-start.2 = (bf16[32,768]{1,0:T(8,128)(2,1)S(1)}, bf16[32,768]{1,0:T(8,128)(2,1)S(1)}, u32[]{:S(2)}, u32[]{:S(2)}) collective-permute-start(bf16[32,768]{1,0:T(8,128)(2,1)S(1)} %outside.8.refs_0_.refs_3_), channel_id=1, source_target_pairs={{0,448},{64,128},{128,64},{192,256},{256,192},{320,384},{384,320},... | collective-permute-start | bytes 147464 | tf_op jit(solution)/shard_map/ppermute | solution.py:209
  35.1 4.8 %all_gather.31.refs_1_ = bf16[64,768]{1,0:T(8,128)(2,1)S(1)} all-gather(bf16[32,768]{1,0:T(8,128)(2,1)S(1)} %outside.8.refs_0_.refs_3_), channel_id=1, replica_groups={{0,64},{128,192},{256,320},{384,448},{1,65},{129,193},{257,321},{385,44..., dimensions={0}, use_global_device_ids=true | all-gather | bytes 147456 | tf_op jit(solution)/shard_map/all_gather | solution.py:210
  39.8 0.5 inside.9.refs_0_
  40.3 0.0 collective-permute-done.2.refs_1_
  40.3 0.3 outside.9.refs_0_.refs_3_
  40.7 4.3 %collective-permute-start.3 = (bf16[32,768]{1,0:T(8,128)(2,1)S(1)}, bf16[32,768]{1,0:T(8,128)(2,1)S(1)}, u32[]{:S(2)}, u32[]{:S(2)}) collective-permute-start(bf16[32,768]{1,0:T(8,128)(2,1)S(1)} %outside.9.refs_0_.refs_3_), channel_id=1, source_target_pairs={{0,448},{64,128},{128,64},{192,256},{256,192},{320,384},{384,320},... | collective-permute-start | bytes 147464 | tf_op jit(solution)/shard_map/ppermute | solution.py:209
  45.0 4.8 %all_gather.32.refs_1_ = bf16[64,768]{1,0:T(8,128)(2,1)S(1)} all-gather(bf16[32,768]{1,0:T(8,128)(2,1)S(1)} %outside.9.refs_0_.refs_3_), channel_id=1, replica_groups={{0,64},{128,192},{256,320},{384,448},{1,65},{129,193},{257,321},{385,44..., dimensions={0}, use_global_device_ids=true | all-gather | bytes 147456 | tf_op jit(solution)/shard_map/all_gather | solution.py:210
  49.7 0.5 inside.10.refs_0_
  50.2 0.0 collective-permute-done.3.refs_1_
  50.3 0.3 outside.10.refs_0_.refs_3_
  50.6 5.1 %collective-permute-start.4 = (bf16[32,768]{1,0:T(8,128)(2,1)S(1)}, bf16[32,768]{1,0:T(8,128)(2,1)S(1)}, u32[]{:S(2)}, u32[]{:S(2)}) collective-permute-start(bf16[32,768]{1,0:T(8,128)(2,1)S(1)} %outside.10.refs_0_.refs_3_), channel_id=1, source_target_pairs={{0,448},{64,128},{128,64},{192,256},{256,192},{320,384},{384,320},... | collective-permute-start | bytes 147464 | tf_op jit(solution)/shard_map/ppermute | solution.py:209
  55.7 4.8 %all_gather.33.refs_1_ = bf16[64,768]{1,0:T(8,128)(2,1)S(1)} all-gather(bf16[32,768]{1,0:T(8,128)(2,1)S(1)} %outside.10.refs_0_.refs_3_), channel_id=1, replica_groups={{0,64},{128,192},{256,320},{384,448},{1,65},{129,193},{257,321},{385,44..., dimensions={0}, use_global_device_ids=true | all-gather | bytes 147456 | tf_op jit(solution)/shard_map/all_gather | solution.py:210
  60.5 0.5 inside.11.refs_0_
  61.0 0.0 collective-permute-done.4.refs_1_
  61.0 0.3 outside.11.refs_0_.refs_3_
  61.3 4.3 %collective-permute-start.5 = (bf16[32,768]{1,0:T(8,128)(2,1)S(1)}, bf16[32,768]{1,0:T(8,128)(2,1)S(1)}, u32[]{:S(2)}, u32[]{:S(2)}) collective-permute-start(bf16[32,768]{1,0:T(8,128)(2,1)S(1)} %outside.11.refs_0_.refs_3_), channel_id=1, source_target_pairs={{0,448},{64,128},{128,64},{192,256},{256,192},{320,384},{384,320},... | collective-permute-start | bytes 147464 | tf_op jit(solution)/shard_map/ppermute | solution.py:209
  65.7 4.8 %all_gather.34.refs_1_ = bf16[64,768]{1,0:T(8,128)(2,1)S(1)} all-gather(bf16[32,768]{1,0:T(8,128)(2,1)S(1)} %outside.11.refs_0_.refs_3_), channel_id=1, replica_groups={{0,64},{128,192},{256,320},{384,448},{1,65},{129,193},{257,321},{385,44..., dimensions={0}, use_global_device_ids=true | all-gather | bytes 147456 | tf_op jit(solution)/shard_map/all_gather | solution.py:210
  70.4 0.5 inside.12.refs_0_
  70.9 0.0 collective-permute-done.5.refs_1_
  70.9 0.3 outside.12.refs_0_.refs_3_
  71.3 5.1 %collective-permute-start.6 = (bf16[32,768]{1,0:T(8,128)(2,1)S(1)}, bf16[32,768]{1,0:T(8,128)(2,1)S(1)}, u32[]{:S(2)}, u32[]{:S(2)}) collective-permute-start(bf16[32,768]{1,0:T(8,128)(2,1)S(1)} %outside.12.refs_0_.refs_3_), channel_id=1, source_target_pairs={{0,448},{64,128},{128,64},{192,256},{256,192},{320,384},{384,320},... | collective-permute-start | bytes 147464 | tf_op jit(solution)/shard_map/ppermute | solution.py:209
  76.4 4.8 %all_gather.35.refs_1_ = bf16[64,768]{1,0:T(8,128)(2,1)S(1)} all-gather(bf16[32,768]{1,0:T(8,128)(2,1)S(1)} %outside.12.refs_0_.refs_3_), channel_id=1, replica_groups={{0,64},{128,192},{256,320},{384,448},{1,65},{129,193},{257,321},{385,44..., dimensions={0}, use_global_device_ids=true | all-gather | bytes 147456 | tf_op jit(solution)/shard_map/all_gather | solution.py:210
  81.2 0.5 inside.13.refs_0_
  81.7 0.0 collective-permute-done.6.refs_1_
  81.7 0.3 outside.13.refs_0_.refs_3_
  82.0 4.3 %collective-permute-start.7 = (bf16[32,768]{1,0:T(8,128)(2,1)S(1)}, bf16[32,768]{1,0:T(8,128)(2,1)S(1)}, u32[]{:S(2)}, u32[]{:S(2)}) collective-permute-start(bf16[32,768]{1,0:T(8,128)(2,1)S(1)} %outside.13.refs_0_.refs_3_), channel_id=1, source_target_pairs={{0,448},{64,128},{128,64},{192,256},{256,192},{320,384},{384,320},... | collective-permute-start | bytes 147464 | tf_op jit(solution)/shard_map/ppermute | solution.py:209
  86.3 5.1 %all_gather.36.refs_1_ = bf16[64,768]{1,0:T(8,128)(2,1)S(1)} all-gather(bf16[32,768]{1,0:T(8,128)(2,1)S(1)} %outside.13.refs_0_.refs_3_), channel_id=1, replica_groups={{0,64},{128,192},{256,320},{384,448},{1,65},{129,193},{257,321},{385,44..., dimensions={0}, use_global_device_ids=true | all-gather | bytes 147456 | tf_op jit(solution)/shard_map/all_gather | solution.py:210
  91.5 0.5 inside.14.refs_0_
  92.0 0.3 outside.14.refs_0_
  92.3 4.9 %collective-permute-start.8 = (bf16[32,768]{1,0:T(8,128)(2,1)S(1)}, bf16[32,768]{1,0:T(8,128)(2,1)S(1)}, u32[]{:S(2)}, u32[]{:S(2)}) collective-permute-start(bf16[32,768]{1,0:T(8,128)(2,1)S(1)} %outside.14.refs_0_), channel_id=1, source_target_pairs={{0,448},{64,128},{128,64},{192,256},{256,192},{320,384},{384,320},... | collective-permute-start | bytes 147464 | tf_op jit(solution)/shard_map/ppermute | solution.py:209
  97.2 4.8 %all_gather.37.refs_1_ = bf16[64,768]{1,0:T(8,128)(2,1)S(1)} all-gather(bf16[32,768]{1,0:T(8,128)(2,1)S(1)} %outside.14.refs_0_), channel_id=1, replica_groups={{0,64},{128,192},{256,320},{384,448},{1,65},{129,193},{257,321},{385,44..., dimensions={0}, use_global_device_ids=true | all-gather | bytes 147456 | tf_op jit(solution)/shard_map/all_gather | solution.py:210
  101.9 0.5 inside.15.refs_0_
  102.4 0.3 outside.15
  102.8 5.6 %all_gather.38.y_ref = bf16[128,768]{1,0:T(8,128)(2,1)S(1)} all-gather(bf16[32,768]{1,0:T(8,128)(2,1)S(1)} %outside.15), channel_id=1, replica_groups=mesh['elem'=8,'z'=16,'yl'=2,'c'=2] {'yl','c'}, dimensions={0}, use_global_device_ids=true | all-gather | bytes 245760 | tf_op jit(solution)/shard_map/all_gather | solution.py:269
  108.4 1.3 pick.1
  109.6 30.4 %all_to_all.5.x_ref = bf16[16,40,128]{2,1,0:T(8,128)(2,1)S(1)} all-to-all(bf16[16,40,128]{2,1,0:T(8,128)(2,1)S(1)} %get-tuple-element.20), channel_id=1, replica_groups=mesh['elem'=8,'z'=16,'yl'=2,'c'=2] {'z'}, dimensions={0} | all-to-all | bytes 327680 | tf_op jit(solution)/shard_map/all_to_all | solution.py:283
  140.0 5.4 %rotate.1 = bf16[36,2048]{1,0:T(8,128)(2,1)} custom-call(bf16[16,40,128]{2,1,0:T(8,128)(2,1)S(1)} %all_to_all.5.x_ref, bf16[2048,2048]{1,0:T(8,128)(2,1)} %all-gather.2.cloned.1.call-done.r_ref), custom_call_target="tpu_custom_call" | custom-call | tf_op jit(solution)/shard_map/rotate/pallas_call | solution.py:284
  (7 shorter events, 0.0 us)
Async XLA Ops:
  7.2 132.8 %all-gather.2.cloned.1.call-start = ((), (), s32[]{:S(2)}) async-start(), calls=%async_computation.1 | async-start | bytes 8650752 | tf_op jit(solution)/shard_map/all_gather | solution.py:228
  7.2 9.3 %collective-permute-start = (bf16[32,2048]{1,0:T(8,128)(2,1)}, bf16[32,2048]{1,0:T(8,128)(2,1)S(1)}, u32[]{:S(2)}, u32[]{:S(2)}) collective-permute-start(bf16[32,2048]{1,0:T(8,128)(2,1)} %bitcast.5), channel_id=1, source_target_pairs={{0,2},{2,0},{1,3},{3,1},{4,6},{6,4},{5,7},{7,5},{8,10},{10,8},{9,1... | collective-permute-start | bytes 393224 | tf_op jit(solution)/shard_map/ppermute | solution.py:212
  18.1 9.8 %collective-permute-start.1 = (bf16[32,768]{1,0:T(8,128)(2,1)S(1)}, bf16[32,768]{1,0:T(8,128)(2,1)S(1)}, u32[]{:S(2)}, u32[]{:S(2)}) collective-permute-start(bf16[32,768]{1,0:T(8,128)(2,1)S(1)} %mask.1.refs_0_.refs_3_), channel_id=1, source_target_pairs={{0,448},{64,128},{128,64},{192,256},{256,192},{320,384},{384,320},... | collective-permute-start | bytes 147464 | tf_op jit(solution)/shard_map/ppermute | solution.py:209
  28.3 12.1 %collective-permute-start.2 = (bf16[32,768]{1,0:T(8,128)(2,1)S(1)}, bf16[32,768]{1,0:T(8,128)(2,1)S(1)}, u32[]{:S(2)}, u32[]{:S(2)}) collective-permute-start(bf16[32,768]{1,0:T(8,128)(2,1)S(1)} %outside.8.refs_0_.refs_3_), channel_id=1, source_target_pairs={{0,448},{64,128},{128,64},{192,256},{256,192},{320,384},{384,320},... | collective-permute-start | bytes 147464 | tf_op jit(solution)/shard_map/ppermute | solution.py:209
  40.7 9.6 %collective-permute-start.3 = (bf16[32,768]{1,0:T(8,128)(2,1)S(1)}, bf16[32,768]{1,0:T(8,128)(2,1)S(1)}, u32[]{:S(2)}, u32[]{:S(2)}) collective-permute-start(bf16[32,768]{1,0:T(8,128)(2,1)S(1)} %outside.9.refs_0_.refs_3_), channel_id=1, source_target_pairs={{0,448},{64,128},{128,64},{192,256},{256,192},{320,384},{384,320},... | collective-permute-start | bytes 147464 | tf_op jit(solution)/shard_map/ppermute | solution.py:209
  50.6 10.4 %collective-permute-start.4 = (bf16[32,768]{1,0:T(8,128)(2,1)S(1)}, bf16[32,768]{1,0:T(8,128)(2,1)S(1)}, u32[]{:S(2)}, u32[]{:S(2)}) collective-permute-start(bf16[32,768]{1,0:T(8,128)(2,1)S(1)} %outside.10.refs_0_.refs_3_), channel_id=1, source_target_pairs={{0,448},{64,128},{128,64},{192,256},{256,192},{320,384},{384,320},... | collective-permute-start | bytes 147464 | tf_op jit(solution)/shard_map/ppermute | solution.py:209
  61.3 9.6 %collective-permute-start.5 = (bf16[32,768]{1,0:T(8,128)(2,1)S(1)}, bf16[32,768]{1,0:T(8,128)(2,1)S(1)}, u32[]{:S(2)}, u32[]{:S(2)}) collective-permute-start(bf16[32,768]{1,0:T(8,128)(2,1)S(1)} %outside.11.refs_0_.refs_3_), channel_id=1, source_target_pairs={{0,448},{64,128},{128,64},{192,256},{256,192},{320,384},{384,320},... | collective-permute-start | bytes 147464 | tf_op jit(solution)/shard_map/ppermute | solution.py:209
  71.3 10.4 %collective-permute-start.6 = (bf16[32,768]{1,0:T(8,128)(2,1)S(1)}, bf16[32,768]{1,0:T(8,128)(2,1)S(1)}, u32[]{:S(2)}, u32[]{:S(2)}) collective-permute-start(bf16[32,768]{1,0:T(8,128)(2,1)S(1)} %outside.12.refs_0_.refs_3_), channel_id=1, source_target_pairs={{0,448},{64,128},{128,64},{192,256},{256,192},{320,384},{384,320},... | collective-permute-start | bytes 147464 | tf_op jit(solution)/shard_map/ppermute | solution.py:209
  82.0 10.0 %collective-permute-start.7 = (bf16[32,768]{1,0:T(8,128)(2,1)S(1)}, bf16[32,768]{1,0:T(8,128)(2,1)S(1)}, u32[]{:S(2)}, u32[]{:S(2)}) collective-permute-start(bf16[32,768]{1,0:T(8,128)(2,1)S(1)} %outside.13.refs_0_.refs_3_), channel_id=1, source_target_pairs={{0,448},{64,128},{128,64},{192,256},{256,192},{320,384},{384,320},... | collective-permute-start | bytes 147464 | tf_op jit(solution)/shard_map/ppermute | solution.py:209
  92.0 16.4 %copy-start = (s32[64]{0:T(128)S(1)}, s32[64]{0:T(128)}, u32[]{:S(2)}) copy-start(s32[64]{0:T(128)} %owner_rows.1) | copy-start | bytes 772
  92.3 10.1 %collective-permute-start.8 = (bf16[32,768]{1,0:T(8,128)(2,1)S(1)}, bf16[32,768]{1,0:T(8,128)(2,1)S(1)}, u32[]{:S(2)}, u32[]{:S(2)}) collective-permute-start(bf16[32,768]{1,0:T(8,128)(2,1)S(1)} %outside.14.refs_0_), channel_id=1, source_target_pairs={{0,448},{64,128},{128,64},{192,256},{256,192},{320,384},{384,320},... | collective-permute-start | bytes 147464 | tf_op jit(solution)/shard_map/ppermute | solution.py:209
Sparse Core Ops, SparseCore 0:
  18.3 82.5 all-gather.1

commit v10 on v8

--- a/solution.py
+++ b/solution.py
@@ -116,8 +116,7 @@
     y_ref[...] = (p_ref[...] + total * scale).astype(BF16)
 
 
-def pick_kernel(owner_rows, quad, y_ref, out_ref, own_ref, turned):
-    own_ref[...] = y_ref[pl.ds(pl.multiple_of(BANDS_DEV * quad[0], BANDS_DEV), BANDS_DEV), :]
+def pick_kernel(owner_rows, quad, y_ref, out_ref, turned):
     for block in range(ROWS // 128):
         part = y_ref[:, 128 * block : 128 * (block + 1)].astype(F32)
         turned[128 * block : 128 * (block + 1), :] = part.T
@@ -152,9 +151,12 @@
     store.wait()
 
 
-def rotate_kernel(x_ref, r_ref, out_ref, gathered):
+def rotate_kernel(x_ref, y_ref, r_ref, out_ref, filtered_hbm, gathered, sem):
+    store = pltpu.make_async_copy(y_ref, filtered_hbm, sem)
+
     @pl.when(pl.program_id(0) == 0)
     def _():
+        store.start()
         for z in range(Z):
             gathered[:, 128 * z : 128 * (z + 1)] = x_ref[z]
 
@@ -170,6 +172,10 @@
         preferred_element_type=F32,
     )
     out_ref[...] = product.T[:CAP].astype(BF16)
+
+    @pl.when(pl.program_id(0) == pl.num_programs(0) - 1)
+    def _():
+        store.wait()
 
 
 def per_device(start_bands, hamiltonian, neighbours, basis_count, owner_rows, rotation):
@@ -264,30 +270,34 @@
         earlier, current = current, following
 
     bands_quad = lax.all_gather(current, ("yl", "c"), axis=0, tiled=True)
-    sent, filtered = pl.pallas_call(
+    sent = pl.pallas_call(
         pick_kernel,
-        out_shape=(jax.ShapeDtypeStruct((Z, CAP_PAD, QUAD * BANDS_DEV), BF16), block_bf16),
+        out_shape=jax.ShapeDtypeStruct((Z, CAP_PAD, QUAD * BANDS_DEV), BF16),
         in_specs=[SMEM, SMEM, VMEM],
-        out_specs=(VMEM, VMEM),
+        out_specs=VMEM,
         scratch_shapes=[pltpu.VMEM((ROWS + 48, QUAD * BANDS_DEV), F32)],
         compiler_params=params(8),
         cost_estimate=COST,
         name="pick",
     )(owner_rows, quad, bands_quad)
     received = lax.all_to_all(sent, "z", split_axis=0, concat_axis=0, tiled=True)
-    rotated = pl.pallas_call(
+    rotated, filtered = pl.pallas_call(
         rotate_kernel,
-        out_shape=jax.ShapeDtypeStruct((CAP, rotation_all.shape[1]), BF16),
+        out_shape=(jax.ShapeDtypeStruct((CAP, rotation_all.shape[1]), BF16), block_bf16),
         grid=(rotation_all.shape[0] // TILE,),
         in_specs=[
             pl.BlockSpec(received.shape, lambda n: (0, 0, 0)),
+            VMEM,
             pl.BlockSpec((TILE, rotation_all.shape[1]), lambda n: (n, 0)),
         ],
-        out_specs=pl.BlockSpec((CAP, TILE), lambda n: (0, n)),
-        scratch_shapes=[pltpu.VMEM((CAP_PAD, rotation_all.shape[1]), BF16)],
+        out_specs=(pl.BlockSpec((CAP, TILE), lambda n: (0, n)), HBM),
+        scratch_shapes=[
+            pltpu.VMEM((CAP_PAD, rotation_all.shape[1]), BF16),
+            pltpu.SemaphoreType.DMA,
+        ],
         compiler_params=params(24),
         name="rotate",
-    )(received, in_hbm(rotation_all))
+    )(received, current, in_hbm(rotation_all))
     return filtered, rotated
 
 

time: 153 us -> 152 us (level)
  no operation moved by 1% of the time
where the time goes in v10:
time: 152 us
  blocking collectives  74.4 us (49%)
  starting transfers between devices  45.4 us (30%)
  Pallas kernels  17.6 us (12%)
  between operations  14.2 us (9%)
    ppermute x8, starting transfers between devices, per_device(): from_far = lax.ppermute(current, 'elem', far)  41.9 us
    all_gather x8, blocking collectives, per_device(): lax.all_gather(current, 'elem', axis=0, tiled=True, axis_index_groups=near)  38.4 us
    all_to_all x1, blocking collectives, per_device(): lax.all_to_all(sent, 'z', split_axis=0, concat_axis=0, tiled=True)  30.4 us
    all_gather x1, blocking collectives, per_device(): bands_quad = lax.all_gather(current, ('yl', 'c'), axis=0, tiled=True)  5.59 us
    pallas_call x1, Pallas kernels, per_device(): pl.pallas_call(rotate_kernel, out_shape=(jax.ShapeDtypeStruct((CAP, rotat...  5.44 us
    pallas_call x8, Pallas kernels, per_device(): pl.pallas_call(lambda *refs, scale=scale, has_prev=bool(previous): inside...  3.96 us
    ppermute x1, starting transfers between devices, per_device(): other_columns = lax.ppermute(columns, 'yl', [(0, 1), (1, 0)])  3.49 us
  transfers between devices with their start and end apart: 10, of which 0 were waited for; matrix products, arithmetic and copies ran while one was open for 0% of the time, Pallas kernels for 7%

profile of v10, /device:TPU:32, one launch (start us, length us, event | category | flops | bytes accessed | tf_op | source)
XLA Modules:
  0.0 151.7 jit_solution(16156530802936207217)
XLA Ops:
  7.2 0.0 all-gather.2.cloned.1.call-start
  7.2 3.5 %collective-permute-start = (bf16[32,2048]{1,0:T(8,128)(2,1)}, bf16[32,2048]{1,0:T(8,128)(2,1)S(1)}, u32[]{:S(2)}, u32[]{:S(2)}) collective-permute-start(bf16[32,2048]{1,0:T(8,128)(2,1)} %bitcast.5), channel_id=1, source_target_pairs={{0,2},{2,0},{1,3},{3,1},{4,6},{6,4},{5,7},{7,5},{8,10},{10,8},{9,1... | collective-permute-start | bytes 393224 | tf_op jit(solution)/shard_map/ppermute | solution.py:215
  10.7 1.0 mask.1.refs_0_.refs_3_
  11.7 4.8 %all_gather.30.refs_1_ = bf16[64,768]{1,0:T(8,128)(2,1)S(1)} all-gather(bf16[32,768]{1,0:T(8,128)(2,1)S(1)} %mask.1.refs_0_.refs_3_), channel_id=1, replica_groups={{0,64},{128,192},{256,320},{384,448},{1,65},{129,193},{257,321},{385,44..., dimensions={0}, use_global_device_ids=true | all-gather | bytes 147456 | tf_op jit(solution)/shard_map/all_gather | solution.py:213
  16.5 1.6 %join.1 = bf16[64,2048]{1,0:T(8,128)(2,1)} custom-call(s32[1]{0:T(128)} %bitcast.low, bf16[32,2048]{1,0:T(8,128)(2,1)} %bitcast.6, bf16[32,2048]{1,0:T(8,128)(2,1)S(1)} %collective-permute-done.other_ref), custom_call_target="tpu_custom_call" | custom-call | flops 300000000 | bytes 3145728 | tf_op jit(solution)/shard_map/join/pallas_call | solution.py:217
  18.1 0.0 all-gather.2.cloned.1.call-update
  18.1 7.0 %collective-permute-start.1 = (bf16[32,768]{1,0:T(8,128)(2,1)S(1)}, bf16[32,768]{1,0:T(8,128)(2,1)S(1)}, u32[]{:S(2)}, u32[]{:S(2)}) collective-permute-start(bf16[32,768]{1,0:T(8,128)(2,1)S(1)} %mask.1.refs_0_.refs_3_), channel_id=1, source_target_pairs={{0,448},{64,128},{128,64},{192,256},{256,192},{320,384},{384,320},... | collective-permute-start | bytes 147464 | tf_op jit(solution)/shard_map/ppermute | solution.py:212
  25.1 2.2 %couple.1 = (bf16[1536,768]{1,0:T(8,128)(2,1)S(1)}, bf16[768,768]{1,0:T(8,128)(2,1)S(1)}) custom-call(s32[4,6]{1,0:T(4,128)} %neighbours_hbm.1, s32[4]{0:T(128)} %counts_hbm.3, s32[1]{0:T(128)} %bitcast.2.parity, bf16[4,7,192,192]{3,2,1,0:T(8,128)(2,1)} %h_hbm.1), custom_call_target="tpu_custom_call" | custom-call | tf_op jit(solution)/shard_map/couple/pallas_call | solution.py:232
  27.4 0.5 inside.8.refs_0_
  27.9 0.0 collective-permute-done.1.refs_1_
  27.9 0.3 outside.8.refs_0_.refs_3_
  28.3 6.8 %collective-permute-start.2 = (bf16[32,768]{1,0:T(8,128)(2,1)S(1)}, bf16[32,768]{1,0:T(8,128)(2,1)S(1)}, u32[]{:S(2)}, u32[]{:S(2)}) collective-permute-start(bf16[32,768]{1,0:T(8,128)(2,1)S(1)} %outside.8.refs_0_.refs_3_), channel_id=1, source_target_pairs={{0,448},{64,128},{128,64},{192,256},{256,192},{320,384},{384,320},... | collective-permute-start | bytes 147464 | tf_op jit(solution)/shard_map/ppermute | solution.py:212
  35.1 4.8 %all_gather.31.refs_1_ = bf16[64,768]{1,0:T(8,128)(2,1)S(1)} all-gather(bf16[32,768]{1,0:T(8,128)(2,1)S(1)} %outside.8.refs_0_.refs_3_), channel_id=1, replica_groups={{0,64},{128,192},{256,320},{384,448},{1,65},{129,193},{257,321},{385,44..., dimensions={0}, use_global_device_ids=true | all-gather | bytes 147456 | tf_op jit(solution)/shard_map/all_gather | solution.py:213
  39.8 0.5 inside.9.refs_0_
  40.3 0.0 collective-permute-done.2.refs_1_
  40.3 0.3 outside.9.refs_0_.refs_3_
  40.7 4.3 %collective-permute-start.3 = (bf16[32,768]{1,0:T(8,128)(2,1)S(1)}, bf16[32,768]{1,0:T(8,128)(2,1)S(1)}, u32[]{:S(2)}, u32[]{:S(2)}) collective-permute-start(bf16[32,768]{1,0:T(8,128)(2,1)S(1)} %outside.9.refs_0_.refs_3_), channel_id=1, source_target_pairs={{0,448},{64,128},{128,64},{192,256},{256,192},{320,384},{384,320},... | collective-permute-start | bytes 147464 | tf_op jit(solution)/shard_map/ppermute | solution.py:212
  45.0 4.8 %all_gather.32.refs_1_ = bf16[64,768]{1,0:T(8,128)(2,1)S(1)} all-gather(bf16[32,768]{1,0:T(8,128)(2,1)S(1)} %outside.9.refs_0_.refs_3_), channel_id=1, replica_groups={{0,64},{128,192},{256,320},{384,448},{1,65},{129,193},{257,321},{385,44..., dimensions={0}, use_global_device_ids=true | all-gather | bytes 147456 | tf_op jit(solution)/shard_map/all_gather | solution.py:213
  49.7 0.5 inside.10.refs_0_
  50.2 0.0 collective-permute-done.3.refs_1_
  50.3 0.3 outside.10.refs_0_.refs_3_
  50.6 5.1 %collective-permute-start.4 = (bf16[32,768]{1,0:T(8,128)(2,1)S(1)}, bf16[32,768]{1,0:T(8,128)(2,1)S(1)}, u32[]{:S(2)}, u32[]{:S(2)}) collective-permute-start(bf16[32,768]{1,0:T(8,128)(2,1)S(1)} %outside.10.refs_0_.refs_3_), channel_id=1, source_target_pairs={{0,448},{64,128},{128,64},{192,256},{256,192},{320,384},{384,320},... | collective-permute-start | bytes 147464 | tf_op jit(solution)/shard_map/ppermute | solution.py:212
  55.7 4.8 %all_gather.33.refs_1_ = bf16[64,768]{1,0:T(8,128)(2,1)S(1)} all-gather(bf16[32,768]{1,0:T(8,128)(2,1)S(1)} %outside.10.refs_0_.refs_3_), channel_id=1, replica_groups={{0,64},{128,192},{256,320},{384,448},{1,65},{129,193},{257,321},{385,44..., dimensions={0}, use_global_device_ids=true | all-gather | bytes 147456 | tf_op jit(solution)/shard_map/all_gather | solution.py:213
  60.5 0.5 inside.11.refs_0_
  61.0 0.0 collective-permute-done.4.refs_1_
  61.0 0.3 outside.11.refs_0_.refs_3_
  61.3 4.3 %collective-permute-start.5 = (bf16[32,768]{1,0:T(8,128)(2,1)S(1)}, bf16[32,768]{1,0:T(8,128)(2,1)S(1)}, u32[]{:S(2)}, u32[]{:S(2)}) collective-permute-start(bf16[32,768]{1,0:T(8,128)(2,1)S(1)} %outside.11.refs_0_.refs_3_), channel_id=1, source_target_pairs={{0,448},{64,128},{128,64},{192,256},{256,192},{320,384},{384,320},... | collective-permute-start | bytes 147464 | tf_op jit(solution)/shard_map/ppermute | solution.py:212
  65.7 4.8 %all_gather.34.refs_1_ = bf16[64,768]{1,0:T(8,128)(2,1)S(1)} all-gather(bf16[32,768]{1,0:T(8,128)(2,1)S(1)} %outside.11.refs_0_.refs_3_), channel_id=1, replica_groups={{0,64},{128,192},{256,320},{384,448},{1,65},{129,193},{257,321},{385,44..., dimensions={0}, use_global_device_ids=true | all-gather | bytes 147456 | tf_op jit(solution)/shard_map/all_gather | solution.py:213
  70.4 0.5 inside.12.refs_0_
  70.9 0.0 collective-permute-done.5.refs_1_
  70.9 0.3 outside.12.refs_0_.refs_3_
  71.3 5.1 %collective-permute-start.6 = (bf16[32,768]{1,0:T(8,128)(2,1)S(1)}, bf16[32,768]{1,0:T(8,128)(2,1)S(1)}, u32[]{:S(2)}, u32[]{:S(2)}) collective-permute-start(bf16[32,768]{1,0:T(8,128)(2,1)S(1)} %outside.12.refs_0_.refs_3_), channel_id=1, source_target_pairs={{0,448},{64,128},{128,64},{192,256},{256,192},{320,384},{384,320},... | collective-permute-start | bytes 147464 | tf_op jit(solution)/shard_map/ppermute | solution.py:212
  76.4 4.8 %all_gather.35.refs_1_ = bf16[64,768]{1,0:T(8,128)(2,1)S(1)} all-gather(bf16[32,768]{1,0:T(8,128)(2,1)S(1)} %outside.12.refs_0_.refs_3_), channel_id=1, replica_groups={{0,64},{128,192},{256,320},{384,448},{1,65},{129,193},{257,321},{385,44..., dimensions={0}, use_global_device_ids=true | all-gather | bytes 147456 | tf_op jit(solution)/shard_map/all_gather | solution.py:213
  81.2 0.5 inside.13.refs_0_
  81.7 0.0 collective-permute-done.6.refs_1_
  81.7 0.3 outside.13.refs_0_.refs_3_
  82.0 4.3 %collective-permute-start.7 = (bf16[32,768]{1,0:T(8,128)(2,1)S(1)}, bf16[32,768]{1,0:T(8,128)(2,1)S(1)}, u32[]{:S(2)}, u32[]{:S(2)}) collective-permute-start(bf16[32,768]{1,0:T(8,128)(2,1)S(1)} %outside.13.refs_0_.refs_3_), channel_id=1, source_target_pairs={{0,448},{64,128},{128,64},{192,256},{256,192},{320,384},{384,320},... | collective-permute-start | bytes 147464 | tf_op jit(solution)/shard_map/ppermute | solution.py:212
  86.3 5.1 %all_gather.36.refs_1_ = bf16[64,768]{1,0:T(8,128)(2,1)S(1)} all-gather(bf16[32,768]{1,0:T(8,128)(2,1)S(1)} %outside.13.refs_0_.refs_3_), channel_id=1, replica_groups={{0,64},{128,192},{256,320},{384,448},{1,65},{129,193},{257,321},{385,44..., dimensions={0}, use_global_device_ids=true | all-gather | bytes 147456 | tf_op jit(solution)/shard_map/all_gather | solution.py:213
  91.5 0.5 inside.14.refs_0_
  92.0 0.3 outside.14.refs_0_
  92.3 4.9 %collective-permute-start.8 = (bf16[32,768]{1,0:T(8,128)(2,1)S(1)}, bf16[32,768]{1,0:T(8,128)(2,1)S(1)}, u32[]{:S(2)}, u32[]{:S(2)}) collective-permute-start(bf16[32,768]{1,0:T(8,128)(2,1)S(1)} %outside.14.refs_0_), channel_id=1, source_target_pairs={{0,448},{64,128},{128,64},{192,256},{256,192},{320,384},{384,320},... | collective-permute-start | bytes 147464 | tf_op jit(solution)/shard_map/ppermute | solution.py:212
  97.2 4.8 %all_gather.37.refs_1_ = bf16[64,768]{1,0:T(8,128)(2,1)S(1)} all-gather(bf16[32,768]{1,0:T(8,128)(2,1)S(1)} %outside.14.refs_0_), channel_id=1, replica_groups={{0,64},{128,192},{256,320},{384,448},{1,65},{129,193},{257,321},{385,44..., dimensions={0}, use_global_device_ids=true | all-gather | bytes 147456 | tf_op jit(solution)/shard_map/all_gather | solution.py:213
  101.9 0.5 inside.15.refs_0_
  102.4 0.3 outside.15.y_ref
  102.8 5.6 %all_gather.38.y_ref = bf16[128,768]{1,0:T(8,128)(2,1)S(1)} all-gather(bf16[32,768]{1,0:T(8,128)(2,1)S(1)} %outside.15.y_ref), channel_id=1, replica_groups=mesh['elem'=8,'z'=16,'yl'=2,'c'=2] {'yl','c'}, dimensions={0}, use_global_device_ids=true | all-gather | bytes 245760 | tf_op jit(solution)/shard_map/all_gather | solution.py:272
  108.4 0.7 pick.1
  109.1 30.4 %all_to_all.5.x_ref = bf16[16,40,128]{2,1,0:T(8,128)(2,1)S(1)} all-to-all(bf16[16,40,128]{2,1,0:T(8,128)(2,1)S(1)} %pick.1), channel_id=1, replica_groups=mesh['elem'=8,'z'=16,'yl'=2,'c'=2] {'z'}, dimensions={0} | all-to-all | bytes 327680 | tf_op jit(solution)/shard_map/all_to_all | solution.py:283
  139.4 5.4 %rotate.1 = (bf16[36,2048]{1,0:T(8,128)(2,1)}, bf16[32,768]{1,0:T(8,128)(2,1)}) custom-call(bf16[16,40,128]{2,1,0:T(8,128)(2,1)S(1)} %all_to_all.5.x_ref, bf16[32,768]{1,0:T(8,128)(2,1)S(1)} %outside.15.y_ref, bf16[2048,2048]{1,0:T(8,128)(2,1)} %all-gather.2.cloned.1.call-done.r_ref), custom_call_target="tpu_custom_call" | custom-call | tf_op jit(solution)/shard_map/rotate/pallas_call | solution.py:284
  (7 shorter events, 0.0 us)
Async XLA Ops:
  7.2 132.3 %all-gather.2.cloned.1.call-start = ((), (), s32[]{:S(2)}) async-start(), calls=%async_computation.1 | async-start | bytes 8650752 | tf_op jit(solution)/shard_map/all_gather | solution.py:231
  7.2 9.3 %collective-permute-start = (bf16[32,2048]{1,0:T(8,128)(2,1)}, bf16[32,2048]{1,0:T(8,128)(2,1)S(1)}, u32[]{:S(2)}, u32[]{:S(2)}) collective-permute-start(bf16[32,2048]{1,0:T(8,128)(2,1)} %bitcast.5), channel_id=1, source_target_pairs={{0,2},{2,0},{1,3},{3,1},{4,6},{6,4},{5,7},{7,5},{8,10},{10,8},{9,1... | collective-permute-start | bytes 393224 | tf_op jit(solution)/shard_map/ppermute | solution.py:215
  18.1 9.8 %collective-permute-start.1 = (bf16[32,768]{1,0:T(8,128)(2,1)S(1)}, bf16[32,768]{1,0:T(8,128)(2,1)S(1)}, u32[]{:S(2)}, u32[]{:S(2)}) collective-permute-start(bf16[32,768]{1,0:T(8,128)(2,1)S(1)} %mask.1.refs_0_.refs_3_), channel_id=1, source_target_pairs={{0,448},{64,128},{128,64},{192,256},{256,192},{320,384},{384,320},... | collective-permute-start | bytes 147464 | tf_op jit(solution)/shard_map/ppermute | solution.py:212
  28.3 12.1 %collective-permute-start.2 = (bf16[32,768]{1,0:T(8,128)(2,1)S(1)}, bf16[32,768]{1,0:T(8,128)(2,1)S(1)}, u32[]{:S(2)}, u32[]{:S(2)}) collective-permute-start(bf16[32,768]{1,0:T(8,128)(2,1)S(1)} %outside.8.refs_0_.refs_3_), channel_id=1, source_target_pairs={{0,448},{64,128},{128,64},{192,256},{256,192},{320,384},{384,320},... | collective-permute-start | bytes 147464 | tf_op jit(solution)/shard_map/ppermute | solution.py:212
  40.7 9.6 %collective-permute-start.3 = (bf16[32,768]{1,0:T(8,128)(2,1)S(1)}, bf16[32,768]{1,0:T(8,128)(2,1)S(1)}, u32[]{:S(2)}, u32[]{:S(2)}) collective-permute-start(bf16[32,768]{1,0:T(8,128)(2,1)S(1)} %outside.9.refs_0_.refs_3_), channel_id=1, source_target_pairs={{0,448},{64,128},{128,64},{192,256},{256,192},{320,384},{384,320},... | collective-permute-start | bytes 147464 | tf_op jit(solution)/shard_map/ppermute | solution.py:212
  50.6 10.4 %collective-permute-start.4 = (bf16[32,768]{1,0:T(8,128)(2,1)S(1)}, bf16[32,768]{1,0:T(8,128)(2,1)S(1)}, u32[]{:S(2)}, u32[]{:S(2)}) collective-permute-start(bf16[32,768]{1,0:T(8,128)(2,1)S(1)} %outside.10.refs_0_.refs_3_), channel_id=1, source_target_pairs={{0,448},{64,128},{128,64},{192,256},{256,192},{320,384},{384,320},... | collective-permute-start | bytes 147464 | tf_op jit(solution)/shard_map/ppermute | solution.py:212
  61.3 9.6 %collective-permute-start.5 = (bf16[32,768]{1,0:T(8,128)(2,1)S(1)}, bf16[32,768]{1,0:T(8,128)(2,1)S(1)}, u32[]{:S(2)}, u32[]{:S(2)}) collective-permute-start(bf16[32,768]{1,0:T(8,128)(2,1)S(1)} %outside.11.refs_0_.refs_3_), channel_id=1, source_target_pairs={{0,448},{64,128},{128,64},{192,256},{256,192},{320,384},{384,320},... | collective-permute-start | bytes 147464 | tf_op jit(solution)/shard_map/ppermute | solution.py:212
  71.3 10.4 %collective-permute-start.6 = (bf16[32,768]{1,0:T(8,128)(2,1)S(1)}, bf16[32,768]{1,0:T(8,128)(2,1)S(1)}, u32[]{:S(2)}, u32[]{:S(2)}) collective-permute-start(bf16[32,768]{1,0:T(8,128)(2,1)S(1)} %outside.12.refs_0_.refs_3_), channel_id=1, source_target_pairs={{0,448},{64,128},{128,64},{192,256},{256,192},{320,384},{384,320},... | collective-permute-start | bytes 147464 | tf_op jit(solution)/shard_map/ppermute | solution.py:212
  82.0 10.0 %collective-permute-start.7 = (bf16[32,768]{1,0:T(8,128)(2,1)S(1)}, bf16[32,768]{1,0:T(8,128)(2,1)S(1)}, u32[]{:S(2)}, u32[]{:S(2)}) collective-permute-start(bf16[32,768]{1,0:T(8,128)(2,1)S(1)} %outside.13.refs_0_.refs_3_), channel_id=1, source_target_pairs={{0,448},{64,128},{128,64},{192,256},{256,192},{320,384},{384,320},... | collective-permute-start | bytes 147464 | tf_op jit(solution)/shard_map/ppermute | solution.py:212
  92.0 16.4 %copy-start = (s32[64]{0:T(128)S(1)}, s32[64]{0:T(128)}, u32[]{:S(2)}) copy-start(s32[64]{0:T(128)} %owner_rows.1) | copy-start | bytes 772
  92.3 10.1 %collective-permute-start.8 = (bf16[32,768]{1,0:T(8,128)(2,1)S(1)}, bf16[32,768]{1,0:T(8,128)(2,1)S(1)}, u32[]{:S(2)}, u32[]{:S(2)}) collective-permute-start(bf16[32,768]{1,0:T(8,128)(2,1)S(1)} %outside.14.refs_0_), channel_id=1, source_target_pairs={{0,448},{64,128},{128,64},{192,256},{256,192},{320,384},{384,320},... | collective-permute-start | bytes 147464 | tf_op jit(solution)/shard_map/ppermute | solution.py:212
Sparse Core Ops, SparseCore 0:
  18.3 82.5 all-gather.1

commit v11 on v10

--- a/solution.py
+++ b/solution.py
@@ -100,11 +100,9 @@
         prev_ref, w_ref, p_ref = refs
     else:
         w_ref, p_ref = refs
-    near = jnp.where(
-        second_ref[...] > 0.0, pair_ref[BANDS_DEV:, :].astype(F32), pair_ref[:BANDS_DEV, :].astype(F32)
-    ).astype(BF16)
+    both = jnp.dot(pair_ref[...], w_ref[ROWS:, :], preferred_element_type=F32)
     total = jnp.dot(y_ref[...], w_ref[:ROWS, :], preferred_element_type=F32)
-    total += jnp.dot(near, w_ref[ROWS:, :], preferred_element_type=F32)
+    total += jnp.where(second_ref[...] > 0.0, both[BANDS_DEV:], both[:BANDS_DEV])
     total = total * scale
     if has_prev:
         total = total - prev_ref[...].astype(F32)

time: 152 us -> 152 us (level)
  no operation moved by 1% of the time
where the time goes in v11:
time: 152 us
  blocking collectives  74.3 us (49%)
  starting transfers between devices  45.4 us (30%)
  Pallas kernels  17.5 us (12%)
  between operations  14.3 us (9%)
    ppermute x8, starting transfers between devices, per_device(): from_far = lax.ppermute(current, 'elem', far)  41.9 us
    all_gather x8, blocking collectives, per_device(): lax.all_gather(current, 'elem', axis=0, tiled=True, axis_index_groups=near)  38.5 us
    all_to_all x1, blocking collectives, per_device(): lax.all_to_all(sent, 'z', split_axis=0, concat_axis=0, tiled=True)  30.3 us
    all_gather x1, blocking collectives, per_device(): bands_quad = lax.all_gather(current, ('yl', 'c'), axis=0, tiled=True)  5.59 us
    pallas_call x1, Pallas kernels, per_device(): pl.pallas_call(rotate_kernel, out_shape=(jax.ShapeDtypeStruct((CAP, rotat...  5.44 us
    pallas_call x8, Pallas kernels, per_device(): pl.pallas_call(lambda *refs, scale=scale, has_prev=bool(previous): inside...  3.89 us
    ppermute x1, starting transfers between devices, per_device(): other_columns = lax.ppermute(columns, 'yl', [(0, 1), (1, 0)])  3.49 us
  transfers between devices with their start and end apart: 10, of which 0 were waited for; matrix products, arithmetic and copies ran while one was open for 0% of the time, Pallas kernels for 7%

profile of v11, /device:TPU:32, one launch (start us, length us, event | category | flops | bytes accessed | tf_op | source)
XLA Modules:
  0.0 151.6 jit_solution(11248267455498084078)
XLA Ops:
  7.2 0.0 all-gather.2.cloned.1.call-start
  7.2 3.5 %collective-permute-start = (bf16[32,2048]{1,0:T(8,128)(2,1)}, bf16[32,2048]{1,0:T(8,128)(2,1)S(1)}, u32[]{:S(2)}, u32[]{:S(2)}) collective-permute-start(bf16[32,2048]{1,0:T(8,128)(2,1)} %bitcast.5), channel_id=1, source_target_pairs={{0,2},{2,0},{1,3},{3,1},{4,6},{6,4},{5,7},{7,5},{8,10},{10,8},{9,1... | collective-permute-start | bytes 393224 | tf_op jit(solution)/shard_map/ppermute | solution.py:213
  10.7 1.0 mask.1.refs_0_.refs_3_
  11.7 4.8 %all_gather.30.refs_1_ = bf16[64,768]{1,0:T(8,128)(2,1)S(1)} all-gather(bf16[32,768]{1,0:T(8,128)(2,1)S(1)} %mask.1.refs_0_.refs_3_), channel_id=1, replica_groups={{0,64},{128,192},{256,320},{384,448},{1,65},{129,193},{257,321},{385,44..., dimensions={0}, use_global_device_ids=true | all-gather | bytes 147456 | tf_op jit(solution)/shard_map/all_gather | solution.py:211
  16.5 1.6 %join.1 = bf16[64,2048]{1,0:T(8,128)(2,1)} custom-call(s32[1]{0:T(128)} %bitcast.low, bf16[32,2048]{1,0:T(8,128)(2,1)} %bitcast.6, bf16[32,2048]{1,0:T(8,128)(2,1)S(1)} %collective-permute-done.other_ref), custom_call_target="tpu_custom_call" | custom-call | flops 300000000 | bytes 3145728 | tf_op jit(solution)/shard_map/join/pallas_call | solution.py:215
  18.1 0.0 all-gather.2.cloned.1.call-update
  18.1 7.0 %collective-permute-start.1 = (bf16[32,768]{1,0:T(8,128)(2,1)S(1)}, bf16[32,768]{1,0:T(8,128)(2,1)S(1)}, u32[]{:S(2)}, u32[]{:S(2)}) collective-permute-start(bf16[32,768]{1,0:T(8,128)(2,1)S(1)} %mask.1.refs_0_.refs_3_), channel_id=1, source_target_pairs={{0,448},{64,128},{128,64},{192,256},{256,192},{320,384},{384,320},... | collective-permute-start | bytes 147464 | tf_op jit(solution)/shard_map/ppermute | solution.py:210
  25.1 2.2 %couple.1 = (bf16[1536,768]{1,0:T(8,128)(2,1)S(1)}, bf16[768,768]{1,0:T(8,128)(2,1)S(1)}) custom-call(s32[4,6]{1,0:T(4,128)} %neighbours_hbm.1, s32[4]{0:T(128)} %counts_hbm.3, s32[1]{0:T(128)} %bitcast.2.parity, bf16[4,7,192,192]{3,2,1,0:T(8,128)(2,1)} %h_hbm.1), custom_call_target="tpu_custom_call" | custom-call | tf_op jit(solution)/shard_map/couple/pallas_call | solution.py:230
  27.4 0.5 inside.8.refs_0_
  27.9 0.3 outside.8.refs_0_.refs_3_
  28.2 6.8 %collective-permute-start.2 = (bf16[32,768]{1,0:T(8,128)(2,1)S(1)}, bf16[32,768]{1,0:T(8,128)(2,1)S(1)}, u32[]{:S(2)}, u32[]{:S(2)}) collective-permute-start(bf16[32,768]{1,0:T(8,128)(2,1)S(1)} %outside.8.refs_0_.refs_3_), channel_id=1, source_target_pairs={{0,448},{64,128},{128,64},{192,256},{256,192},{320,384},{384,320},... | collective-permute-start | bytes 147464 | tf_op jit(solution)/shard_map/ppermute | solution.py:210
  35.1 4.8 %all_gather.31.refs_1_ = bf16[64,768]{1,0:T(8,128)(2,1)S(1)} all-gather(bf16[32,768]{1,0:T(8,128)(2,1)S(1)} %outside.8.refs_0_.refs_3_), channel_id=1, replica_groups={{0,64},{128,192},{256,320},{384,448},{1,65},{129,193},{257,321},{385,44..., dimensions={0}, use_global_device_ids=true | all-gather | bytes 147456 | tf_op jit(solution)/shard_map/all_gather | solution.py:211
  39.8 0.5 inside.9.refs_0_
  40.3 0.0 collective-permute-done.2.refs_1_
  40.3 0.3 outside.9.refs_0_.refs_3_
  40.7 4.3 %collective-permute-start.3 = (bf16[32,768]{1,0:T(8,128)(2,1)S(1)}, bf16[32,768]{1,0:T(8,128)(2,1)S(1)}, u32[]{:S(2)}, u32[]{:S(2)}) collective-permute-start(bf16[32,768]{1,0:T(8,128)(2,1)S(1)} %outside.9.refs_0_.refs_3_), channel_id=1, source_target_pairs={{0,448},{64,128},{128,64},{192,256},{256,192},{320,384},{384,320},... | collective-permute-start | bytes 147464 | tf_op jit(solution)/shard_map/ppermute | solution.py:210
  45.0 4.8 %all_gather.32.refs_1_ = bf16[64,768]{1,0:T(8,128)(2,1)S(1)} all-gather(bf16[32,768]{1,0:T(8,128)(2,1)S(1)} %outside.9.refs_0_.refs_3_), channel_id=1, replica_groups={{0,64},{128,192},{256,320},{384,448},{1,65},{129,193},{257,321},{385,44..., dimensions={0}, use_global_device_ids=true | all-gather | bytes 147456 | tf_op jit(solution)/shard_map/all_gather | solution.py:211
  49.7 0.5 inside.10.refs_0_
  50.2 0.0 collective-permute-done.3.refs_1_
  50.2 0.3 outside.10.refs_0_.refs_3_
  50.6 5.1 %collective-permute-start.4 = (bf16[32,768]{1,0:T(8,128)(2,1)S(1)}, bf16[32,768]{1,0:T(8,128)(2,1)S(1)}, u32[]{:S(2)}, u32[]{:S(2)}) collective-permute-start(bf16[32,768]{1,0:T(8,128)(2,1)S(1)} %outside.10.refs_0_.refs_3_), channel_id=1, source_target_pairs={{0,448},{64,128},{128,64},{192,256},{256,192},{320,384},{384,320},... | collective-permute-start | bytes 147464 | tf_op jit(solution)/shard_map/ppermute | solution.py:210
  55.7 4.8 %all_gather.33.refs_1_ = bf16[64,768]{1,0:T(8,128)(2,1)S(1)} all-gather(bf16[32,768]{1,0:T(8,128)(2,1)S(1)} %outside.10.refs_0_.refs_3_), channel_id=1, replica_groups={{0,64},{128,192},{256,320},{384,448},{1,65},{129,193},{257,321},{385,44..., dimensions={0}, use_global_device_ids=true | all-gather | bytes 147456 | tf_op jit(solution)/shard_map/all_gather | solution.py:211
  60.5 0.5 inside.11.refs_0_
  61.0 0.0 collective-permute-done.4.refs_1_
  61.0 0.3 outside.11.refs_0_.refs_3_
  61.3 4.3 %collective-permute-start.5 = (bf16[32,768]{1,0:T(8,128)(2,1)S(1)}, bf16[32,768]{1,0:T(8,128)(2,1)S(1)}, u32[]{:S(2)}, u32[]{:S(2)}) collective-permute-start(bf16[32,768]{1,0:T(8,128)(2,1)S(1)} %outside.11.refs_0_.refs_3_), channel_id=1, source_target_pairs={{0,448},{64,128},{128,64},{192,256},{256,192},{320,384},{384,320},... | collective-permute-start | bytes 147464 | tf_op jit(solution)/shard_map/ppermute | solution.py:210
  65.6 4.8 %all_gather.34.refs_1_ = bf16[64,768]{1,0:T(8,128)(2,1)S(1)} all-gather(bf16[32,768]{1,0:T(8,128)(2,1)S(1)} %outside.11.refs_0_.refs_3_), channel_id=1, replica_groups={{0,64},{128,192},{256,320},{384,448},{1,65},{129,193},{257,321},{385,44..., dimensions={0}, use_global_device_ids=true | all-gather | bytes 147456 | tf_op jit(solution)/shard_map/all_gather | solution.py:211
  70.4 0.5 inside.12.refs_0_
  70.9 0.0 collective-permute-done.5.refs_1_
  70.9 0.3 outside.12.refs_0_.refs_3_
  71.2 5.1 %collective-permute-start.6 = (bf16[32,768]{1,0:T(8,128)(2,1)S(1)}, bf16[32,768]{1,0:T(8,128)(2,1)S(1)}, u32[]{:S(2)}, u32[]{:S(2)}) collective-permute-start(bf16[32,768]{1,0:T(8,128)(2,1)S(1)} %outside.12.refs_0_.refs_3_), channel_id=1, source_target_pairs={{0,448},{64,128},{128,64},{192,256},{256,192},{320,384},{384,320},... | collective-permute-start | bytes 147464 | tf_op jit(solution)/shard_map/ppermute | solution.py:210
  76.4 4.8 %all_gather.35.refs_1_ = bf16[64,768]{1,0:T(8,128)(2,1)S(1)} all-gather(bf16[32,768]{1,0:T(8,128)(2,1)S(1)} %outside.12.refs_0_.refs_3_), channel_id=1, replica_groups={{0,64},{128,192},{256,320},{384,448},{1,65},{129,193},{257,321},{385,44..., dimensions={0}, use_global_device_ids=true | all-gather | bytes 147456 | tf_op jit(solution)/shard_map/all_gather | solution.py:211
  81.1 0.5 inside.13.refs_0_
  81.6 0.3 outside.13.refs_0_.refs_3_
  82.0 4.3 %collective-permute-start.7 = (bf16[32,768]{1,0:T(8,128)(2,1)S(1)}, bf16[32,768]{1,0:T(8,128)(2,1)S(1)}, u32[]{:S(2)}, u32[]{:S(2)}) collective-permute-start(bf16[32,768]{1,0:T(8,128)(2,1)S(1)} %outside.13.refs_0_.refs_3_), channel_id=1, source_target_pairs={{0,448},{64,128},{128,64},{192,256},{256,192},{320,384},{384,320},... | collective-permute-start | bytes 147464 | tf_op jit(solution)/shard_map/ppermute | solution.py:210
  86.3 5.1 %all_gather.36.refs_1_ = bf16[64,768]{1,0:T(8,128)(2,1)S(1)} all-gather(bf16[32,768]{1,0:T(8,128)(2,1)S(1)} %outside.13.refs_0_.refs_3_), channel_id=1, replica_groups={{0,64},{128,192},{256,320},{384,448},{1,65},{129,193},{257,321},{385,44..., dimensions={0}, use_global_device_ids=true | all-gather | bytes 147456 | tf_op jit(solution)/shard_map/all_gather | solution.py:211
  91.4 0.5 inside.14.refs_0_
  91.9 0.0 copy-start
  91.9 0.0 collective-permute-done.7.refs_1_
  92.0 0.3 outside.14.refs_0_
  92.3 4.9 %collective-permute-start.8 = (bf16[32,768]{1,0:T(8,128)(2,1)S(1)}, bf16[32,768]{1,0:T(8,128)(2,1)S(1)}, u32[]{:S(2)}, u32[]{:S(2)}) collective-permute-start(bf16[32,768]{1,0:T(8,128)(2,1)S(1)} %outside.14.refs_0_), channel_id=1, source_target_pairs={{0,448},{64,128},{128,64},{192,256},{256,192},{320,384},{384,320},... | collective-permute-start | bytes 147464 | tf_op jit(solution)/shard_map/ppermute | solution.py:210
  97.2 4.8 %all_gather.37.refs_1_ = bf16[64,768]{1,0:T(8,128)(2,1)S(1)} all-gather(bf16[32,768]{1,0:T(8,128)(2,1)S(1)} %outside.14.refs_0_), channel_id=1, replica_groups={{0,64},{128,192},{256,320},{384,448},{1,65},{129,193},{257,321},{385,44..., dimensions={0}, use_global_device_ids=true | all-gather | bytes 147456 | tf_op jit(solution)/shard_map/all_gather | solution.py:211
  101.9 0.5 inside.15.refs_0_
  102.4 0.3 outside.15.y_ref
  102.8 5.6 %all_gather.38.y_ref = bf16[128,768]{1,0:T(8,128)(2,1)S(1)} all-gather(bf16[32,768]{1,0:T(8,128)(2,1)S(1)} %outside.15.y_ref), channel_id=1, replica_groups=mesh['elem'=8,'z'=16,'yl'=2,'c'=2] {'yl','c'}, dimensions={0}, use_global_device_ids=true | all-gather | bytes 245760 | tf_op jit(solution)/shard_map/all_gather | solution.py:270
  108.3 0.7 pick.1
  109.1 30.3 %all_to_all.5.x_ref = bf16[16,40,128]{2,1,0:T(8,128)(2,1)S(1)} all-to-all(bf16[16,40,128]{2,1,0:T(8,128)(2,1)S(1)} %pick.1), channel_id=1, replica_groups=mesh['elem'=8,'z'=16,'yl'=2,'c'=2] {'z'}, dimensions={0} | all-to-all | bytes 327680 | tf_op jit(solution)/shard_map/all_to_all | solution.py:281
  139.3 5.4 %rotate.1 = (bf16[36,2048]{1,0:T(8,128)(2,1)}, bf16[32,768]{1,0:T(8,128)(2,1)}) custom-call(bf16[16,40,128]{2,1,0:T(8,128)(2,1)S(1)} %all_to_all.5.x_ref, bf16[32,768]{1,0:T(8,128)(2,1)S(1)} %outside.15.y_ref, bf16[2048,2048]{1,0:T(8,128)(2,1)} %all-gather.2.cloned.1.call-done.r_ref), custom_call_target="tpu_custom_call" | custom-call | tf_op jit(solution)/shard_map/rotate/pallas_call | solution.py:282
  (7 shorter events, 0.0 us)
Async XLA Ops:
  7.2 132.2 %all-gather.2.cloned.1.call-start = ((), (), s32[]{:S(2)}) async-start(), calls=%async_computation.1 | async-start | bytes 8650752 | tf_op jit(solution)/shard_map/all_gather | solution.py:229
  7.2 9.3 %collective-permute-start = (bf16[32,2048]{1,0:T(8,128)(2,1)}, bf16[32,2048]{1,0:T(8,128)(2,1)S(1)}, u32[]{:S(2)}, u32[]{:S(2)}) collective-permute-start(bf16[32,2048]{1,0:T(8,128)(2,1)} %bitcast.5), channel_id=1, source_target_pairs={{0,2},{2,0},{1,3},{3,1},{4,6},{6,4},{5,7},{7,5},{8,10},{10,8},{9,1... | collective-permute-start | bytes 393224 | tf_op jit(solution)/shard_map/ppermute | solution.py:213
  18.1 9.8 %collective-permute-start.1 = (bf16[32,768]{1,0:T(8,128)(2,1)S(1)}, bf16[32,768]{1,0:T(8,128)(2,1)S(1)}, u32[]{:S(2)}, u32[]{:S(2)}) collective-permute-start(bf16[32,768]{1,0:T(8,128)(2,1)S(1)} %mask.1.refs_0_.refs_3_), channel_id=1, source_target_pairs={{0,448},{64,128},{128,64},{192,256},{256,192},{320,384},{384,320},... | collective-permute-start | bytes 147464 | tf_op jit(solution)/shard_map/ppermute | solution.py:210
  28.2 12.1 %collective-permute-start.2 = (bf16[32,768]{1,0:T(8,128)(2,1)S(1)}, bf16[32,768]{1,0:T(8,128)(2,1)S(1)}, u32[]{:S(2)}, u32[]{:S(2)}) collective-permute-start(bf16[32,768]{1,0:T(8,128)(2,1)S(1)} %outside.8.refs_0_.refs_3_), channel_id=1, source_target_pairs={{0,448},{64,128},{128,64},{192,256},{256,192},{320,384},{384,320},... | collective-permute-start | bytes 147464 | tf_op jit(solution)/shard_map/ppermute | solution.py:210
  40.7 9.6 %collective-permute-start.3 = (bf16[32,768]{1,0:T(8,128)(2,1)S(1)}, bf16[32,768]{1,0:T(8,128)(2,1)S(1)}, u32[]{:S(2)}, u32[]{:S(2)}) collective-permute-start(bf16[32,768]{1,0:T(8,128)(2,1)S(1)} %outside.9.refs_0_.refs_3_), channel_id=1, source_target_pairs={{0,448},{64,128},{128,64},{192,256},{256,192},{320,384},{384,320},... | collective-permute-start | bytes 147464 | tf_op jit(solution)/shard_map/ppermute | solution.py:210
  50.6 10.4 %collective-permute-start.4 = (bf16[32,768]{1,0:T(8,128)(2,1)S(1)}, bf16[32,768]{1,0:T(8,128)(2,1)S(1)}, u32[]{:S(2)}, u32[]{:S(2)}) collective-permute-start(bf16[32,768]{1,0:T(8,128)(2,1)S(1)} %outside.10.refs_0_.refs_3_), channel_id=1, source_target_pairs={{0,448},{64,128},{128,64},{192,256},{256,192},{320,384},{384,320},... | collective-permute-start | bytes 147464 | tf_op jit(solution)/shard_map/ppermute | solution.py:210
  61.3 9.6 %collective-permute-start.5 = (bf16[32,768]{1,0:T(8,128)(2,1)S(1)}, bf16[32,768]{1,0:T(8,128)(2,1)S(1)}, u32[]{:S(2)}, u32[]{:S(2)}) collective-permute-start(bf16[32,768]{1,0:T(8,128)(2,1)S(1)} %outside.11.refs_0_.refs_3_), channel_id=1, source_target_pairs={{0,448},{64,128},{128,64},{192,256},{256,192},{320,384},{384,320},... | collective-permute-start | bytes 147464 | tf_op jit(solution)/shard_map/ppermute | solution.py:210
  71.2 10.4 %collective-permute-start.6 = (bf16[32,768]{1,0:T(8,128)(2,1)S(1)}, bf16[32,768]{1,0:T(8,128)(2,1)S(1)}, u32[]{:S(2)}, u32[]{:S(2)}) collective-permute-start(bf16[32,768]{1,0:T(8,128)(2,1)S(1)} %outside.12.refs_0_.refs_3_), channel_id=1, source_target_pairs={{0,448},{64,128},{128,64},{192,256},{256,192},{320,384},{384,320},... | collective-permute-start | bytes 147464 | tf_op jit(solution)/shard_map/ppermute | solution.py:210
  82.0 10.0 %collective-permute-start.7 = (bf16[32,768]{1,0:T(8,128)(2,1)S(1)}, bf16[32,768]{1,0:T(8,128)(2,1)S(1)}, u32[]{:S(2)}, u32[]{:S(2)}) collective-permute-start(bf16[32,768]{1,0:T(8,128)(2,1)S(1)} %outside.13.refs_0_.refs_3_), channel_id=1, source_target_pairs={{0,448},{64,128},{128,64},{192,256},{256,192},{320,384},{384,320},... | collective-permute-start | bytes 147464 | tf_op jit(solution)/shard_map/ppermute | solution.py:210
  91.9 16.4 %copy-start = (s32[64]{0:T(128)S(1)}, s32[64]{0:T(128)}, u32[]{:S(2)}) copy-start(s32[64]{0:T(128)} %owner_rows.1) | copy-start | bytes 772
  92.3 10.1 %collective-permute-start.8 = (bf16[32,768]{1,0:T(8,128)(2,1)S(1)}, bf16[32,768]{1,0:T(8,128)(2,1)S(1)}, u32[]{:S(2)}, u32[]{:S(2)}) collective-permute-start(bf16[32,768]{1,0:T(8,128)(2,1)S(1)} %outside.14.refs_0_), channel_id=1, source_target_pairs={{0,448},{64,128},{128,64},{192,256},{256,192},{320,384},{384,320},... | collective-permute-start | bytes 147464 | tf_op jit(solution)/shard_map/ppermute | solution.py:210
Sparse Core Ops, SparseCore 0:
  18.3 82.4 all-gather.1
